TPU v7x, 32 devices: a whole 2x2x4 slice. The times are simulated.
32 devices in a mesh: narrow: 2 (over x), wide: 16 (over z, y, core).
Axes of the slice: x: 2, y: 2, z: 4, core: 2. Of those that a mesh axis runs over, the one named last changes fastest.
Arguments:
- patches: bfloat16 [64, 256, 1152], P(('narrow', 'wide')), may hold values from -6 to 6
- condition: float32 [64, 1152], P(('narrow', 'wide')), may hold values from -6 to 6
- image_counts: int32 [32], P(('narrow', 'wide')), may hold values from 1 to 2, as said below
- ada_weight: bfloat16 [1152, 6912], P(None, 'wide'), may hold values from -0.1875 to 0.1875
- ada_bias: bfloat16 [6912], P('wide'), may hold values from -3 to 3
- inproj_weight: bfloat16 [1152, 3456], P('wide'), may hold values from -0.1875 to 0.1875
- inproj_bias: bfloat16 [2304], P('wide'), may hold values from -2 to 2
- outproj_weight: bfloat16 [1152, 1152], P('wide'), may hold values from -0.75 to 0.75
- outproj_bias: bfloat16 [1152], P('wide'), may hold values from -2 to 2
- up_weight: bfloat16 [1152, 4608], P('wide'), may hold values from -0.1875 to 0.1875
- up_bias: bfloat16 [4608], P('wide'), may hold values from -3 to 3
- down_weight: bfloat16 [4608, 1152], P('wide'), may hold values from -0.09375 to 0.09375
- down_bias: bfloat16 [1152], P('wide'), may hold values from -2 to 2
- cotangent: bfloat16 [64, 256, 1152], P(('narrow', 'wide')), may hold values from -6 to 6
Outputs:
- output: bfloat16 [64, 256, 1152], P(('narrow', 'wide'))
- grad_patches: bfloat16 [64, 256, 1152], P(('narrow', 'wide'))
- grad_condition: float32 [64, 1152], P(('narrow', 'wide'))
- grad_ada_weight: float32 [1152, 6912], P(None, 'wide')
- grad_ada_bias: float32 [6912], P('wide')
- grad_inproj_weight: float32 [1152, 3456], P('wide')
- grad_inproj_bias: float32 [2304], P('wide')
- grad_outproj_weight: float32 [1152, 1152], P('wide')
- grad_outproj_bias: float32 [1152], P('wide')
- grad_up_weight: float32 [1152, 4608], P('wide')
- grad_up_bias: float32 [4608], P('wide')
- grad_down_weight: float32 [4608, 1152], P('wide')
- grad_down_bias: float32 [1152], P('wide')
Inputs may be any that keep to these rules, and one draw needn't show every extreme that they name: `image_counts`: each device's number of live image slots; a device's live slots are its first ones. In every draw some device has 2 and some device has 1.
All inputs are finite; a program needn't handle non-finite values.
Results may differ from a plain program's by a relative error of at most 0.02.
The roundings to bfloat16 on the way count: a program that leaves them out, or rounds other values in their place, can miss the bound.
Values may be sent and summed in bfloat16 or wider, within the bound.
A program may use at most 192 MiB of HBM per device.

v0:
```python
from functools import partial

import jax
import jax.numpy as jnp
from jax import lax
from jax.sharding import PartitionSpec as P

HEADS = 16


norm_eps = 1e-06


def normalize(values):
    center = jnp.mean(values, axis=-1, keepdims=True)
    shifted = values - center
    inv_std = lax.rsqrt(jnp.mean(shifted * shifted, axis=-1, keepdims=True) + norm_eps)
    return (shifted * inv_std, inv_std)


def normalize_reverse(normed, inv_std, grad_normed):
    mean_grad = jnp.mean(grad_normed, axis=-1, keepdims=True)
    mean_proj = jnp.mean(grad_normed * normed, axis=-1, keepdims=True)
    return inv_std * (grad_normed - mean_grad - normed * mean_proj)


def matmul_rows(left, right):
    return jnp.dot(left, right, preferred_element_type=jnp.float32)


def matmul_back(left, right):
    return lax.dot_general(
        left, right, (((1,), (1,)), ((), ())), preferred_element_type=jnp.float32
    )


def matmul_outer(left, right):
    return lax.dot_general(
        left, right, (((0,), (0,)), ((), ())), preferred_element_type=jnp.float32
    )


def block_term(factors, count, first, width):
    pieces = []
    for left, right, base in factors:
        lower = max(first, base)
        upper = min(first + width, base + right.shape[1])
        if lower < upper:
            rows_part = lax.slice_in_dim(left, 0, count, axis=1)
            pieces.append(matmul_outer(rows_part, right[:, lower - base : upper - base]))
    return jnp.concatenate(pieces, axis=1)


def per_device(
    patches,
    condition,
    image_counts,
    ada_weight,
    ada_bias,
    inproj_weight,
    inproj_bias,
    outproj_weight,
    outproj_bias,
    up_weight,
    up_bias,
    down_weight,
    down_bias,
    cotangent,
):
    slots, seq_len, model_width = patches.shape
    head_dim = model_width // HEADS
    scale_qk = head_dim ** (-0.5)
    row_total = slots * seq_len
    wide_count = lax.axis_size("wide")
    live = (jnp.arange(slots) < image_counts[0]).astype(jnp.float32)[:, None, None]
    cond_act = jax.nn.silu(condition).astype(jnp.bfloat16)
    cond_all = lax.all_gather(cond_act, "wide", axis=0, tiled=True)
    mod_part = (matmul_rows(cond_all, ada_weight) + ada_bias.astype(jnp.float32)).astype(
        jnp.bfloat16
    )
    modulation = lax.all_to_all(mod_part, "wide", split_axis=0, concat_axis=1, tiled=True).astype(
        jnp.float32
    )
    segment_list = [
        modulation[:, None, number * model_width : (number + 1) * model_width]
        for number in range(6)
    ]
    (
        selfattn_offset,
        selfattn_scale,
        selfattn_gate,
        perceptron_offset,
        perceptron_scale,
        perceptron_gate,
    ) = segment_list
    fetched = (
        lax.all_gather(inproj_weight, "wide", axis=0, tiled=True),
        lax.all_gather(inproj_bias, "wide", axis=0, tiled=True),
        lax.all_gather(outproj_weight, "wide", axis=0, tiled=True),
        lax.all_gather(outproj_bias, "wide", axis=0, tiled=True),
        lax.all_gather(up_weight, "wide", axis=0, tiled=True),
        lax.all_gather(up_bias, "wide", axis=0, tiled=True),
        lax.all_gather(down_weight, "wide", axis=0, tiled=True),
        lax.all_gather(down_bias, "wide", axis=0, tiled=True),
    )
    w_inproj, b_inproj, w_outproj, b_outproj, w_up, b_up, w_down, b_down = fetched
    input_rows = patches.astype(jnp.float32)
    normalized_first, inverse_deviation = normalize(input_rows)
    first_input = (
        (normalized_first * (1.0 + selfattn_scale) + selfattn_offset)
        .astype(jnp.bfloat16)
        .reshape(row_total, model_width)
    )
    proj_bias = b_inproj.astype(jnp.float32)
    full_bias = jnp.concatenate(
        [proj_bias[:model_width], jnp.zeros((model_width,), jnp.float32), proj_bias[model_width:]]
    )
    projected = (matmul_rows(first_input, w_inproj) + full_bias).astype(jnp.bfloat16)
    query_rows = projected[:, :model_width].reshape(slots, seq_len, HEADS, head_dim)
    key_rows = projected[:, model_width : 2 * model_width].reshape(slots, seq_len, HEADS, head_dim)
    value_rows = projected[:, 2 * model_width :].reshape(slots, seq_len, HEADS, head_dim)
    scores = (
        jnp.einsum("sqhe,skhe->shqk", query_rows, key_rows, preferred_element_type=jnp.float32)
        * scale_qk
    )
    log_total = jax.nn.logsumexp(scores, axis=-1, keepdims=True)
    probs = jnp.exp(scores - log_total).astype(jnp.bfloat16)
    attended = jnp.einsum("shqk,skhe->sqhe", probs, value_rows, preferred_element_type=jnp.float32)
    attended = attended.astype(jnp.bfloat16).reshape(row_total, model_width)
    residual_branch = (matmul_rows(attended, w_outproj) + b_outproj.astype(jnp.float32)).reshape(
        slots, seq_len, model_width
    )
    between_state = input_rows + selfattn_gate * residual_branch
    normed_b, inv_b = normalize(between_state)
    second_in = (
        (normed_b * (1.0 + perceptron_scale) + perceptron_offset)
        .astype(jnp.bfloat16)
        .reshape(row_total, model_width)
    )
    hidden = matmul_rows(second_in, w_up) + b_up.astype(jnp.float32)
    gelu_value, gelu_pull = jax.vjp(partial(jax.nn.gelu, approximate=True), hidden)
    activated = gelu_value.astype(jnp.bfloat16)
    mlp_out = (matmul_rows(activated, w_down) + b_down.astype(jnp.float32)).reshape(
        slots, seq_len, model_width
    )
    output = ((between_state + perceptron_gate * mlp_out) * live).astype(jnp.bfloat16)
    back_weights = (
        lax.all_gather(inproj_weight, "wide", axis=0, tiled=True),
        lax.all_gather(inproj_bias, "wide", axis=0, tiled=True),
        lax.all_gather(outproj_weight, "wide", axis=0, tiled=True),
        lax.all_gather(outproj_bias, "wide", axis=0, tiled=True),
        lax.all_gather(up_weight, "wide", axis=0, tiled=True),
        lax.all_gather(up_bias, "wide", axis=0, tiled=True),
        lax.all_gather(down_weight, "wide", axis=0, tiled=True),
        lax.all_gather(down_bias, "wide", axis=0, tiled=True),
    )
    wb_inproj, _, wb_outproj, _, wb_up, _, wb_down, _ = back_weights
    grad_out = cotangent.astype(jnp.float32) * live
    grad_gate_mlp = jnp.sum(grad_out * mlp_out, axis=1)
    grad_mlp = (grad_out * perceptron_gate).astype(jnp.bfloat16).reshape(row_total, model_width)
    grad_down_bias = jnp.sum(grad_mlp.astype(jnp.float32), axis=0)
    grad_act = matmul_back(grad_mlp, wb_down)
    grad_hidden = gelu_pull(grad_act)[0].astype(jnp.bfloat16)
    grad_up_bias = jnp.sum(grad_hidden.astype(jnp.float32), axis=0)
    grad_second = matmul_back(grad_hidden, wb_up).reshape(slots, seq_len, model_width)
    grad_scale_mlp = jnp.sum(grad_second * normed_b, axis=1)
    grad_shift_mlp = jnp.sum(grad_second, axis=1)
    between_gradient = grad_out + normalize_reverse(
        normed_b, inv_b, grad_second * (1.0 + perceptron_scale)
    )
    selfattn_gate_gradient = jnp.sum(between_gradient * residual_branch, axis=1)
    residual_branch_gradient = (
        (between_gradient * selfattn_gate).astype(jnp.bfloat16).reshape(row_total, model_width)
    )
    grad_outproj_bias = jnp.sum(residual_branch_gradient.astype(jnp.float32), axis=0)
    grad_attended = (
        matmul_back(residual_branch_gradient, wb_outproj)
        .astype(jnp.bfloat16)
        .reshape(slots, seq_len, HEADS, head_dim)
    )
    scores_again = (
        jnp.einsum("sqhe,skhe->shqk", query_rows, key_rows, preferred_element_type=jnp.float32)
        * scale_qk
    )
    probs_full = jnp.exp(scores_again - log_total)
    grad_values = jnp.einsum(
        "shqk,sqhe->skhe",
        probs_full.astype(jnp.bfloat16),
        grad_attended,
        preferred_element_type=jnp.float32,
    )
    grad_probs = jnp.einsum(
        "sqhe,skhe->shqk", grad_attended, value_rows, preferred_element_type=jnp.float32
    )
    row_dot = jnp.sum(grad_probs * probs_full, axis=-1, keepdims=True)
    grad_scores = (probs_full * (grad_probs - row_dot)).astype(jnp.bfloat16)
    grad_queries = (
        jnp.einsum("shqk,skhe->sqhe", grad_scores, key_rows, preferred_element_type=jnp.float32)
        * scale_qk
    )
    grad_keys = (
        jnp.einsum("shqk,sqhe->skhe", grad_scores, query_rows, preferred_element_type=jnp.float32)
        * scale_qk
    )
    grad_projected = jnp.concatenate(
        [
            grad_queries.reshape(row_total, model_width),
            grad_keys.reshape(row_total, model_width),
            grad_values.reshape(row_total, model_width),
        ],
        axis=1,
    ).astype(jnp.bfloat16)
    proj_sums = jnp.sum(grad_projected.astype(jnp.float32), axis=0)
    grad_inproj_bias = jnp.concatenate([proj_sums[:model_width], proj_sums[2 * model_width :]])
    first_gradient = matmul_back(grad_projected, wb_inproj).reshape(slots, seq_len, model_width)
    selfattn_scale_gradient = jnp.sum(first_gradient * normalized_first, axis=1)
    selfattn_offset_gradient = jnp.sum(first_gradient, axis=1)
    grad_patches = (
        between_gradient
        + normalize_reverse(
            normalized_first, inverse_deviation, first_gradient * (1.0 + selfattn_scale)
        )
    ).astype(jnp.bfloat16)
    grad_modulation = jnp.concatenate(
        [
            selfattn_offset_gradient,
            selfattn_scale_gradient,
            selfattn_gate_gradient,
            grad_shift_mlp,
            grad_scale_mlp,
            grad_gate_mlp,
        ],
        axis=1,
    ).astype(jnp.bfloat16)
    grad_mod_part = lax.all_to_all(grad_modulation, "wide", split_axis=1, concat_axis=0, tiled=True)
    grad_ada_weight = matmul_outer(cond_all, grad_mod_part)
    grad_ada_bias = jnp.sum(grad_mod_part.astype(jnp.float32), axis=0)
    grad_cond_part = matmul_back(grad_mod_part, ada_weight)
    grad_cond_act = lax.psum_scatter(
        grad_cond_part.astype(jnp.bfloat16), "wide", scatter_dimension=0, tiled=True
    ).astype(jnp.float32)
    _, silu_pull = jax.vjp(jax.nn.silu, condition)
    grad_condition = silu_pull(grad_cond_act)[0]
    bias_shares = (
        lax.psum_scatter(
            grad_inproj_bias.astype(jnp.bfloat16), "wide", scatter_dimension=0, tiled=True
        ).astype(jnp.float32),
        lax.psum_scatter(
            grad_outproj_bias.astype(jnp.bfloat16), "wide", scatter_dimension=0, tiled=True
        ).astype(jnp.float32),
        lax.psum_scatter(
            grad_up_bias.astype(jnp.bfloat16), "wide", scatter_dimension=0, tiled=True
        ).astype(jnp.float32),
        lax.psum_scatter(
            grad_down_bias.astype(jnp.bfloat16), "wide", scatter_dimension=0, tiled=True
        ).astype(jnp.float32),
    )
    ff_width = activated.shape[1]
    input_factors = (
        (first_input, grad_projected, 0),
        (attended, residual_branch_gradient, 3 * model_width),
        (second_in, grad_hidden, 4 * model_width),
    )
    down_factors = ((activated, grad_mlp, 0),)
    input_block = (4 * model_width + ff_width) // 4
    down_block = model_width // 2
    block_jobs = [
        (input_factors, model_width, number * input_block, input_block) for number in range(4)
    ]
    block_jobs = block_jobs + [
        (down_factors, ff_width, number * down_block, down_block) for number in range(2)
    ]

    def reduce_block(factors, rows, first, width):
        return lax.psum_scatter(
            block_term(factors, lax.axis_size("wide") * (rows // wide_count), first, width).astype(
                jnp.bfloat16
            ),
            "wide",
            scatter_dimension=0,
            tiled=True,
        ).astype(jnp.float32)

    shards = [reduce_block(*job) for job in block_jobs]
    input_grads = jnp.concatenate(shards[:4], axis=1)
    grad_down_weight = jnp.concatenate(shards[4:], axis=1)
    summed = (
        lax.psum(grad_ada_weight.astype(jnp.bfloat16), "narrow").astype(jnp.float32),
        lax.psum(grad_ada_bias.astype(jnp.bfloat16), "narrow").astype(jnp.float32),
        lax.psum(input_grads[:, : 3 * model_width].astype(jnp.bfloat16), "narrow").astype(
            jnp.float32
        ),
        lax.psum(bias_shares[0].astype(jnp.bfloat16), "narrow").astype(jnp.float32),
        lax.psum(
            input_grads[:, 3 * model_width : 4 * model_width].astype(jnp.bfloat16), "narrow"
        ).astype(jnp.float32),
        lax.psum(bias_shares[1].astype(jnp.bfloat16), "narrow").astype(jnp.float32),
        lax.psum(input_grads[:, 4 * model_width :].astype(jnp.bfloat16), "narrow").astype(
            jnp.float32
        ),
        lax.psum(bias_shares[2].astype(jnp.bfloat16), "narrow").astype(jnp.float32),
        lax.psum(grad_down_weight.astype(jnp.bfloat16), "narrow").astype(jnp.float32),
        lax.psum(bias_shares[3].astype(jnp.bfloat16), "narrow").astype(jnp.float32),
    )
    return (
        output,
        grad_patches,
        grad_condition,
        summed[0],
        summed[1],
        summed[2],
        summed[3],
        summed[4],
        summed[5],
        summed[6],
        summed[7],
        summed[8],
        summed[9],
    )


def solution(mesh):
    in_specs = (
        P(("narrow", "wide"), None, None),
        P(("narrow", "wide"), None),
        P(("narrow", "wide")),
        P(None, "wide"),
        P("wide"),
        P("wide", None),
        P("wide"),
        P("wide", None),
        P("wide"),
        P("wide", None),
        P("wide"),
        P("wide", None),
        P("wide"),
        P(("narrow", "wide"), None, None),
    )
    out_specs = (
        P(("narrow", "wide"), None, None),
        P(("narrow", "wide"), None, None),
        P(("narrow", "wide"), None),
        P(None, "wide"),
        P("wide"),
        P("wide", None),
        P("wide"),
        P("wide", None),
        P("wide"),
        P("wide", None),
        P("wide"),
        P("wide", None),
        P("wide"),
    )
    return jax.shard_map(
        per_device, mesh=mesh, in_specs=in_specs, out_specs=out_specs, check_vma=False
    )
```

profile of v0, /device:TPU:0, one launch (start us, length us, event | category | flops | bytes accessed | tf_op | source)
XLA Modules:
  0.0 1012.4 jit_solution(17286262413155684345)
XLA Ops:
  10.9 23.9 %all-gather = bf16[16,2,1152]{2,1,0:T(2,128)(2,1)S(1)} all-gather(bf16[1,2,1152]{2,1,0:T(2,128)(2,1)S(1)} %fusion.42), channel_id=1, replica_groups=mesh['narrow'=2,'wide'=16] {'wide'}, dimensions={0}, use_global_device_ids=true | all-gather | bytes 78336 | tf_op jit(solution)/shard_map/all_gather | solution.py:77
  44.1 64.5 %all-reduce.10 = (bf16[2304]{0:T(1024)(128)(2,1)S(1)}, bf16[1152]{0:T(1024)(128)(2,1)S(1)}, bf16[4608]{0:T(1024)(128)(2,1)S(1)}) all-reduce(bf16[2304]{0:T(1024)(128)(2,1)S(1)} %dynamic-update-slice, bf16[1152]{0:T(1024)(128)(2,1)S(1)} %dynamic-update-slice.1, ...), channel_id=1, replica_groups=mesh['narrow'=2,'wide'=16] {'wide'}, use_global_device_ids=true, to_apply=%add | all-reduce | flops 8064 | bytes 32256
  116.3 8.9 add_convert_fusion
  168.6 50.5 %all-gather.10.cloned.1.call-done = bf16[1152,4608]{1,0:T(8,128)(2,1)} async-done(((bf16[72,4608]{1,0:T(8,128)(2,1)}), bf16[1152,4608]{1,0:T(8,128)(2,1)}) %all-gather.10.cloned.1.call-update) | async-done | bytes 10616848 | tf_op jit(solution)/shard_map/all_gather | solution.py:101
  219.0 13.7 %multiply_convert_fusion = (bf16[512,4608]{1,0:T(8,128)(2,1)}, f32[512,4608]{1,0:T(8,128)}) fusion(f32[4608]{0:T(1024)S(1)} %copy-done.51, bf16[512,1152]{1,0:T(8,128)(2,1)} %bitcast.131, bf16[1152,4608]{1,0:T(8,128)(2,1)} %all-gather.10.cloned.1.call-done), kind=kOutput, calls=%fused_computation.12 | convolution fusion | flops 5459410944 | bytes 25970688 | tf_op jit(solution)/shard_map/dot_general | solution.py:28
  232.7 75.1 %all-gather.12.cloned.1.call-done = bf16[4608,1152]{1,0:T(8,128)(2,1)} async-done(((bf16[288,1152]{1,0:T(8,128)(2,1)}), bf16[4608,1152]{1,0:T(8,128)(2,1)}) %all-gather.12.cloned.1.call-update) | async-done | bytes 10616848 | tf_op jit(solution)/shard_map/all_gather | solution.py:103
  307.8 16.0 %fusion.47 = (bf16[4608]{0:T(1024)(128)(2,1)S(1)}, bf16[512,4608]{1,0:T(8,128)(2,1)S(1)}) fusion(f32[512,4608]{1,0:T(8,128)} %get-tuple-element.67, f32[4608]{0:T(1024)S(1)} %copy-done.51, bf16[512,1152]{1,0:T(8,128)(2,1)} %bitcast.125, bf16[4608,1152]{1,0:T(8,128)(2,1)} %all-gather.12.cloned.1.call-done), kind=kOutput, calls=%fused_computation.124 | convolution fusion | flops 5487717888 | bytes 25979904 | tf_op jit(solution)/shard_map/dot_general | solution.py:32
  331.1 7.4 convolution_convert_fusion
  338.6 13.5 %fusion.29 = (f32[512]{0:T(512)S(1)}, f32[512,1152]{1,0:T(8,128)}) fusion(f32[2,1152]{1,0:T(2,128)S(1)} %get-tuple-element.52, bf16[512,4608]{1,0:T(8,128)(2,1)} %copy-done.60, bf16[1152,4608]{1,0:T(8,128)(2,1)} %all-gather.10.cloned.1.call-done), kind=kOutput, calls=%fused_computation.56 | convolution fusion | flops 5436997120 | bytes 17705984 | tf_op jit(solution)/shard_map/dot_general | solution.py:32
  372.9 6.4 multiply_reduce_fusion
  390.5 5.9 convolution_convert_fusion.2
  410.0 8.9 convolution_convert_fusion.4
  419.0 12.5 %reduce-scatter.17.cloned.1.call-start = ((), (), s32[]{:S(2)}) async-start(), calls=%async_computation.17 | async-start | bytes 6266880 | tf_op jit(solution)/shard_map/reduce_scatter | solution.py:275
  431.5 8.9 convolution_convert_fusion.3
  448.7 60.2 %all-reduce.9 = (bf16[1152]{0:T(1024)(128)(2,1)S(1)}, bf16[2304]{0:T(1024)(128)(2,1)S(1)}, bf16[1152]{0:T(1024)(128)(2,1)S(1)}, bf16[4608]{0:T(1024)(128)(2,1)S(1)}, bf16[1152]{0:T(1024)(128)(2,1)S(1)}) all-reduce(bf16[1152]{0:T(1024)(128)(2,1)S(1)} %dynamic-update-slice.3, ...), channel_id=1, replica_groups=mesh['narrow'=2,'wide'=16] {'wide'}, use_global_device_ids=true, to_apply=%add.3 | all-reduce | flops 10368 | bytes 41472
  509.0 9.6 fusion.28
  520.1 10.0 convolution_add_fusion
  532.1 9.7 all_to_all.29
  546.2 24.3 %reduce-scatter.7.cloned.1.call-done = bf16[72,2304]{1,0:T(8,128)(2,1)} async-done(((bf16[1152,2304]{1,0:T(8,128)(2,1)}), bf16[72,2304]{1,0:T(8,128)(2,1)}) %reduce-scatter.7.cloned.1.call-update) | async-done | bytes 331792 | tf_op jit(solution)/shard_map/reduce_scatter | solution.py:275
  570.5 81.2 %reduce-scatter.9.cloned.1.call-done = bf16[72,2304]{1,0:T(8,128)(2,1)} async-done(((bf16[1152,2304]{1,0:T(8,128)(2,1)}), bf16[72,2304]{1,0:T(8,128)(2,1)}) %reduce-scatter.9.cloned.1.call-update) | async-done | bytes 331792 | tf_op jit(solution)/shard_map/reduce_scatter | solution.py:275
  653.6 83.3 %reduce-scatter.15.cloned.1.call-done = bf16[288,576]{1,0:T(8,128)(2,1)} async-done(((bf16[4608,576]{1,0:T(8,128)(2,1)}), bf16[288,576]{1,0:T(8,128)(2,1)}) %reduce-scatter.15.cloned.1.call-update) | async-done | bytes 331792 | tf_op jit(solution)/shard_map/reduce_scatter | solution.py:275
  736.9 85.3 %reduce-scatter.17.cloned.1.call-done = bf16[288,576]{1,0:T(8,128)(2,1)} async-done(((bf16[4608,576]{1,0:T(8,128)(2,1)}), bf16[288,576]{1,0:T(8,128)(2,1)}) %reduce-scatter.17.cloned.1.call-update) | async-done | bytes 331792 | tf_op jit(solution)/shard_map/reduce_scatter | solution.py:275
  840.0 71.6 %all-reduce.16.cloned.1.call-done = bf16[32,1152]{1,0:T(8,128)(2,1)} async-done(((bf16[32,1152]{1,0:T(8,128)(2,1)}), bf16[32,1152]{1,0:T(8,128)(2,1)}) %all-reduce.16.cloned.1.call-update) | async-done | bytes 73744
  912.9 85.7 %all-reduce.18.cloned.1.call-done = (bf16[1152,432]{0,1:T(8,128)(2,1)}, bf16[72,3456]{1,0:T(8,128)(2,1)}, bf16[72,1152]{1,0:T(8,128)(2,1)}, bf16[72,4608]{1,0:T(8,128)(2,1)}, bf16[288,1152]{1,0:T(8,128)(2,1)}) async-done(((bf16[1152,432]{0,1:T(8,128)(2,1)}, bf16[72,3456]{1,0:T(8,128)(2,1)}, bf16[72,1152]{1,0:T(8,128)(2,1)}, bf16[72,4608]{1,0:T(8,128)(2,1)}, bf16[288,1152]{1,0:T(8,128)(2,1)}), ...) | async-done | bytes 2986000 | tf_op jit(solution)/shard_map/psum | solution.py:288
  (269 shorter events, 155.1 us)
Async XLA Ops:
  7.2 36.1 %copy-start.57 = (bf16[72]{0:T(256)(128)(2,1)S(1)}, bf16[72]{0:T(256)(128)(2,1)}, u32[]{:S(2)}) copy-start(bf16[72]{0:T(256)(128)(2,1)} %param.22) | copy-start | bytes 436
  7.2 36.4 %copy-start.56 = (bf16[288]{0:T(512)(128)(2,1)S(1)}, bf16[288]{0:T(512)(128)(2,1)}, u32[]{:S(2)}) copy-start(bf16[288]{0:T(512)(128)(2,1)} %param.24) | copy-start | bytes 1732
  7.2 36.6 %copy-start.58 = (bf16[144]{0:T(256)(128)(2,1)S(1)}, bf16[144]{0:T(256)(128)(2,1)}, u32[]{:S(2)}) copy-start(bf16[144]{0:T(256)(128)(2,1)} %param.20) | copy-start | bytes 868
  7.2 101.9 %copy-start.2 = (bf16[2,256,1152]{2,1,0:T(8,128)(2,1)S(1)}, bf16[2,256,1152]{2,1,0:T(8,128)(2,1)}, u32[]{:S(2)}) copy-start(bf16[2,256,1152]{2,1,0:T(8,128)(2,1)} %param.14) | copy-start | bytes 3538948
  7.2 109.0 %all-gather.6.cloned.1.call-start = ((), (), s32[]{:S(2)}) async-start(), calls=%async_computation.8 | async-start | bytes 8460288 | tf_op jit(solution)/shard_map/all_gather | solution.py:97
  8.0 152.9 %all-gather.8.cloned.1.call-start = ((), (), s32[]{:S(2)}) async-start(), calls=%async_computation.9 | async-start | bytes 2820096 | tf_op jit(solution)/shard_map/all_gather | solution.py:99
  8.7 210.3 %all-gather.10.cloned.1.call-start = ((), (), s32[]{:S(2)}) async-start(), calls=%async_computation.10 | async-start | bytes 11280384 | tf_op jit(solution)/shard_map/all_gather | solution.py:101
  9.5 298.3 %all-gather.12.cloned.1.call-start = ((), (), s32[]{:S(2)}) async-start(), calls=%async_computation.11 | async-start | bytes 11280384 | tf_op jit(solution)/shard_map/all_gather | solution.py:103
  10.0 102.9 %copy-start.15 = (bf16[2,256,1152]{2,1,0:T(8,128)(2,1)S(1)}, bf16[2,256,1152]{2,1,0:T(8,128)(2,1)}, u32[]{:S(2)}) copy-start(bf16[2,256,1152]{2,1,0:T(8,128)(2,1)} %param.27) | copy-start | bytes 3538948
  34.8 80.9 %copy-start.34 = (bf16[32,1152]{1,0:T(8,128)(2,1)}, bf16[32,1152]{1,0:T(8,128)(2,1)S(1)}, u32[]{:S(2)}) copy-start(bf16[32,1152]{1,0:T(8,128)(2,1)S(1)} %reshape.206) | copy-start | bytes 221188
  36.5 75.6 %all-to-all-start = ((bf16[16,2,432]{2,1,0:T(2,128)(2,1)}), bf16[16,2,432]{2,1,0:T(2,128)(2,1)S(1)}, u32[]{:S(2)}, u32[]{:S(2)}) async-start(bf16[16,2,432]{2,1,0:T(2,128)(2,1)} %all_to_all.22), calls=%async_computation | async-start | bytes 65536 | tf_op jit(solution)/shard_map/all_to_all | solution.py:81
  40.0 504.2 %reduce-scatter.11.cloned.1.call-start = ((), (), s32[]{:S(2)}) async-start(), calls=%async_computation.14 | async-start | bytes 5640192 | tf_op jit(solution)/shard_map/reduce_scatter | solution.py:275
  166.7 52.3 %copy-start.51 = (f32[4608]{0:T(1024)S(1)}, f32[4608]{0:T(1024)}, u32[]{:S(2)}) copy-start(f32[4608]{0:T(1024)} %convert_element_type.192) | copy-start | bytes 55300
  331.1 213.2 %reduce-scatter.13.cloned.1.call-start = ((), (), s32[]{:S(2)}) async-start(), calls=%async_computation.15 | async-start | bytes 5640192 | tf_op jit(solution)/shard_map/reduce_scatter | solution.py:275
  338.5 232.0 %reduce-scatter.7.cloned.1.call-start = ((), (), s32[]{:S(2)}) async-start(), calls=%async_computation.12 | async-start | bytes 5640192 | tf_op jit(solution)/shard_map/reduce_scatter | solution.py:275
  396.4 255.3 %reduce-scatter.9.cloned.1.call-start = ((), (), s32[]{:S(2)}) async-start(), calls=%async_computation.13 | async-start | bytes 5640192 | tf_op jit(solution)/shard_map/reduce_scatter | solution.py:275
  410.0 326.9 %reduce-scatter.15.cloned.1.call-start = ((), (), s32[]{:S(2)}) async-start(), calls=%async_computation.16 | async-start | bytes 6266880 | tf_op jit(solution)/shard_map/reduce_scatter | solution.py:275
  419.0 403.2 %reduce-scatter.17.cloned.1.call-start = ((), (), s32[]{:S(2)}) async-start(), calls=%async_computation.17 | async-start | bytes 6266880 | tf_op jit(solution)/shard_map/reduce_scatter | solution.py:275
  440.5 471.1 %all-reduce.16.cloned.1.call-start = ((), (), s32[]{:S(2)}) async-start(), calls=%async_computation.18 | async-start | bytes 147456
  446.1 62.9 %copy-start.42 = (f32[2,1152]{1,0:T(2,128)S(1)}, f32[2,1152]{1,0:T(2,128)}, u32[]{:S(2)}) copy-start(f32[2,1152]{1,0:T(2,128)} %copy-done.41) | copy-start | bytes 27652
  544.1 454.4 %all-reduce.18.cloned.1.call-start = ((), (), s32[]{:S(2)}) async-start(), calls=%async_computation.19 | async-start | bytes 5971968 | tf_op jit(solution)/shard_map/psum | solution.py:288
  651.7 172.6 %copy-start.33 = (bf16[72,2304]{1,0:T(8,128)(2,1)S(1)}, bf16[72,2304]{1,0:T(8,128)(2,1)}, u32[]{:S(2)}) copy-start(bf16[72,2304]{1,0:T(8,128)(2,1)} %reduce-scatter.9.cloned.1.call-done) | copy-start | bytes 995332
  653.6 174.4 %copy-start.5 = (bf16[2,256,1152]{2,1,0:T(8,128)(2,1)S(1)}, bf16[2,256,1152]{2,1,0:T(8,128)(2,1)}, u32[]{:S(2)}) copy-start(bf16[2,256,1152]{2,1,0:T(8,128)(2,1)} %param.14) | copy-start | bytes 3538948
  828.0 83.6 %copy-start.47 = (f32[2,1152]{1,0:T(2,128)S(1)}, f32[2,1152]{1,0:T(2,128)}, u32[]{:S(2)}) copy-start(f32[2,1152]{1,0:T(2,128)} %param.15) | copy-start | bytes 27652
  (50 other events, 264.7 us)
Sparse Core Ops, SparseCore 0:
  10.2 75.2 all-gather.5
  87.7 41.8 all-gather.7
  131.9 87.1 all-gather.9
  221.2 86.5 all-gather.11
  331.2 76.3 reduce-scatter.10
  411.5 77.3 reduce-scatter.12
  493.0 77.5 reduce-scatter.6
  574.5 77.0 reduce-scatter.8
  655.6 81.2 reduce-scatter.14
  740.7 81.4 reduce-scatter.16
  825.7 85.8 all-reduce.15
  915.2 83.3 all-reduce.17
where the time goes:
time: 1020 us; the launch traced here: 1010 us
  waiting for transfers between devices  560 us (55%)
  blocking collectives  163 us (16%)
  matrix products  140 us (14%)
  local copies, waits for them, and re-layouts  60.8 us (6%)
  other arithmetic  51.9 us (5%)
  between operations  20.5 us (2%)
  starting transfers between devices  16.8 us (2%)
    reduce_scatter x6, waiting for transfers between devices, reduce_block(): lax.psum_scatter(block_term(factors, lax.axis_size('wide') * (rows // wid...  274 us
    unnamed x2, blocking collectives  125 us
    psum x1, waiting for transfers between devices, per_device(): lax.psum(grad_ada_weight.astype(jnp.bfloat16), 'narrow').astype(jnp.float32)  85.7 us
    all_gather x1, waiting for transfers between devices, per_device(): lax.all_gather(down_weight, 'wide', axis=0, tiled=True)  75.1 us
    unnamed x13, waiting for transfers between devices  74.3 us
    all_gather x1, waiting for transfers between devices, per_device(): lax.all_gather(up_weight, 'wide', axis=0, tiled=True)  50.5 us
    dot_general x5, matrix products, matmul_back(): lax.dot_general(left, right, (((1,), (1,)), ((), ())), preferred_element_...  43 us
    dot_general x8, matrix products, matmul_outer(): lax.dot_general(left, right, (((0,), (0,)), ((), ())), preferred_element_...  41 us
  transfers between devices with their start and end apart: 13, of which 8 were waited for; matrix products, arithmetic and copies ran while one was open for 21% of the time, Pallas kernels for 0%

commit v1 on v0

--- a/solution.py
+++ b/solution.py
@@ -5,7 +5,12 @@
 from jax import lax
 from jax.sharding import PartitionSpec as P
 
+from jax.experimental import pallas as pl
+from jax.experimental.pallas import tpu as pltpu
+
 HEADS = 16
+MESH = pl.DeviceIdType.MESH
+DEPTH = 2
 
 
 norm_eps = 1e-06
@@ -49,6 +54,243 @@
             rows_part = lax.slice_in_dim(left, 0, count, axis=1)
             pieces.append(matmul_outer(rows_part, right[:, lower - base : upper - base]))
     return jnp.concatenate(pieces, axis=1)
+
+LANES = 384
+PER_HALF = 18
+
+
+def reduce_kernel(
+    at_ref, b_ref, out_ref,
+    bbuf, gbuf, sbuf, tbuf, ubuf, fbuf, core_in, one_in, two_in, z_in, far_in,
+    bsem, core_sem, one_sem, two_sem, zs_sem, zr_sem, far_sem,
+):
+    narrow = lax.axis_index("narrow")
+    wide = lax.axis_index("wide")
+    core = wide % 2
+    row = (wide // 2) % 2
+    deep = wide // 4
+    core_peer = (narrow, wide + 1 - 2 * core)
+    x_peer = (1 - narrow, wide)
+    y_peer = (narrow, wide + 2 - 4 * row)
+    z_to = [(narrow, (deep + o) % 4 * 4 + wide % 4) for o in (1, 2, 3)]
+
+    barrier = pltpu.get_barrier_semaphore()
+    for peer in [core_peer, x_peer, y_peer] + z_to:
+        pl.semaphore_signal(barrier, inc=1, device_id=peer, device_id_type=MESH)
+    pl.semaphore_wait(barrier, 6)
+
+    def fetch(chunk, half):
+        number = chunk + half * PER_HALF
+        column = number - 3 * ((number - 24) // 3) * (number // 24)
+        column = pl.multiple_of(column * LANES, LANES)
+        return pltpu.make_async_copy(
+            b_ref.at[:, pl.ds(column, LANES)], bbuf.at[half], bsem.at[half]
+        )
+
+    def send(src, dst, sems, chunk, peer):
+        return pltpu.make_async_remote_copy(
+            src_ref=src, dst_ref=dst, send_sem=sems.at[0, chunk], recv_sem=sems.at[1, chunk],
+            device_id=peer, device_id_type=MESH,
+        )
+
+    def core_copy(chunk):
+        return send(gbuf.at[1 - core], core_in.at[chunk], core_sem, chunk, core_peer)
+
+    def one_copy(chunk, even):
+        slot = chunk % DEPTH
+        if even:
+            return send(sbuf.at[slot, 1 - narrow], one_in.at[chunk], one_sem, chunk, x_peer)
+        return send(sbuf.at[slot, 1 - row], one_in.at[chunk], one_sem, chunk, y_peer)
+
+    def two_copy(chunk, even):
+        slot = chunk % DEPTH
+        if even:
+            return send(tbuf.at[slot, 1 - row], two_in.at[chunk], two_sem, chunk, y_peer)
+        return send(tbuf.at[slot, 1 - narrow], two_in.at[chunk], two_sem, chunk, x_peer)
+
+    def z_copies(chunk):
+        slot = chunk % DEPTH
+        return [
+            pltpu.make_async_remote_copy(
+                src_ref=ubuf.at[slot, (deep + o) % 4], dst_ref=z_in.at[chunk, o - 1],
+                send_sem=zs_sem.at[chunk, o - 1], recv_sem=zr_sem.at[chunk, o - 1],
+                device_id=z_to[o - 1], device_id_type=MESH,
+            )
+            for o in (1, 2, 3)
+        ]
+
+    def far_copy(chunk):
+        return send(fbuf.at[chunk], far_in.at[chunk], far_sem, chunk, x_peer)
+
+    def add(left, right):
+        return left.astype(jnp.float32) + right.astype(jnp.float32)
+
+    def make(chunk):
+        for half in range(2):
+            number = chunk + half * PER_HALF
+            which = (
+                jnp.where(number >= 9, 1, 0) + jnp.where(number >= 12, 1, 0)
+                + jnp.where(number >= 24, 1, 0) + jnp.where(number >= 27, 1, 0)
+                + jnp.where(number >= 30, 1, 0) + jnp.where(number >= 33, 1, 0)
+            )
+            fetch(chunk, half).wait()
+            for side in range(2):
+                product = jnp.dot(
+                    at_ref[which, side], bbuf[half], preferred_element_type=jnp.float32
+                )
+                for unit in range(8):
+                    gbuf[side, half, unit] = product[unit * 72 : unit * 72 + 72].astype(jnp.bfloat16)
+
+            @pl.when(chunk + 1 < PER_HALF)
+            def _():
+                fetch(chunk + 1, half).start()
+
+        core_copy(chunk).start()
+
+    def pair(chunk, even):
+        core_copy(chunk).wait()
+        slot = chunk % DEPTH
+
+        def body(step, carry):
+            half, unit = step // 8, step % 8
+            value = add(gbuf[core, half, unit], core_in[chunk, half, unit]).astype(jnp.bfloat16)
+            deep_at, row_at = unit // 2, unit % 2
+            if even:
+                sbuf[slot, half, row_at, deep_at] = value
+            else:
+                sbuf[slot, row_at, half, deep_at] = value
+            return carry
+
+        lax.fori_loop(0, 16, body, 0)
+        one_copy(chunk, even).start()
+
+    def first(chunk, even):
+        one_copy(chunk, even).wait()
+        slot = chunk % DEPTH
+        mine = narrow if even else row
+
+        def body(step, carry):
+            outer, inner = step // 4, step % 4
+            tbuf[slot, outer, inner] = add(
+                sbuf[slot, mine, outer, inner], one_in[chunk, outer, inner]
+            ).astype(jnp.bfloat16)
+            return carry
+
+        lax.fori_loop(0, 8, body, 0)
+        two_copy(chunk, even).start()
+
+    def second(chunk, even):
+        two_copy(chunk, even).wait()
+        slot = chunk % DEPTH
+        mine = row if even else narrow
+
+        def body(step, carry):
+            ubuf[slot, step] = add(tbuf[slot, mine, step], two_in[chunk, step]).astype(jnp.bfloat16)
+            return carry
+
+        lax.fori_loop(0, 4, body, 0)
+        for copy in z_copies(chunk):
+            copy.start()
+
+    def third(chunk):
+        for copy in z_copies(chunk):
+            copy.wait()
+        total = add(ubuf[chunk % DEPTH, deep], z_in[chunk, 0])
+        total = total + add(z_in[chunk, 1], z_in[chunk, 2])
+        out_ref[narrow * PER_HALF + chunk] = total
+        fbuf[chunk] = total.astype(jnp.bfloat16)
+        far_copy(chunk).start()
+
+    for half in range(2):
+        fetch(0, half).start()
+
+    def turn(step, carry):
+        for parity in range(2):
+            now = step * 2 + parity
+            for lag, action, fixed in (
+                (1 + 3 * DEPTH, third, False),
+                (1 + 2 * DEPTH, second, True),
+                (1 + DEPTH, first, True),
+                (1, pair, True),
+                (0, make, False),
+            ):
+                chunk = now - lag
+                even = (parity - lag) % 2 == 0
+
+                @pl.when(jnp.logical_and(chunk >= 0, chunk < PER_HALF))
+                def _(action=action, fixed=fixed, chunk=chunk, even=even):
+                    action(chunk, even) if fixed else action(chunk)
+
+        return carry
+
+    lax.fori_loop(0, (PER_HALF + 3 * DEPTH + 2) // 2, turn, 0)
+
+    def finish(chunk, carry):
+        far_copy(chunk).wait()
+        out_ref[(1 - narrow) * PER_HALF + chunk] = far_in[chunk].astype(jnp.float32)
+        return carry
+
+    lax.fori_loop(0, PER_HALF, finish, 0)
+
+
+def reduce_weights(transposed, right):
+    bf = jnp.bfloat16
+    dma = pltpu.SemaphoreType.DMA
+    unit = (72, LANES)
+    n = PER_HALF
+    return pl.pallas_call(
+        reduce_kernel,
+        out_shape=jax.ShapeDtypeStruct((2 * n,) + unit, jnp.float32),
+        in_specs=[
+            pl.BlockSpec(memory_space=pltpu.VMEM),
+            pl.BlockSpec(memory_space=pl.ANY),
+        ],
+        out_specs=pl.BlockSpec(memory_space=pltpu.VMEM),
+        scratch_shapes=[
+            pltpu.VMEM((2, 512, LANES), bf),
+            pltpu.VMEM((2, 2, 8) + unit, bf),
+            pltpu.VMEM((DEPTH, 2, 2, 4) + unit, bf),
+            pltpu.VMEM((DEPTH, 2, 4) + unit, bf),
+            pltpu.VMEM((DEPTH, 4) + unit, bf),
+            pltpu.VMEM((n,) + unit, bf),
+            pltpu.VMEM((n, 2, 8) + unit, bf),
+            pltpu.VMEM((n, 2, 4) + unit, bf),
+            pltpu.VMEM((n, 4) + unit, bf),
+            pltpu.VMEM((n, 3) + unit, bf),
+            pltpu.VMEM((n,) + unit, bf),
+            dma((2,)),
+            dma((2, n)),
+            dma((2, n)),
+            dma((2, n)),
+            dma((n, 3)),
+            dma((n, 3)),
+            dma((2, n)),
+        ],
+        compiler_params=pltpu.CompilerParams(
+            collective_id=1, has_side_effects=True, vmem_limit_bytes=66_000_000
+        ),
+        name="reduce_weights",
+    )(transposed, right)
+
+
+def by_holder(left, parts):
+    tokens = left.shape[0]
+    rows = left.T.reshape(8, 2, parts, 72, tokens)
+    return rows.transpose(2, 1, 0, 3, 4).reshape(parts, 2, 576, tokens)
+
+
+def weight_grads(first_input, attended, second_in, activated, grad_projected, grad_branch, grad_hidden, grad_mlp):
+    transposed = jnp.concatenate(
+        [by_holder(first_input, 1), by_holder(attended, 1), by_holder(second_in, 1), by_holder(activated, 4)]
+    )
+    right = jnp.concatenate([grad_projected, grad_branch, grad_hidden, grad_mlp], axis=1)
+    done = reduce_weights(transposed, right)
+
+    def flat(lower, upper):
+        return done[lower:upper].transpose(1, 0, 2).reshape(72, (upper - lower) * LANES)
+
+    down = done[24:].reshape(4, 3, 72, LANES).transpose(0, 2, 1, 3).reshape(288, 3 * LANES)
+    return flat(0, 9), flat(9, 12), flat(12, 24), down
 
 
 def per_device(
@@ -281,41 +523,41 @@
             tiled=True,
         ).astype(jnp.float32)
 
-    shards = [reduce_block(*job) for job in block_jobs]
-    input_grads = jnp.concatenate(shards[:4], axis=1)
-    grad_down_weight = jnp.concatenate(shards[4:], axis=1)
-    summed = (
-        lax.psum(grad_ada_weight.astype(jnp.bfloat16), "narrow").astype(jnp.float32),
-        lax.psum(grad_ada_bias.astype(jnp.bfloat16), "narrow").astype(jnp.float32),
-        lax.psum(input_grads[:, : 3 * model_width].astype(jnp.bfloat16), "narrow").astype(
-            jnp.float32
-        ),
-        lax.psum(bias_shares[0].astype(jnp.bfloat16), "narrow").astype(jnp.float32),
-        lax.psum(
-            input_grads[:, 3 * model_width : 4 * model_width].astype(jnp.bfloat16), "narrow"
-        ).astype(jnp.float32),
-        lax.psum(bias_shares[1].astype(jnp.bfloat16), "narrow").astype(jnp.float32),
-        lax.psum(input_grads[:, 4 * model_width :].astype(jnp.bfloat16), "narrow").astype(
-            jnp.float32
-        ),
-        lax.psum(bias_shares[2].astype(jnp.bfloat16), "narrow").astype(jnp.float32),
-        lax.psum(grad_down_weight.astype(jnp.bfloat16), "narrow").astype(jnp.float32),
-        lax.psum(bias_shares[3].astype(jnp.bfloat16), "narrow").astype(jnp.float32),
-    )
+    if lax.axis_size("narrow") == 2 and wide_count == 16:
+        w_grads = weight_grads(
+            first_input, attended, second_in, activated,
+            grad_projected, residual_branch_gradient, grad_hidden, grad_mlp,
+        )
+    else:
+        shards = [reduce_block(*job) for job in block_jobs]
+        input_grads = jnp.concatenate(shards[:4], axis=1)
+        w_grads = tuple(
+            lax.psum(part.astype(jnp.bfloat16), "narrow").astype(jnp.float32)
+            for part in (
+                input_grads[:, : 3 * model_width],
+                input_grads[:, 3 * model_width : 4 * model_width],
+                input_grads[:, 4 * model_width :],
+                jnp.concatenate(shards[4:], axis=1),
+            )
+        )
+    small = [
+        lax.psum(part.astype(jnp.bfloat16), "narrow").astype(jnp.float32)
+        for part in (grad_ada_weight, grad_ada_bias) + bias_shares
+    ]
     return (
         output,
         grad_patches,
         grad_condition,
-        summed[0],
-        summed[1],
-        summed[2],
-        summed[3],
-        summed[4],
-        summed[5],
-        summed[6],
-        summed[7],
-        summed[8],
-        summed[9],
+        small[0],
+        small[1],
+        w_grads[0],
+        small[2],
+        w_grads[1],
+        small[3],
+        w_grads[2],
+        small[4],
+        w_grads[3],
+        small[5],
     )
 
 

time: 1020 us -> 853 us (0.84)
  waiting for transfers between devices: 560 us -> 236 us
  Pallas kernels: 0 us -> 175 us
  local copies, waits for them, and re-layouts: 60.8 us -> 116 us
  matrix products: 140 us -> 96.3 us
  blocking collectives: 163 us -> 151 us
    reduce_scatter x6 -> x0, waiting for transfers between devices: 274 us -> none  [reduce_block(): lax.psum_scatter(block_term(factors, lax.axis_size('wide') * (rows // wid...]
    pallas_call x0 -> x1, Pallas kernels: none -> 175 us  [reduce_weights(): pl.pallas_call(reduce_kernel, out_shape=jax.ShapeDtypeStruct((2 * n,) + u...]
    psum x1, waiting for transfers between devices: 85.7 us -> 41.3 us  [per_device(): lax.psum(part.astype(jnp.bfloat16), 'narrow').astype(jnp.float32)]
    dot_general x8 -> x1, matrix products: 41 us -> 1.41 us  [matmul_outer(): lax.dot_general(left, right, (((0,), (0,)), ((), ())), preferred_element_...]
    unnamed x147 -> x165, local copies, waits for them, and re-layouts: 17.1 us -> 36.5 us
    reshape x0 -> x9, local copies, waits for them, and re-layouts: none -> 13.6 us  [the longest x3 5.11 us: flat(): done[lower:upper].transpose(1, 0, 2).reshape(72, (upper - lower) * LANES)]
    reduce_scatter x6 -> x0, starting transfers between devices: 13.1 us -> none  [reduce_block(): lax.psum_scatter(block_term(factors, lax.axis_size('wide') * (rows // wid...]
    unnamed x13 -> x7, waiting for transfers between devices: 74.3 us -> 76.4 us
  transfers between devices with their start and end apart: 13 -> 8, of which waited for: 8 -> 4; matrix products, arithmetic and copies ran while one was open for 21% -> 12% of each run, Pallas kernels for 0% -> 0%
where the time goes in v1:
time: 853 us; the launch traced here: 843 us
  waiting for transfers between devices  236 us (28%)
  Pallas kernels  175 us (21%)
  blocking collectives  151 us (18%)
  local copies, waits for them, and re-layouts  116 us (14%)
  matrix products  96.3 us (11%)
  other arithmetic  41.7 us (5%)
  between operations  20.7 us (2%)
    pallas_call x1, Pallas kernels, reduce_weights(): pl.pallas_call(reduce_kernel, out_shape=jax.ShapeDtypeStruct((2 * n,) + u...  175 us
    unnamed x2, blocking collectives  122 us
    unnamed x7, waiting for transfers between devices  76.4 us
    all_gather x1, waiting for transfers between devices, per_device(): lax.all_gather(down_weight, 'wide', axis=0, tiled=True)  74.7 us
    all_gather x1, waiting for transfers between devices, per_device(): lax.all_gather(up_weight, 'wide', axis=0, tiled=True)  43.2 us
    psum x1, waiting for transfers between devices, per_device(): lax.psum(part.astype(jnp.bfloat16), 'narrow').astype(jnp.float32)  41.3 us
    dot_general x5, matrix products, matmul_rows(): return jnp.dot(left, right, preferred_element_type=jnp.float32)  39.9 us
    dot_general x5, matrix products, matmul_back(): lax.dot_general(left, right, (((1,), (1,)), ((), ())), preferred_element_...  39.6 us
  transfers between devices with their start and end apart: 8, of which 4 were waited for; matrix products, arithmetic and copies ran while one was open for 12% of the time, Pallas kernels for 0%

profile of v1, /device:TPU:0, one launch (start us, length us, event | category | flops | bytes accessed | tf_op | source)
XLA Modules:
  0.0 843.3 jit_solution(5734450958640715684)
XLA Ops:
  10.8 23.9 %all-gather = bf16[16,2,1152]{2,1,0:T(2,128)(2,1)S(1)} all-gather(bf16[1,2,1152]{2,1,0:T(2,128)(2,1)S(1)} %fusion.45), channel_id=1, replica_groups=mesh['narrow'=2,'wide'=16] {'wide'}, dimensions={0}, use_global_device_ids=true | all-gather | bytes 78336 | tf_op jit(solution)/shard_map/all_gather | solution.py:319
  43.9 63.9 %all-reduce.10 = (bf16[2304]{0:T(1024)(128)(2,1)S(1)}, bf16[1152]{0:T(1024)(128)(2,1)S(1)}, bf16[4608]{0:T(1024)(128)(2,1)S(1)}) all-reduce(bf16[2304]{0:T(1024)(128)(2,1)S(1)} %dynamic-update-slice, bf16[1152]{0:T(1024)(128)(2,1)S(1)} %dynamic-update-slice.1, ...), channel_id=1, replica_groups=mesh['narrow'=2,'wide'=16] {'wide'}, use_global_device_ids=true, to_apply=%add | all-reduce | flops 8064 | bytes 32256
  117.5 8.4 %add_convert_fusion = bf16[512,3456]{1,0:T(8,128)(2,1)S(1)} fusion(bf16[512,1152]{1,0:T(8,128)(2,1)S(1)} %bitcast.173, bf16[1152,3456]{1,0:T(8,128)(2,1)} %all-gather.6.cloned.1.call-done, f32[3456]{0:T(1024)S(1)} %pad_maximum_fusion.1), kind=kOutput, calls=%fused_computation.25 | convolution fusion | flops 4080402432 | bytes 12695040 | tf_op jit(solution)/shard_map/dot_general | solution.py:33
  127.3 4.6 reshape.272
  134.9 4.7 reshape.273
  142.7 6.0 reshape.274
  175.8 43.2 %all-gather.10.cloned.1.call-done = bf16[1152,4608]{1,0:T(8,128)(2,1)} async-done(((bf16[72,4608]{1,0:T(8,128)(2,1)}), bf16[1152,4608]{1,0:T(8,128)(2,1)}) %all-gather.10.cloned.1.call-update) | async-done | bytes 10616848 | tf_op jit(solution)/shard_map/all_gather | solution.py:343
  219.0 14.0 %fusion.14 = (bf16[4608,512]{0,1:T(8,128)(2,1)}, f32[512,4608]{1,0:T(8,128)}) fusion(f32[4608]{0:T(1024)S(1)} %convert_element_type.157, bf16[512,1152]{1,0:T(8,128)(2,1)} %bitcast.175, bf16[1152,4608]{1,0:T(8,128)(2,1)} %all-gather.10.cloned.1.call-done), kind=kOutput, calls=%fused_computation.17 | convolution fusion | flops 5459410944 | bytes 25970688 | tf_op jit(solution)/shard_map/dot_general | solution.py:33
  233.0 74.7 %all-gather.12.cloned.1.call-done = bf16[4608,1152]{1,0:T(8,128)(2,1)} async-done(((bf16[288,1152]{1,0:T(8,128)(2,1)}), bf16[4608,1152]{1,0:T(8,128)(2,1)}) %all-gather.12.cloned.1.call-update) | async-done | bytes 10616848 | tf_op jit(solution)/shard_map/all_gather | solution.py:345
  307.8 15.6 %fusion.53 = (bf16[4608]{0:T(1024)(128)(2,1)S(1)}, bf16[512,4608]{1,0:T(8,128)(2,1)S(1)}) fusion(f32[512,4608]{1,0:T(8,128)} %get-tuple-element.70, f32[4608]{0:T(1024)S(1)} %convert_element_type.157, bf16[512,1152]{1,0:T(8,128)(2,1)} %bitcast.164, bf16[4608,1152]{1,0:T(8,128)(2,1)} %all-gather.12.cloned.1.call-done), kind=kOutput, calls=%fused_computation.129 | convolution fusion | flops 5487717888 | bytes 25979904 | tf_op jit(solution)/shard_map/dot_general | solution.py:37
  323.4 11.1 %fusion.34 = (f32[512]{0:T(512)S(1)}, f32[512,1152]{1,0:T(8,128)S(1)}) fusion(f32[2,1152]{1,0:T(2,128)S(1)} %get-tuple-element.49, bf16[512,4608]{1,0:T(8,128)(2,1)S(1)} %get-tuple-element.37, bf16[1152,4608]{1,0:T(8,128)(2,1)} %all-gather.10.cloned.1.call-done), kind=kOutput, calls=%fused_computation.54 | convolution fusion | flops 5436997120 | bytes 17705984 | tf_op jit(solution)/shard_map/dot_general | solution.py:37
  345.1 4.7 reshape.275
  353.0 5.3 multiply_reduce_fusion
  358.4 4.6 multiply_convert_fusion.1
  376.5 7.1 copy.143
  383.6 5.0 copy.144
  396.8 5.6 constant_dynamic-update-slice_fusion.10
  408.3 174.8 %reduce_weights.1 = f32[36,72,384]{2,1,0:T(8,128)} custom-call(bf16[7,2,576,512]{3,2,1,0:T(8,128)(2,1)} %pad_maximum_fusion.at_ref, bf16[512,10368]{1,0:T(8,128)(2,1)} %constant_dynamic-update-slice_fusion.9.b_ref), custom_call_target="tpu_custom_call" | custom-call | tf_op jit(solution)/shard_map/reduce_weights/pallas_call | solution.py:241
  595.6 58.0 %all-reduce.9 = (bf16[1152]{0:T(1024)(128)(2,1)S(1)}, bf16[2304]{0:T(1024)(128)(2,1)}, bf16[1152]{0:T(1024)(128)(2,1)}, bf16[4608]{0:T(1024)(128)(2,1)}, bf16[1152]{0:T(1024)(128)(2,1)}) all-reduce(bf16[1152]{0:T(1024)(128)(2,1)S(1)} %dynamic-update-slice.3, ...), channel_id=1, replica_groups=mesh['narrow'=2,'wide'=16] {'wide'}, use_global_device_ids=true, to_apply=%add.3 | all-reduce | flops 10368 | bytes 41472
  653.6 13.0 %fusion.17 = f32[512,1152]{1,0:T(8,128)S(1)} fusion(bf16[4608,1152]{1,0:T(8,128)(2,1)} %all-gather.12.cloned.1.call-done, f32[512,4608]{1,0:T(8,128)} %get-tuple-element.70, f32[4608]{0:T(1024)S(1)} %convert_element_type.157, f32[1152]{0:T(1024)S(1)} %convert_element_type.159), kind=kOutput, calls=%fused_computation.32 | convolution fusion | flops 5460000768 | bytes 22436352 | tf_op jit(solution)/shard_map/dot_general | solution.py:33
  668.3 10.0 %fusion.33 = (f32[512]{0:T(512)}, f32[512,1152]{1,0:T(8,128)S(1)}) fusion(f32[2,1152]{1,0:T(2,128)S(1)} %copy-done.40, bf16[512,3456]{0,1:T(8,128)(2,1)} %constant_dynamic-update-slice_fusion, bf16[1152,3456]{1,0:T(8,128)(2,1)} %all-gather.6.cloned.1.call-done), kind=kOutput, calls=%fused_computation.51 | convolution fusion | flops 4078042624 | bytes 13872128 | tf_op jit(solution)/shard_map/dot_general | solution.py:37
  709.3 4.9 all-reduce.11
  717.0 73.8 %all-reduce.17.cloned.1.call-done = bf16[32,1152]{1,0:T(8,128)(2,1)} async-done(((bf16[32,1152]{1,0:T(8,128)(2,1)}), bf16[32,1152]{1,0:T(8,128)(2,1)}) %all-reduce.17.cloned.1.call-update) | async-done | bytes 73744
  792.1 41.3 %all-reduce.15.cloned.1.call-done = bf16[1152,432]{0,1:T(8,128)(2,1)} async-done(((bf16[1152,432]{0,1:T(8,128)(2,1)}), bf16[1152,432]{0,1:T(8,128)(2,1)}) %all-reduce.15.cloned.1.call-update) | async-done | bytes 995344 | tf_op jit(solution)/shard_map/psum | solution.py:544
  (274 shorter events, 144.1 us)
Async XLA Ops:
  7.2 28.2 %copy-start = (bf16[1152,432]{0,1:T(8,128)(2,1)S(1)}, bf16[1152,432]{0,1:T(8,128)(2,1)}, u32[]{:S(2)}) copy-start(bf16[1152,432]{0,1:T(8,128)(2,1)} %param.17) | copy-start | bytes 2985988
  7.2 33.4 %copy-start.55 = (u32[32]{0:T(128)S(1)}, u32[32]{0:T(128)}, u32[]{:S(2)}) copy-start(u32[32]{0:T(128)} %constant.56) | copy-start | bytes 388
  7.2 36.0 %copy-start.59 = (bf16[144]{0:T(256)(128)(2,1)S(1)}, bf16[144]{0:T(256)(128)(2,1)}, u32[]{:S(2)}) copy-start(bf16[144]{0:T(256)(128)(2,1)} %param.20) | copy-start | bytes 868
  7.2 36.2 %copy-start.60 = (bf16[72]{0:T(256)(128)(2,1)S(1)}, bf16[72]{0:T(256)(128)(2,1)}, u32[]{:S(2)}) copy-start(bf16[72]{0:T(256)(128)(2,1)} %param.22) | copy-start | bytes 436
  7.2 36.5 %copy-start.56 = (bf16[288]{0:T(512)(128)(2,1)S(1)}, bf16[288]{0:T(512)(128)(2,1)}, u32[]{:S(2)}) copy-start(bf16[288]{0:T(512)(128)(2,1)} %param.24) | copy-start | bytes 1732
  7.2 100.6 %copy-start.4 = (bf16[2,256,1152]{2,1,0:T(8,128)(2,1)S(1)}, bf16[2,256,1152]{2,1,0:T(8,128)(2,1)}, u32[]{:S(2)}) copy-start(bf16[2,256,1152]{2,1,0:T(8,128)(2,1)} %param.14) | copy-start | bytes 3538948
  7.2 110.3 %all-gather.6.cloned.1.call-start = ((), (), s32[]{:S(2)}) async-start(), calls=%async_computation.2 | async-start | bytes 8460288 | tf_op jit(solution)/shard_map/all_gather | solution.py:339
  8.0 154.1 %all-gather.8.cloned.1.call-start = ((), (), s32[]{:S(2)}) async-start(), calls=%async_computation.3 | async-start | bytes 2820096 | tf_op jit(solution)/shard_map/all_gather | solution.py:341
  8.7 210.3 %all-gather.10.cloned.1.call-start = ((), (), s32[]{:S(2)}) async-start(), calls=%async_computation.4 | async-start | bytes 11280384 | tf_op jit(solution)/shard_map/all_gather | solution.py:343
  9.5 101.8 %copy-start.61 = (bf16[72]{0:T(256)(128)(2,1)S(1)}, bf16[72]{0:T(256)(128)(2,1)}, u32[]{:S(2)}) copy-start(bf16[72]{0:T(256)(128)(2,1)} %param.26) | copy-start | bytes 436
  9.5 298.3 %all-gather.12.cloned.1.call-start = ((), (), s32[]{:S(2)}) async-start(), calls=%async_computation.5 | async-start | bytes 11280384 | tf_op jit(solution)/shard_map/all_gather | solution.py:345
  34.7 78.6 %copy-start.37 = (bf16[32,1152]{1,0:T(8,128)(2,1)}, bf16[32,1152]{1,0:T(8,128)(2,1)S(1)}, u32[]{:S(2)}) copy-start(bf16[32,1152]{1,0:T(8,128)(2,1)S(1)} %reshape.258) | copy-start | bytes 221188
  36.4 75.0 %all-to-all-start = ((bf16[16,2,432]{2,1,0:T(2,128)(2,1)}), bf16[16,2,432]{2,1,0:T(2,128)(2,1)S(1)}, u32[]{:S(2)}, u32[]{:S(2)}) async-start(bf16[16,2,432]{2,1,0:T(2,128)(2,1)} %all_to_all.22), calls=%async_computation | async-start | bytes 65536 | tf_op jit(solution)/shard_map/all_to_all | solution.py:323
  108.6 227.5 %copy-start.53 = (f32[2]{0:T(128)}, f32[2]{0:T(128)S(1)}, u32[]{:S(2)}) copy-start(f32[2]{0:T(128)S(1)} %compare_convert_fusion) | copy-start | bytes 28
  134.9 22.3 %copy-start.11 = (bf16[2,256,16,72]{1,3,2,0:T(8,128)(2,1)}, bf16[2,256,16,72]{1,3,2,0:T(8,128)(2,1)S(1)}, u32[]{:S(2)}) copy-start(bf16[2,256,16,72]{1,3,2,0:T(8,128)(2,1)S(1)} %copy.123) | copy-start | bytes 3538948
  167.6 168.5 %copy-start.2 = (f32[2,256,1152]{2,1,0:T(8,128)}, f32[2,256,1152]{2,1,0:T(8,128)S(1)}, u32[]{:S(2)}) copy-start(f32[2,256,1152]{2,1,0:T(8,128)S(1)} %get-tuple-element.41) | copy-start | bytes 7077892
  353.0 13.6 %slice-start = ((s8[8388608]{0:T(1024)(128)(4,1)}), s8[4194304]{0:T(1024)(128)(4,1)S(1)}, s32[]{:S(2)}) async-start(s8[8388608]{0:T(1024)(128)(4,1)} %bitcast.140), calls=%async_computation.8 | async-start | bytes 8388608
  375.0 14.9 %copy-start.16 = (bf16[144,8,2,256]{3,1,2,0:T(8,128)(2,1)}, bf16[144,8,2,256]{3,1,2,0:T(8,128)(2,1)S(1)}, u32[]{:S(2)}) copy-start(bf16[144,8,2,256]{3,1,2,0:T(8,128)(2,1)S(1)} %copy.171) | copy-start | bytes 3538948
  376.4 14.8 %copy-start.18 = (bf16[144,8,2,256]{3,1,2,0:T(8,128)(2,1)}, bf16[144,8,2,256]{3,1,2,0:T(8,128)(2,1)S(1)}, u32[]{:S(2)}) copy-start(bf16[144,8,2,256]{3,1,2,0:T(8,128)(2,1)S(1)} %copy.172) | copy-start | bytes 3538948
  653.5 13.0 %copy-start.54 = (f32[2]{0:T(128)S(1)}, f32[2]{0:T(128)}, u32[]{:S(2)}) copy-start(f32[2]{0:T(128)} %copy-done.53) | copy-start | bytes 28
  685.4 17.0 %all-to-all-start.1 = ((bf16[2,16,432]{2,0,1:T(2,128)(2,1)}), bf16[2,16,432]{2,0,1:T(2,128)(2,1)S(1)}, u32[]{:S(2)}, u32[]{:S(2)}) async-start(bf16[2,16,432]{2,0,1:T(2,128)(2,1)} %copy.139), calls=%async_computation.1 | async-start | bytes 65536 | tf_op jit(solution)/shard_map/all_to_all | solution.py:477
  688.9 101.9 %all-reduce.17.cloned.1.call-start = ((), (), s32[]{:S(2)}) async-start(), calls=%async_computation.7 | async-start | bytes 147456
  703.4 130.0 %all-reduce.15.cloned.1.call-start = ((), (), s32[]{:S(2)}) async-start(), calls=%async_computation.6 | async-start | bytes 1990656 | tf_op jit(solution)/shard_map/psum | solution.py:544
  705.0 85.8 %copy-start.45 = (f32[2,1152]{1,0:T(2,128)S(1)}, f32[2,1152]{1,0:T(2,128)}, u32[]{:S(2)}) copy-start(f32[2,1152]{1,0:T(2,128)} %param.15) | copy-start | bytes 27652
  (50 other events, 243.7 us)
Sparse Core Ops, SparseCore 0:
  10.2 75.2 all-gather.5
  87.7 41.8 all-gather.7
  131.8 87.1 all-gather.9
  221.1 86.5 all-gather.11
  703.5 87.1 all-reduce.16
  793.5 39.8 all-reduce.14

commit v2 on v1

--- a/solution.py
+++ b/solution.py
@@ -293,6 +293,186 @@
     return flat(0, 9), flat(9, 12), flat(12, 24), down
 
 
+def place(index, wide_count):
+    return (index // wide_count, index % wide_count)
+
+
+def meet(total, me, wide_count):
+    barrier = pltpu.get_barrier_semaphore()
+
+    def greet(step, carry):
+        pl.semaphore_signal(
+            barrier, inc=1, device_id=place((me + step) % total, wide_count), device_id_type=MESH
+        )
+        return carry
+
+    lax.fori_loop(1, total, greet, 0)
+    pl.semaphore_wait(barrier, total - 1)
+
+
+def exchange(step, source, landing, send_sems, recv_sems, peer):
+    return pltpu.make_async_remote_copy(
+        src_ref=source, dst_ref=landing, send_sem=send_sems.at[step], recv_sem=recv_sems.at[step],
+        device_id=peer, device_id_type=MESH,
+    )
+
+
+def loop(count, action):
+    def body(step, carry):
+        action(step)
+        return carry
+
+    lax.fori_loop(1, count, body, 0)
+
+
+def front_kernel(
+    narrow_count, wide_count, pack_ref, weight_ref, bias_ref, all_ref, mod_ref,
+    part, send_sem, recv_sem, send_two, recv_two,
+):
+    total = narrow_count * wide_count
+    narrow, wide = lax.axis_index("narrow"), lax.axis_index("wide")
+    me = narrow * wide_count + wide
+    base = narrow * wide_count
+    meet(total, me, wide_count)
+
+    def spread(step):
+        return exchange(
+            step, pack_ref, all_ref.at[me], send_sem, recv_sem, place((me + step) % total, wide_count)
+        )
+
+    loop(total, lambda step: spread(step).start())
+    all_ref[me] = pack_ref[...]
+    loop(total, lambda step: spread(step).wait())
+    rows = all_ref[pl.ds(base, wide_count)].astype(jnp.float32)
+    rows = rows.reshape(wide_count * 8, rows.shape[2]).astype(jnp.bfloat16)
+    product = jnp.dot(rows, weight_ref[...], preferred_element_type=jnp.float32)
+    product = product + bias_ref[...].astype(jnp.float32)
+    part[...] = product.reshape(part.shape).astype(jnp.bfloat16)
+
+    def deal(step):
+        to = (wide + step) % wide_count
+        return exchange(step, part.at[to], mod_ref.at[wide], send_two, recv_two, (narrow, to))
+
+    loop(wide_count, lambda step: deal(step).start())
+    mod_ref[wide] = part[wide]
+    loop(wide_count, lambda step: deal(step).wait())
+
+
+def tail_kernel(
+    narrow_count, wide_count, gift_ref, all_ref, weight_ref, ada_ref, misc_ref, cond_ref,
+    gifts, part, shares, send_sem, recv_sem, send_two, recv_two,
+):
+    total = narrow_count * wide_count
+    narrow, wide = lax.axis_index("narrow"), lax.axis_index("wide")
+    me = narrow * wide_count + wide
+    base = narrow * wide_count
+    meet(total, me, wide_count)
+
+    def spread(step):
+        to = (me + step) % total
+        return exchange(
+            step, gift_ref.at[to % wide_count], gifts.at[me], send_sem, recv_sem, place(to, wide_count)
+        )
+
+    loop(total, lambda step: spread(step).start())
+    gifts[me] = gift_ref[wide]
+    loop(total, lambda step: spread(step).wait())
+    mine = gifts[pl.ds(base, wide_count)].astype(jnp.float32)
+    mine = mine.reshape(wide_count * 8, mine.shape[2]).astype(jnp.bfloat16)
+    share = matmul_back(mine, weight_ref[...])
+    part[...] = share.reshape(part.shape).astype(jnp.bfloat16)
+
+    def deal(step):
+        to = (wide + step) % wide_count
+        return exchange(step, part.at[to], shares.at[wide], send_two, recv_two, (narrow, to))
+
+    loop(wide_count, lambda step: deal(step).start())
+    shares[wide] = part[wide]
+    every = gifts[...].astype(jnp.float32)
+    misc_ref[...] = jnp.sum(every, axis=0)
+    grads = every.reshape(total * 8, every.shape[2]).astype(jnp.bfloat16)
+    conds = all_ref[...].astype(jnp.float32)
+    conds = conds.reshape(total * 8, conds.shape[2]).astype(jnp.bfloat16)
+    ada_ref[...] = matmul_outer(conds, grads)
+    loop(wide_count, lambda step: deal(step).wait())
+    cond_ref[...] = jnp.sum(shares[...].astype(jnp.float32), axis=0)
+
+
+def in_vmem(count):
+    return [pl.BlockSpec(memory_space=pltpu.VMEM)] * count
+
+
+def dmas(*counts):
+    return [pltpu.SemaphoreType.DMA((count,)) for count in counts]
+
+
+def front(cond_act, biases, ada_weight, ada_bias):
+    narrow_count, wide_count = lax.axis_size("narrow"), lax.axis_size("wide")
+    total = narrow_count * wide_count
+    slots, model_width = cond_act.shape
+    columns = ada_weight.shape[1]
+    bias_row = jnp.concatenate(biases)
+    bias_row = jnp.pad(bias_row, (0, model_width - bias_row.shape[0]))[None]
+    pack = jnp.concatenate(
+        [cond_act, bias_row, jnp.zeros((7 - slots, model_width), jnp.bfloat16)]
+    )
+    return pl.pallas_call(
+        partial(front_kernel, narrow_count, wide_count),
+        out_shape=(
+            jax.ShapeDtypeStruct((total, 8, model_width), jnp.bfloat16),
+            jax.ShapeDtypeStruct((wide_count, 8, columns), jnp.bfloat16),
+        ),
+        in_specs=in_vmem(3),
+        out_specs=tuple(in_vmem(2)),
+        scratch_shapes=[pltpu.VMEM((wide_count, 8, columns), jnp.bfloat16)]
+        + dmas(total, total, wide_count, wide_count),
+        compiler_params=pltpu.CompilerParams(collective_id=2, has_side_effects=True),
+        name="front",
+    )(pack, ada_weight, ada_bias[None])
+
+
+def tail(grad_modulation, bias_grads, gathered, ada_weight):
+    narrow_count, wide_count = lax.axis_size("narrow"), lax.axis_size("wide")
+    total = narrow_count * wide_count
+    slots = grad_modulation.shape[0]
+    model_width, columns = ada_weight.shape
+    blocks = grad_modulation.reshape(slots, wide_count, columns).transpose(1, 0, 2)
+    held = jnp.concatenate(
+        [grad.reshape(wide_count, -1) for grad in bias_grads], axis=1
+    ).astype(jnp.bfloat16)
+    lines = -(-held.shape[1] // columns)
+    held_rows = jnp.pad(held, ((0, 0), (0, lines * columns - held.shape[1])))
+    held_rows = held_rows.reshape(wide_count, lines, columns)
+    gap = jnp.zeros((wide_count, 4 - slots, columns), jnp.bfloat16)
+    end = jnp.zeros((wide_count, 4 - lines, columns), jnp.bfloat16)
+    gift = jnp.concatenate([blocks, gap, held_rows, end], axis=1)
+    ada, misc, cond = pl.pallas_call(
+        partial(tail_kernel, narrow_count, wide_count),
+        out_shape=(
+            jax.ShapeDtypeStruct((model_width, columns), jnp.float32),
+            jax.ShapeDtypeStruct((8, columns), jnp.float32),
+            jax.ShapeDtypeStruct((8, model_width), jnp.float32),
+        ),
+        in_specs=in_vmem(3),
+        out_specs=tuple(in_vmem(3)),
+        scratch_shapes=[
+            pltpu.VMEM((total, 8, columns), jnp.bfloat16),
+            pltpu.VMEM((wide_count, 8, model_width), jnp.bfloat16),
+            pltpu.VMEM((wide_count, 8, model_width), jnp.bfloat16),
+        ]
+        + dmas(total, total, wide_count, wide_count),
+        compiler_params=pltpu.CompilerParams(collective_id=3, has_side_effects=True),
+        name="tail",
+    )(gift, gathered, ada_weight)
+    flat = misc[4:].reshape(-1)
+    grads, at = [], 0
+    for grad in bias_grads:
+        width = grad.shape[0] // wide_count
+        grads.append(flat[at : at + width])
+        at += width
+    return ada, misc[:slots].sum(axis=0), cond[:slots], grads
+
+
 def per_device(
     patches,
     condition,
@@ -316,13 +496,20 @@
     wide_count = lax.axis_size("wide")
     live = (jnp.arange(slots) < image_counts[0]).astype(jnp.float32)[:, None, None]
     cond_act = jax.nn.silu(condition).astype(jnp.bfloat16)
-    cond_all = lax.all_gather(cond_act, "wide", axis=0, tiled=True)
-    mod_part = (matmul_rows(cond_all, ada_weight) + ada_bias.astype(jnp.float32)).astype(
-        jnp.bfloat16
-    )
-    modulation = lax.all_to_all(mod_part, "wide", split_axis=0, concat_axis=1, tiled=True).astype(
-        jnp.float32
-    )
+    gathered, mod_blocks = front(
+        cond_act, (inproj_bias, outproj_bias, up_bias, down_bias), ada_weight, ada_bias
+    )
+    modulation = (
+        mod_blocks[:, :slots].transpose(1, 0, 2).reshape(slots, 6 * model_width).astype(jnp.float32)
+    )
+    group = lax.dynamic_slice_in_dim(
+        gathered[:, slots], lax.axis_index("narrow") * wide_count, wide_count
+    )
+    all_biases, bias_at = [], 0
+    for bias in (inproj_bias, outproj_bias, up_bias, down_bias):
+        all_biases.append(group[:, bias_at : bias_at + bias.shape[0]].reshape(-1))
+        bias_at += bias.shape[0]
+    b_inproj, b_outproj, b_up, b_down = all_biases
     segment_list = [
         modulation[:, None, number * model_width : (number + 1) * model_width]
         for number in range(6)
@@ -337,15 +524,11 @@
     ) = segment_list
     fetched = (
         lax.all_gather(inproj_weight, "wide", axis=0, tiled=True),
-        lax.all_gather(inproj_bias, "wide", axis=0, tiled=True),
         lax.all_gather(outproj_weight, "wide", axis=0, tiled=True),
-        lax.all_gather(outproj_bias, "wide", axis=0, tiled=True),
         lax.all_gather(up_weight, "wide", axis=0, tiled=True),
-        lax.all_gather(up_bias, "wide", axis=0, tiled=True),
         lax.all_gather(down_weight, "wide", axis=0, tiled=True),
-        lax.all_gather(down_bias, "wide", axis=0, tiled=True),
-    )
-    w_inproj, b_inproj, w_outproj, b_outproj, w_up, b_up, w_down, b_down = fetched
+    )
+    w_inproj, w_outproj, w_up, w_down = fetched
     input_rows = patches.astype(jnp.float32)
     normalized_first, inverse_deviation = normalize(input_rows)
     first_input = (
@@ -388,15 +571,11 @@
     output = ((between_state + perceptron_gate * mlp_out) * live).astype(jnp.bfloat16)
     back_weights = (
         lax.all_gather(inproj_weight, "wide", axis=0, tiled=True),
-        lax.all_gather(inproj_bias, "wide", axis=0, tiled=True),
         lax.all_gather(outproj_weight, "wide", axis=0, tiled=True),
-        lax.all_gather(outproj_bias, "wide", axis=0, tiled=True),
         lax.all_gather(up_weight, "wide", axis=0, tiled=True),
-        lax.all_gather(up_bias, "wide", axis=0, tiled=True),
         lax.all_gather(down_weight, "wide", axis=0, tiled=True),
-        lax.all_gather(down_bias, "wide", axis=0, tiled=True),
-    )
-    wb_inproj, _, wb_outproj, _, wb_up, _, wb_down, _ = back_weights
+    )
+    wb_inproj, wb_outproj, wb_up, wb_down = back_weights
     grad_out = cotangent.astype(jnp.float32) * live
     grad_gate_mlp = jnp.sum(grad_out * mlp_out, axis=1)
     grad_mlp = (grad_out * perceptron_gate).astype(jnp.bfloat16).reshape(row_total, model_width)
@@ -474,29 +653,14 @@
         ],
         axis=1,
     ).astype(jnp.bfloat16)
-    grad_mod_part = lax.all_to_all(grad_modulation, "wide", split_axis=1, concat_axis=0, tiled=True)
-    grad_ada_weight = matmul_outer(cond_all, grad_mod_part)
-    grad_ada_bias = jnp.sum(grad_mod_part.astype(jnp.float32), axis=0)
-    grad_cond_part = matmul_back(grad_mod_part, ada_weight)
-    grad_cond_act = lax.psum_scatter(
-        grad_cond_part.astype(jnp.bfloat16), "wide", scatter_dimension=0, tiled=True
-    ).astype(jnp.float32)
+    grad_ada_weight, grad_ada_bias, grad_cond_act, bias_shares = tail(
+        grad_modulation,
+        (grad_inproj_bias, grad_outproj_bias, grad_up_bias, grad_down_bias),
+        gathered,
+        ada_weight,
+    )
     _, silu_pull = jax.vjp(jax.nn.silu, condition)
     grad_condition = silu_pull(grad_cond_act)[0]
-    bias_shares = (
-        lax.psum_scatter(
-            grad_inproj_bias.astype(jnp.bfloat16), "wide", scatter_dimension=0, tiled=True
-        ).astype(jnp.float32),
-        lax.psum_scatter(
-            grad_outproj_bias.astype(jnp.bfloat16), "wide", scatter_dimension=0, tiled=True
-        ).astype(jnp.float32),
-        lax.psum_scatter(
-            grad_up_bias.astype(jnp.bfloat16), "wide", scatter_dimension=0, tiled=True
-        ).astype(jnp.float32),
-        lax.psum_scatter(
-            grad_down_bias.astype(jnp.bfloat16), "wide", scatter_dimension=0, tiled=True
-        ).astype(jnp.float32),
-    )
     ff_width = activated.shape[1]
     input_factors = (
         (first_input, grad_projected, 0),
@@ -540,24 +704,20 @@
                 jnp.concatenate(shards[4:], axis=1),
             )
         )
-    small = [
-        lax.psum(part.astype(jnp.bfloat16), "narrow").astype(jnp.float32)
-        for part in (grad_ada_weight, grad_ada_bias) + bias_shares
-    ]
     return (
         output,
         grad_patches,
         grad_condition,
-        small[0],
-        small[1],
+        grad_ada_weight,
+        grad_ada_bias,
         w_grads[0],
-        small[2],
+        bias_shares[0],
         w_grads[1],
-        small[3],
+        bias_shares[1],
         w_grads[2],
-        small[4],
+        bias_shares[2],
         w_grads[3],
-        small[5],
+        bias_shares[3],
     )
 
 

time: 853 us -> 687 us (0.81)
  blocking collectives: 151 us -> 0 us
  Pallas kernels: 175 us -> 236 us
  waiting for transfers between devices: 236 us -> 179 us
    unnamed x2 -> x0, blocking collectives: 122 us -> none
    unnamed x7 -> x4, waiting for transfers between devices: 76.4 us -> 2.58 us
    pallas_call x0 -> x2, Pallas kernels: none -> 61.5 us  [the longest x1 41.6 us: front(): pl.pallas_call(partial(front_kernel, narrow_count, wide_count), out_shape...]
    psum x1 -> x0, waiting for transfers between devices: 41.3 us -> none  [per_device(): lax.psum(part.astype(jnp.bfloat16), 'narrow').astype(jnp.float32)]
    all_gather x1, waiting for transfers between devices: 43.2 us -> 74.8 us  [per_device(): lax.all_gather(up_weight, 'wide', axis=0, tiled=True)]
    all_gather x1, waiting for transfers between devices: 0.01 us -> 27.2 us  [per_device(): lax.all_gather(inproj_weight, 'wide', axis=0, tiled=True)]
    all_gather x1 -> x0, blocking collectives: 23.9 us -> none  [per_device(): cond_all = lax.all_gather(cond_act, 'wide', axis=0, tiled=True)]
    unnamed x165 -> x176, local copies, waits for them, and re-layouts: 36.5 us -> 31.3 us
  transfers between devices with their start and end apart: 8 -> 4, of which waited for: 4 -> 3; matrix products, arithmetic and copies ran while one was open for 12% -> 13% of each run, Pallas kernels for 0% -> 6%
where the time goes in v2:
time: 687 us; the launch traced here: 677 us
  Pallas kernels  236 us (34%)
  waiting for transfers between devices  179 us (26%)
  local copies, waits for them, and re-layouts  113 us (16%)
  matrix products  94.7 us (14%)
  other arithmetic  37.8 us (6%)
  between operations  16 us (2%)
    pallas_call x1, Pallas kernels, reduce_weights(): pl.pallas_call(reduce_kernel, out_shape=jax.ShapeDtypeStruct((2 * n,) + u...  175 us
    all_gather x1, waiting for transfers between devices, per_device(): lax.all_gather(up_weight, 'wide', axis=0, tiled=True)  74.8 us
    all_gather x1, waiting for transfers between devices, per_device(): lax.all_gather(down_weight, 'wide', axis=0, tiled=True)  74.7 us
    pallas_call x1, Pallas kernels, front(): pl.pallas_call(partial(front_kernel, narrow_count, wide_count), out_shape...  41.6 us
    dot_general x4, matrix products, matmul_rows(): return jnp.dot(left, right, preferred_element_type=jnp.float32)  39.6 us
    dot_general x4, matrix products, matmul_back(): lax.dot_general(left, right, (((1,), (1,)), ((), ())), preferred_element_...  38.8 us
    unnamed x176, local copies, waits for them, and re-layouts  31.3 us
    all_gather x1, waiting for transfers between devices, per_device(): lax.all_gather(inproj_weight, 'wide', axis=0, tiled=True)  27.2 us
  transfers between devices with their start and end apart: 4, of which 3 were waited for; matrix products, arithmetic and copies ran while one was open for 13% of the time, Pallas kernels for 6%

profile of v2, /device:TPU:0, one launch (start us, length us, event | category | flops | bytes accessed | tf_op | source)
XLA Modules:
  0.0 676.7 jit_solution(2184371023489897469)
XLA Ops:
  13.2 41.6 %front.1 = (bf16[32,8,1152]{2,1,0:T(8,128)(2,1)}, bf16[16,8,432]{2,1,0:T(8,128)(2,1)}) custom-call(bf16[8,1152]{1,0:T(8,128)(2,1)} %maximum_maximum_fusion.pack_ref, bf16[1152,432]{1,0:T(8,128)(2,1)} %copy.48.weight_ref, bf16[1,432]{1,0:T(2,128)(2,1)} %broadcast_in_dim.12.bias_ref), custom_call_target="tpu_custom_call" | custom-call | tf_op jit(solution)/shard_map/front/pallas_call | solution.py:419
  70.1 27.2 %all-gather.5.cloned.1.call-done = bf16[1152,3456]{1,0:T(8,128)(2,1)} async-done(((bf16[72,3456]{1,0:T(8,128)(2,1)}), bf16[1152,3456]{1,0:T(8,128)(2,1)}) %all-gather.5.cloned.1.call-update) | async-done | bytes 7962640 | tf_op jit(solution)/shard_map/all_gather | solution.py:526
  97.3 8.3 %add_convert_fusion = bf16[512,3456]{1,0:T(8,128)(2,1)S(1)} fusion(bf16[512,1152]{1,0:T(8,128)(2,1)S(1)} %bitcast.164, bf16[1152,3456]{1,0:T(8,128)(2,1)} %all-gather.5.cloned.1.call-done, f32[3456]{0:T(1024)S(1)} %pad_maximum_fusion.2), kind=kOutput, calls=%fused_computation.25 | convolution fusion | flops 4080402432 | bytes 12695040 | tf_op jit(solution)/shard_map/dot_general | solution.py:33
  106.9 4.6 reshape.312
  114.6 6.0 reshape.313
  120.6 4.2 copy.55
  124.8 4.6 reshape.311
  142.2 4.0 convolution_add_fusion
  156.0 74.8 %all-gather.9.cloned.1.call-done = bf16[1152,4608]{1,0:T(8,128)(2,1)} async-done(((bf16[72,4608]{1,0:T(8,128)(2,1)}), bf16[1152,4608]{1,0:T(8,128)(2,1)}) %all-gather.9.cloned.1.call-update) | async-done | bytes 10616848 | tf_op jit(solution)/shard_map/all_gather | solution.py:528
  230.8 14.1 %fusion.14 = (bf16[4608,512]{0,1:T(8,128)(2,1)}, f32[512,4608]{1,0:T(8,128)}) fusion(f32[4608]{0:T(1024)} %reshape.309, bf16[512,1152]{1,0:T(8,128)(2,1)} %bitcast.166, bf16[1152,4608]{1,0:T(8,128)(2,1)} %all-gather.9.cloned.1.call-done), kind=kOutput, calls=%fused_computation.17 | convolution fusion | flops 5459410944 | bytes 25970688 | tf_op jit(solution)/shard_map/dot_general | solution.py:33
  244.9 74.7 %all-gather.11.cloned.1.call-done = bf16[4608,1152]{1,0:T(8,128)(2,1)} async-done(((bf16[288,1152]{1,0:T(8,128)(2,1)}), bf16[4608,1152]{1,0:T(8,128)(2,1)}) %all-gather.11.cloned.1.call-update) | async-done | bytes 10616848 | tf_op jit(solution)/shard_map/all_gather | solution.py:529
  319.5 16.0 %fusion.67 = (bf16[4608]{0:T(1024)(128)(2,1)}, bf16[512,4608]{1,0:T(8,128)(2,1)S(1)}) fusion(f32[512,4608]{1,0:T(8,128)} %get-tuple-element.95, f32[4608]{0:T(1024)} %reshape.309, bf16[512,1152]{1,0:T(8,128)(2,1)S(1)} %bitcast.155, bf16[4608,1152]{1,0:T(8,128)(2,1)} %all-gather.11.cloned.1.call-done), kind=kOutput, calls=%fused_computation.149 | convolution fusion | flops 5487717888 | bytes 25979904 | tf_op jit(solution)/shard_map/dot_general | solution.py:37
  335.5 11.0 %fusion.34 = (f32[512]{0:T(512)S(1)}, f32[512,1152]{1,0:T(8,128)S(1)}) fusion(f32[2,1152]{1,0:T(2,128)S(1)} %copy-done.45, bf16[512,4608]{1,0:T(8,128)(2,1)S(1)} %get-tuple-element.60, bf16[1152,4608]{1,0:T(8,128)(2,1)} %all-gather.9.cloned.1.call-done), kind=kOutput, calls=%fused_computation.53 | convolution fusion | flops 5436997120 | bytes 17705984 | tf_op jit(solution)/shard_map/dot_general | solution.py:37
  348.2 13.2 %fusion.17 = f32[512,1152]{1,0:T(8,128)S(1)} fusion(bf16[4608,1152]{1,0:T(8,128)(2,1)} %all-gather.11.cloned.1.call-done, f32[512,4608]{1,0:T(8,128)} %get-tuple-element.95, f32[4608]{0:T(1024)S(1)} %copy-done.59, f32[1152]{0:T(1024)S(1)} %copy-done.67), kind=kOutput, calls=%fused_computation.32 | convolution fusion | flops 5460000768 | bytes 22436352 | tf_op jit(solution)/shard_map/dot_general | solution.py:33
  369.0 4.6 reshape.314
  376.8 5.6 multiply_reduce_fusion
  382.5 4.9 multiply_convert_fusion.1
  409.4 5.0 constant_dynamic-update-slice_fusion.10
  415.6 6.7 copy.77
  425.7 3.8 pad_maximum_fusion.at_ref
  429.5 174.9 %reduce_weights.1 = f32[36,72,384]{2,1,0:T(8,128)} custom-call(bf16[7,2,576,512]{3,2,1,0:T(8,128)(2,1)} %pad_maximum_fusion.at_ref, bf16[512,10368]{1,0:T(8,128)(2,1)} %constant_dynamic-update-slice_fusion.9.b_ref), custom_call_target="tpu_custom_call" | custom-call | tf_op jit(solution)/shard_map/reduce_weights/pallas_call | solution.py:241
  616.2 10.0 %fusion.33 = (f32[512]{0:T(512)}, f32[512,1152]{1,0:T(8,128)S(1)}) fusion(f32[2,1152]{1,0:T(2,128)S(1)} %copy-done.44, bf16[512,3456]{0,1:T(8,128)(2,1)} %copy-done.23, bf16[1152,3456]{1,0:T(8,128)(2,1)} %all-gather.5.cloned.1.call-done), kind=kOutput, calls=%fused_computation.50 | convolution fusion | flops 4078042624 | bytes 13872128 | tf_op jit(solution)/shard_map/dot_general | solution.py:37
  629.6 19.8 %tail.1 = (f32[1152,432]{1,0:T(8,128)}, f32[8,432]{1,0:T(8,128)}, f32[8,1152]{1,0:T(8,128)}) custom-call(bf16[16,8,432]{2,1,0:T(8,128)(2,1)} %pad_maximum_fusion.1.gift_ref, bf16[32,8,1152]{2,1,0:T(8,128)(2,1)} %get-tuple-element.19.all_ref, bf16[1152,432]{1,0:T(8,128)(2,1)} %copy.48.weight_ref), custom_call_target="tpu_custom_call" | custom-call | tf_op jit(solution)/shard_map/tail/pallas_call | solution.py:449
  666.2 3.5 fusion.30
  (285 shorter events, 117.5 us)
Async XLA Ops:
  7.2 5.2 copy-start.52
  7.3 90.0 %all-gather.5.cloned.1.call-start = ((), (), s32[]{:S(2)}) async-start(), calls=%async_computation | async-start | bytes 8460288 | tf_op jit(solution)/shard_map/all_gather | solution.py:526
  8.0 134.2 %all-gather.7.cloned.1.call-start = ((), (), s32[]{:S(2)}) async-start(), calls=%async_computation.1 | async-start | bytes 2820096 | tf_op jit(solution)/shard_map/all_gather | solution.py:527
  8.7 222.1 %all-gather.9.cloned.1.call-start = ((), (), s32[]{:S(2)}) async-start(), calls=%async_computation.2 | async-start | bytes 11280384 | tf_op jit(solution)/shard_map/all_gather | solution.py:528
  9.5 310.1 %all-gather.11.cloned.1.call-start = ((), (), s32[]{:S(2)}) async-start(), calls=%async_computation.3 | async-start | bytes 11280384 | tf_op jit(solution)/shard_map/all_gather | solution.py:529
  10.0 50.2 %copy-start.1 = (bf16[2,256,1152]{2,1,0:T(8,128)(2,1)S(1)}, bf16[2,256,1152]{2,1,0:T(8,128)(2,1)}, u32[]{:S(2)}) copy-start(bf16[2,256,1152]{2,1,0:T(8,128)(2,1)} %param.14) | copy-start | bytes 3538948
  66.0 31.3 %copy-start.36 = (bf16[2,256,1152]{2,1,0:T(8,128)(2,1)S(1)}, bf16[2,256,1152]{2,1,0:T(8,128)(2,1)}, u32[]{:S(2)}) copy-start(bf16[2,256,1152]{2,1,0:T(8,128)(2,1)} %fusion.25) | copy-start | bytes 3538948
  114.6 18.1 %copy-start.12 = (bf16[2,256,16,72]{1,3,2,0:T(8,128)(2,1)}, bf16[2,256,16,72]{1,3,2,0:T(8,128)(2,1)S(1)}, u32[]{:S(2)}) copy-start(bf16[2,256,16,72]{1,3,2,0:T(8,128)(2,1)S(1)} %copy.54) | copy-start | bytes 3538948
  156.0 163.5 %copy-start.33 = (bf16[2,256,1152]{2,1,0:T(8,128)(2,1)S(1)}, bf16[2,256,1152]{2,1,0:T(8,128)(2,1)}, u32[]{:S(2)}) copy-start(bf16[2,256,1152]{2,1,0:T(8,128)(2,1)} %get-tuple-element.62) | copy-start | bytes 3538948
  335.5 11.0 %copy-start.32 = (bf16[512,4608]{1,0:T(8,128)(2,1)}, bf16[512,4608]{1,0:T(8,128)(2,1)S(1)}, u32[]{:S(2)}) copy-start(bf16[512,4608]{1,0:T(8,128)(2,1)S(1)} %get-tuple-element.60) | copy-start | bytes 14155780
  335.5 11.0 %copy-start.56 = (f32[2,256]{1,0:T(2,128)S(1)}, f32[2,256]{1,0:T(2,128)}, u32[]{:S(2)}) copy-start(f32[2,256]{1,0:T(2,128)} %copy-done.55) | copy-start | bytes 6148
  348.1 13.3 %copy-start.4 = (f32[512,1152]{1,0:T(8,128)S(1)}, f32[512,1152]{1,0:T(8,128)}, u32[]{:S(2)}) copy-start(f32[512,1152]{1,0:T(8,128)} %copy-done.3) | copy-start | bytes 7077892
  348.1 13.3 %copy-start.9 = (f32[512,1152]{1,0:T(8,128)S(1)}, f32[512,1152]{1,0:T(8,128)}, u32[]{:S(2)}) copy-start(f32[512,1152]{1,0:T(8,128)} %copy-done.8) | copy-start | bytes 7077892
  348.1 13.3 %copy-start.27 = (bf16[2,256,1152]{2,1,0:T(8,128)(2,1)S(1)}, bf16[2,256,1152]{2,1,0:T(8,128)(2,1)}, u32[]{:S(2)}) copy-start(bf16[2,256,1152]{2,1,0:T(8,128)(2,1)} %param.27) | copy-start | bytes 3538948
  348.1 13.3 %copy-start.47 = (f32[2,1152]{1,0:T(2,128)S(1)}, f32[2,1152]{1,0:T(2,128)}, u32[]{:S(2)}) copy-start(f32[2,1152]{1,0:T(2,128)} %get-tuple-element.72) | copy-start | bytes 27652
  348.1 13.3 %copy-start.69 = (f32[2]{0:T(128)S(1)}, f32[2]{0:T(128)}, u32[]{:S(2)}) copy-start(f32[2]{0:T(128)} %copy-done.68) | copy-start | bytes 28
  376.8 5.6 copy-start.42
  376.8 14.2 %slice-start = ((s8[8388608]{0:T(1024)(128)(4,1)}), s8[4194304]{0:T(1024)(128)(4,1)S(1)}, s32[]{:S(2)}) async-start(s8[8388608]{0:T(1024)(128)(4,1)} %bitcast.133), calls=%async_computation.4 | async-start | bytes 8388608
  382.4 8.6 %slice-start.1 = ((s8[8388608]{0:T(1024)(128)(4,1)}), s8[4194304]{0:T(1024)(128)(4,1)S(1)}, s32[]{:S(2)}) async-start(s8[8388608]{0:T(1024)(128)(4,1)} %bitcast.133), calls=%async_computation.5 | async-start | bytes 8388608
  616.2 10.0 %copy-start.2 = (bf16[2,256,1152]{2,1,0:T(8,128)(2,1)S(1)}, bf16[2,256,1152]{2,1,0:T(8,128)(2,1)}, u32[]{:S(2)}) copy-start(bf16[2,256,1152]{2,1,0:T(8,128)(2,1)} %param.14) | copy-start | bytes 3538948
  616.2 10.0 %copy-start.51 = (f32[2,256]{1,0:T(2,128)S(1)}, f32[2,256]{1,0:T(2,128)}, u32[]{:S(2)}) copy-start(f32[2,256]{1,0:T(2,128)} %copy-done.50) | copy-start | bytes 6148
  616.2 10.0 %copy-start.58 = (f32[2,256]{1,0:T(2,128)S(1)}, f32[2,256]{1,0:T(2,128)}, u32[]{:S(2)}) copy-start(f32[2,256]{1,0:T(2,128)} %copy-done.57) | copy-start | bytes 6148
  627.8 25.5 %copy-start.25 = (f32[12,72,384]{2,1,0:T(8,128)S(1)}, f32[12,72,384]{2,1,0:T(8,128)}, u32[]{:S(2)}) copy-start(f32[12,72,384]{2,1,0:T(8,128)} %get-tuple-element.65) | copy-start | bytes 3981316
  657.9 8.3 %copy-start.6 = (f32[2,256,1152]{2,1,0:T(8,128)S(1)}, f32[2,256,1152]{2,1,0:T(8,128)}, u32[]{:S(2)}) copy-start(f32[2,256,1152]{2,1,0:T(8,128)} %copy-done.5) | copy-start | bytes 7077892
  (57 other events, 152.2 us)
Sparse Core Ops, SparseCore 0:
  10.2 87.0 all-gather.4
  99.4 41.8 all-gather.6
  143.6 87.1 all-gather.8
  232.9 86.5 all-gather.10

commit v3 on v2

--- a/solution.py
+++ b/solution.py
@@ -325,10 +325,93 @@
     lax.fori_loop(1, count, body, 0)
 
 
-def front_kernel(
-    narrow_count, wide_count, pack_ref, weight_ref, bias_ref, all_ref, mod_ref,
-    part, send_sem, recv_sem, send_two, recv_two,
-):
+GATHER_CHUNKS = 6
+
+
+def gather_steps(shard_ref, full_ref, own_sem, zs_sem, zr_sem, one_sem, two_sem, core_sem):
+    narrow, wide = lax.axis_index("narrow"), lax.axis_index("wide")
+    core, row, deep = wide % 2, (wide // 2) % 2, wide // 4
+    core_peer = (narrow, wide + 1 - 2 * core)
+    x_peer = (1 - narrow, wide)
+    y_peer = (narrow, wide + 2 - 4 * row)
+
+    def span(chunk, half):
+        return pl.ds(pl.multiple_of((chunk + half * GATHER_CHUNKS) * LANES, LANES), LANES)
+
+    def send(view, sems, chunk, number, peer):
+        return pltpu.make_async_remote_copy(
+            src_ref=view, dst_ref=view, send_sem=sems.at[0, chunk, number],
+            recv_sem=sems.at[1, chunk, number], device_id=peer, device_id_type=MESH,
+        )
+
+    def own(chunk):
+        return pltpu.make_async_copy(
+            shard_ref.at[:, span(chunk, narrow)],
+            full_ref.at[deep, row, core, :, span(chunk, narrow)],
+            own_sem.at[chunk],
+        )
+
+    def along_z(chunk):
+        return [
+            pltpu.make_async_remote_copy(
+                src_ref=shard_ref.at[:, span(chunk, narrow)],
+                dst_ref=full_ref.at[deep, row, core, :, span(chunk, narrow)],
+                send_sem=zs_sem.at[chunk, o - 1], recv_sem=zr_sem.at[chunk, o - 1],
+                device_id=(narrow, (deep + o) % 4 * 4 + wide % 4), device_id_type=MESH,
+            )
+            for o in (1, 2, 3)
+        ]
+
+    def one(chunk):
+        view = full_ref.at[:, row, core, :, span(chunk, narrow)]
+        return [send(view, one_sem, chunk, 0, x_peer if chunk % 2 else y_peer)]
+
+    def two(chunk):
+        if chunk % 2:
+            return [
+                send(full_ref.at[:, row, core, :, span(chunk, half)], two_sem, chunk, half, y_peer)
+                for half in range(2)
+            ]
+        return [
+            send(full_ref.at[:, side, core, :, span(chunk, narrow)], two_sem, chunk, side, x_peer)
+            for side in range(2)
+        ]
+
+    def across(chunk):
+        return [
+            send(full_ref.at[:, :, core, :, span(chunk, half)], core_sem, chunk, half, core_peer)
+            for half in range(2)
+        ]
+
+    def begin():
+        for chunk in range(GATHER_CHUNKS):
+            own(chunk).start()
+            for copy in along_z(chunk):
+                copy.start()
+
+    def run():
+        stages = (lambda chunk: [own(chunk)] + along_z(chunk), one, two, across)
+        for turn in range(GATHER_CHUNKS + 3):
+            for stage in (3, 2, 1, 0):
+                chunk = turn - stage
+                if 0 <= chunk < GATHER_CHUNKS:
+                    for copy in stages[stage](chunk):
+                        copy.wait()
+                    if stage < 3:
+                        for copy in stages[stage + 1](chunk):
+                            copy.start()
+
+    return begin, run
+
+
+def front_kernel(narrow_count, wide_count, with_weights, *refs):
+    if with_weights:
+        pack_ref, weight_ref, bias_ref, shard_ref, all_ref, mod_ref, full_ref = refs[:7]
+        part, send_sem, recv_sem, send_two, recv_two = refs[7:12]
+        begin, run = gather_steps(shard_ref, full_ref, *refs[12:])
+    else:
+        pack_ref, weight_ref, bias_ref, all_ref, mod_ref = refs[:5]
+        part, send_sem, recv_sem, send_two, recv_two = refs[5:]
     total = narrow_count * wide_count
     narrow, wide = lax.axis_index("narrow"), lax.axis_index("wide")
     me = narrow * wide_count + wide
@@ -341,6 +424,8 @@
         )
 
     loop(total, lambda step: spread(step).start())
+    if with_weights:
+        begin()
     all_ref[me] = pack_ref[...]
     loop(total, lambda step: spread(step).wait())
     rows = all_ref[pl.ds(base, wide_count)].astype(jnp.float32)
@@ -355,6 +440,8 @@
 
     loop(wide_count, lambda step: deal(step).start())
     mod_ref[wide] = part[wide]
+    if with_weights:
+        run()
     loop(wide_count, lambda step: deal(step).wait())
 
 
@@ -406,7 +493,7 @@
     return [pltpu.SemaphoreType.DMA((count,)) for count in counts]
 
 
-def front(cond_act, biases, ada_weight, ada_bias):
+def front(cond_act, biases, ada_weight, ada_bias, shards):
     narrow_count, wide_count = lax.axis_size("narrow"), lax.axis_size("wide")
     total = narrow_count * wide_count
     slots, model_width = cond_act.shape
@@ -416,19 +503,37 @@
     pack = jnp.concatenate(
         [cond_act, bias_row, jnp.zeros((7 - slots, model_width), jnp.bfloat16)]
     )
-    return pl.pallas_call(
-        partial(front_kernel, narrow_count, wide_count),
-        out_shape=(
-            jax.ShapeDtypeStruct((total, 8, model_width), jnp.bfloat16),
-            jax.ShapeDtypeStruct((wide_count, 8, columns), jnp.bfloat16),
-        ),
-        in_specs=in_vmem(3),
-        out_specs=tuple(in_vmem(2)),
-        scratch_shapes=[pltpu.VMEM((wide_count, 8, columns), jnp.bfloat16)]
-        + dmas(total, total, wide_count, wide_count),
+    with_weights = narrow_count == 2 and wide_count == 16
+    operands = [pack, ada_weight, ada_bias[None]]
+    shapes = [
+        jax.ShapeDtypeStruct((total, 8, model_width), jnp.bfloat16),
+        jax.ShapeDtypeStruct((wide_count, 8, columns), jnp.bfloat16),
+    ]
+    out_specs = in_vmem(2)
+    scratch = [pltpu.VMEM((wide_count, 8, columns), jnp.bfloat16)]
+    scratch += dmas(total, total, wide_count, wide_count)
+    if with_weights:
+        shard = jnp.concatenate(shards, axis=1)
+        operands.append(shard)
+        shapes.append(jax.ShapeDtypeStruct((4, 2, 2) + shard.shape, jnp.bfloat16))
+        out_specs.append(pl.BlockSpec(memory_space=pl.ANY))
+        n = GATHER_CHUNKS
+        for dims in ((n,), (n, 3), (n, 3), (2, n, 1), (2, n, 2), (2, n, 2)):
+            scratch.append(pltpu.SemaphoreType.DMA(dims))
+    results = pl.pallas_call(
+        partial(front_kernel, narrow_count, wide_count, with_weights),
+        out_shape=tuple(shapes),
+        in_specs=in_vmem(len(operands)),
+        out_specs=tuple(out_specs),
+        scratch_shapes=scratch,
         compiler_params=pltpu.CompilerParams(collective_id=2, has_side_effects=True),
         name="front",
-    )(pack, ada_weight, ada_bias[None])
+    )(*operands)
+    if not with_weights:
+        return results + tuple(lax.all_gather(shard, "wide", axis=0, tiled=True) for shard in shards)
+    full = results[2].reshape(wide_count * shard.shape[0], shard.shape[1])
+    cut = shards[0].shape[1]
+    return results[0], results[1], full[:, :cut], full[:, cut:]
 
 
 def tail(grad_modulation, bias_grads, gathered, ada_weight):
@@ -496,8 +601,9 @@
     wide_count = lax.axis_size("wide")
     live = (jnp.arange(slots) < image_counts[0]).astype(jnp.float32)[:, None, None]
     cond_act = jax.nn.silu(condition).astype(jnp.bfloat16)
-    gathered, mod_blocks = front(
-        cond_act, (inproj_bias, outproj_bias, up_bias, down_bias), ada_weight, ada_bias
+    gathered, mod_blocks, w_inproj, w_outproj = front(
+        cond_act, (inproj_bias, outproj_bias, up_bias, down_bias), ada_weight, ada_bias,
+        (inproj_weight, outproj_weight),
     )
     modulation = (
         mod_blocks[:, :slots].transpose(1, 0, 2).reshape(slots, 6 * model_width).astype(jnp.float32)
@@ -522,13 +628,8 @@
         perceptron_scale,
         perceptron_gate,
     ) = segment_list
-    fetched = (
-        lax.all_gather(inproj_weight, "wide", axis=0, tiled=True),
-        lax.all_gather(outproj_weight, "wide", axis=0, tiled=True),
-        lax.all_gather(up_weight, "wide", axis=0, tiled=True),
-        lax.all_gather(down_weight, "wide", axis=0, tiled=True),
-    )
-    w_inproj, w_outproj, w_up, w_down = fetched
+    w_up = lax.all_gather(up_weight, "wide", axis=0, tiled=True)
+    w_down = lax.all_gather(down_weight, "wide", axis=0, tiled=True)
     input_rows = patches.astype(jnp.float32)
     normalized_first, inverse_deviation = normalize(input_rows)
     first_input = (
@@ -569,13 +670,7 @@
         slots, seq_len, model_width
     )
     output = ((between_state + perceptron_gate * mlp_out) * live).astype(jnp.bfloat16)
-    back_weights = (
-        lax.all_gather(inproj_weight, "wide", axis=0, tiled=True),
-        lax.all_gather(outproj_weight, "wide", axis=0, tiled=True),
-        lax.all_gather(up_weight, "wide", axis=0, tiled=True),
-        lax.all_gather(down_weight, "wide", axis=0, tiled=True),
-    )
-    wb_inproj, wb_outproj, wb_up, wb_down = back_weights
+    wb_inproj, wb_outproj, wb_up, wb_down = w_inproj, w_outproj, w_up, w_down
     grad_out = cotangent.astype(jnp.float32) * live
     grad_gate_mlp = jnp.sum(grad_out * mlp_out, axis=1)
     grad_mlp = (grad_out * perceptron_gate).astype(jnp.bfloat16).reshape(row_total, model_width)

time: 687 us -> 641 us (0.933)
  waiting for transfers between devices: 179 us -> 1.38 us
  Pallas kernels: 236 us -> 363 us
    all_gather x4 -> x2, waiting for transfers between devices: 177 us -> 0.01 us  [the longest x1 0.01 us: per_device(): w_up = lax.all_gather(up_weight, 'wide', axis=0, tiled=True)]
    pallas_call x1, Pallas kernels: 41.6 us -> 161 us  [front(): pl.pallas_call(partial(front_kernel, narrow_count, wide_count, with_weigh...]
    pallas_call x1, Pallas kernels: 175 us -> 182 us  [reduce_weights(): pl.pallas_call(reduce_kernel, out_shape=jax.ShapeDtypeStruct((2 * n,) + u...]
    unnamed x176 -> x168, local copies, waits for them, and re-layouts: 31.3 us -> 32.3 us
  transfers between devices with their start and end apart: 4 -> 2, of which waited for: 3 -> 0; matrix products, arithmetic and copies ran while one was open for 13% -> 13% of each run, Pallas kernels for 6% -> 25%
where the time goes in v3:
time: 641 us; the launch traced here: 631 us
  Pallas kernels  363 us (57%)
  local copies, waits for them, and re-layouts  115 us (18%)
  matrix products  94.7 us (15%)
  other arithmetic  40.1 us (6%)
  between operations  16.2 us (3%)
    pallas_call x1, Pallas kernels, reduce_weights(): pl.pallas_call(reduce_kernel, out_shape=jax.ShapeDtypeStruct((2 * n,) + u...  182 us
    pallas_call x1, Pallas kernels, front(): pl.pallas_call(partial(front_kernel, narrow_count, wide_count, with_weigh...  161 us
    dot_general x4, matrix products, matmul_back(): lax.dot_general(left, right, (((1,), (1,)), ((), ())), preferred_element_...  39.4 us
    dot_general x4, matrix products, matmul_rows(): return jnp.dot(left, right, preferred_element_type=jnp.float32)  39.2 us
    unnamed x168, local copies, waits for them, and re-layouts  32.3 us
    pallas_call x1, Pallas kernels, tail(): pl.pallas_call(partial(tail_kernel, narrow_count, wide_count), out_shape=...  20.3 us
  transfers between devices with their start and end apart: 2, of which 0 were waited for; matrix products, arithmetic and copies ran while one was open for 13% of the time, Pallas kernels for 25%

profile of v3, /device:TPU:0, one launch (start us, length us, event | category | flops | bytes accessed | tf_op | source)
XLA Modules:
  0.0 630.7 jit_solution(1490817179132488527)
XLA Ops:
  13.5 160.6 %front.1 = (bf16[32,8,1152]{2,1,0:T(8,128)(2,1)}, bf16[16,8,432]{2,1,0:T(8,128)(2,1)}, bf16[4,2,2,72,4608]{4,3,2,1,0:T(8,128)(2,1)}) custom-call(bf16[8,1152]{1,0:T(8,128)(2,1)} %maximum_maximum_fusion.refs_0_, bf16[1152,432]{1,0:T(8,128)(2,1)} %copy.48.refs_1_.weight_ref, bf16[1,432]{1,0:T(2,128)(2,1)} %broadcast_in_dim.12.refs_2_, ...), custom_call_target="tpu_custom_call" | custom-call | tf_op jit(solution)/shard_map/front/pallas_call | solution.py:523
  180.7 8.4 %add_convert_fusion = bf16[512,3456]{1,0:T(8,128)(2,1)S(1)} fusion(bf16[512,1152]{1,0:T(8,128)(2,1)S(1)} %bitcast.161, bf16[1152,4608]{1,0:T(8,128)(2,1)} %bitcast.167, f32[3456]{0:T(1024)S(1)} %pad_maximum_fusion.3), kind=kOutput, calls=%fused_computation.25 | convolution fusion | flops 4080402432 | bytes 12695040 | tf_op jit(solution)/shard_map/dot_general | solution.py:33
  190.3 4.6 reshape.316
  198.0 6.0 reshape.317
  204.0 4.1 copy.55
  208.2 4.6 reshape.315
  227.8 3.6 convolution_add_fusion
  244.8 14.0 %fusion.14 = (bf16[4608,512]{0,1:T(8,128)(2,1)}, f32[512,4608]{1,0:T(8,128)}) fusion(f32[4608]{0:T(1024)} %reshape.313, bf16[512,1152]{1,0:T(8,128)(2,1)} %bitcast.163, bf16[1152,4608]{1,0:T(8,128)(2,1)} %all-gather.3.cloned.1.call-done), kind=kOutput, calls=%fused_computation.17 | convolution fusion | flops 5459410944 | bytes 25970688 | tf_op jit(solution)/shard_map/dot_general | solution.py:33
  258.8 16.0 %fusion.75 = (bf16[4608]{0:T(1024)(128)(2,1)}, bf16[512,4608]{1,0:T(8,128)(2,1)S(1)}) fusion(f32[512,4608]{1,0:T(8,128)} %get-tuple-element.97, f32[4608]{0:T(1024)} %reshape.313, bf16[512,1152]{1,0:T(8,128)(2,1)S(1)} %bitcast.152, bf16[4608,1152]{1,0:T(8,128)(2,1)} %all-gather.5.cloned.1.call-done), kind=kOutput, calls=%fused_computation.156 | convolution fusion | flops 5487717888 | bytes 25979904 | tf_op jit(solution)/shard_map/dot_general | solution.py:37
  274.8 11.0 %fusion.40 = (f32[512]{0:T(512)S(1)}, f32[512,1152]{1,0:T(8,128)S(1)}) fusion(f32[2,1152]{1,0:T(2,128)S(1)} %get-tuple-element.76, bf16[512,4608]{1,0:T(8,128)(2,1)S(1)} %get-tuple-element.62, bf16[1152,4608]{1,0:T(8,128)(2,1)} %all-gather.3.cloned.1.call-done), kind=kOutput, calls=%fused_computation.57 | convolution fusion | flops 5436997120 | bytes 17705984 | tf_op jit(solution)/shard_map/dot_general | solution.py:37
  287.5 13.2 %fusion.23 = f32[512,1152]{1,0:T(8,128)S(1)} fusion(bf16[4608,1152]{1,0:T(8,128)(2,1)} %all-gather.5.cloned.1.call-done, f32[512,4608]{1,0:T(8,128)} %get-tuple-element.97, f32[4608]{0:T(1024)S(1)} %copy-done.58, f32[1152]{0:T(1024)S(1)} %copy-done.63), kind=kOutput, calls=%fused_computation.36 | convolution fusion | flops 5460000768 | bytes 22436352 | tf_op jit(solution)/shard_map/dot_general | solution.py:33
  306.1 3.6 convolution_convert_fusion
  309.8 4.7 reshape.318
  317.6 5.5 multiply_reduce_fusion
  323.1 4.9 multiply_convert_fusion.1
  350.1 4.9 constant_dynamic-update-slice_fusion.10
  356.2 6.7 %copy.77 = bf16[4608,512]{1,0:T(8,128)(2,1)} copy(bf16[4608,512]{0,1:T(8,128)(2,1)} %get-tuple-element.96) | data formatting | bytes 9437184 | tf_op jit(solution)/shard_map/convert_element_type | solution.py:668
  366.3 3.7 pad_maximum_fusion.at_ref
  370.0 182.4 %reduce_weights.1 = f32[36,72,384]{2,1,0:T(8,128)} custom-call(bf16[7,2,576,512]{3,2,1,0:T(8,128)(2,1)} %pad_maximum_fusion.at_ref, bf16[512,10368]{1,0:T(8,128)(2,1)} %constant_dynamic-update-slice_fusion.9.b_ref), custom_call_target="tpu_custom_call" | custom-call | tf_op jit(solution)/shard_map/reduce_weights/pallas_call | solution.py:241
  552.5 3.4 fusion.79
  563.2 8.9 %fusion.39 = (f32[512]{0:T(512)}, f32[512,1152]{1,0:T(8,128)S(1)}) fusion(f32[2,1152]{1,0:T(2,128)S(1)} %copy-done.44, bf16[512,3456]{0,1:T(8,128)(2,1)S(1)} %constant_dynamic-update-slice_fusion, bf16[1152,4608]{1,0:T(8,128)(2,1)} %bitcast.170), kind=kOutput, calls=%fused_computation.54 | convolution fusion | flops 4078042624 | bytes 13872128 | tf_op jit(solution)/shard_map/dot_general | solution.py:37
  572.1 4.0 reduce.4
  582.9 20.3 %tail.1 = (f32[1152,432]{1,0:T(8,128)}, f32[8,432]{1,0:T(8,128)}, f32[8,1152]{1,0:T(8,128)}) custom-call(bf16[16,8,432]{2,1,0:T(8,128)(2,1)} %pad_maximum_fusion.2.gift_ref, bf16[32,8,1152]{2,1,0:T(8,128)(2,1)} %get-tuple-element.21.all_ref, bf16[1152,432]{1,0:T(8,128)(2,1)} %copy.48.refs_1_.weight_ref), custom_call_target="tpu_custom_call" | custom-call | tf_op jit(solution)/shard_map/tail/pallas_call | solution.py:554
  619.9 3.5 fusion.36
  (272 shorter events, 111.8 us)
Async XLA Ops:
  7.2 5.4 copy-start.41
  7.3 5.4 copy-start.42
  7.3 237.5 %all-gather.3.cloned.1.call-start = ((), (), s32[]{:S(2)}) async-start(), calls=%async_computation | async-start | bytes 11280384 | tf_op jit(solution)/shard_map/all_gather | solution.py:631
  8.0 250.8 %all-gather.5.cloned.1.call-start = ((), (), s32[]{:S(2)}) async-start(), calls=%async_computation.1 | async-start | bytes 11280384 | tf_op jit(solution)/shard_map/all_gather | solution.py:632
  11.2 165.6 %copy-start.1 = (bf16[2,256,1152]{2,1,0:T(8,128)(2,1)S(1)}, bf16[2,256,1152]{2,1,0:T(8,128)(2,1)}, u32[]{:S(2)}) copy-start(bf16[2,256,1152]{2,1,0:T(8,128)(2,1)} %param.14) | copy-start | bytes 3538948
  198.0 18.0 %copy-start.12 = (bf16[2,256,16,72]{1,3,2,0:T(8,128)(2,1)}, bf16[2,256,16,72]{1,3,2,0:T(8,128)(2,1)S(1)}, u32[]{:S(2)}) copy-start(bf16[2,256,16,72]{1,3,2,0:T(8,128)(2,1)S(1)} %copy.54) | copy-start | bytes 3538948
  225.5 6.0 copy-start.21
  235.0 5.1 copy-start.22
  243.4 15.4 %copy-start.33 = (bf16[2,256,1152]{2,1,0:T(8,128)(2,1)}, bf16[2,256,1152]{2,1,0:T(8,128)(2,1)S(1)}, u32[]{:S(2)}) copy-start(bf16[2,256,1152]{2,1,0:T(8,128)(2,1)S(1)} %get-tuple-element.64) | copy-start | bytes 3538948
  274.8 11.0 %copy-start.32 = (bf16[512,4608]{1,0:T(8,128)(2,1)}, bf16[512,4608]{1,0:T(8,128)(2,1)S(1)}, u32[]{:S(2)}) copy-start(bf16[512,4608]{1,0:T(8,128)(2,1)S(1)} %get-tuple-element.62) | copy-start | bytes 14155780
  274.8 11.0 %copy-start.56 = (f32[2,256]{1,0:T(2,128)S(1)}, f32[2,256]{1,0:T(2,128)}, u32[]{:S(2)}) copy-start(f32[2,256]{1,0:T(2,128)} %copy-done.55) | copy-start | bytes 6148
  287.4 13.2 %copy-start.4 = (f32[512,1152]{1,0:T(8,128)S(1)}, f32[512,1152]{1,0:T(8,128)}, u32[]{:S(2)}) copy-start(f32[512,1152]{1,0:T(8,128)} %copy-done.3) | copy-start | bytes 7077892
  287.4 13.2 %copy-start.9 = (f32[512,1152]{1,0:T(8,128)S(1)}, f32[512,1152]{1,0:T(8,128)}, u32[]{:S(2)}) copy-start(f32[512,1152]{1,0:T(8,128)} %copy-done.8) | copy-start | bytes 7077892
  287.4 13.2 %copy-start.27 = (bf16[2,256,1152]{2,1,0:T(8,128)(2,1)S(1)}, bf16[2,256,1152]{2,1,0:T(8,128)(2,1)}, u32[]{:S(2)}) copy-start(bf16[2,256,1152]{2,1,0:T(8,128)(2,1)} %param.27) | copy-start | bytes 3538948
  287.4 13.2 %copy-start.48 = (f32[2,1152]{1,0:T(2,128)S(1)}, f32[2,1152]{1,0:T(2,128)}, u32[]{:S(2)}) copy-start(f32[2,1152]{1,0:T(2,128)} %get-tuple-element.74) | copy-start | bytes 27652
  287.5 13.2 %copy-start.65 = (f32[2]{0:T(128)S(1)}, f32[2]{0:T(128)}, u32[]{:S(2)}) copy-start(f32[2]{0:T(128)} %copy-done.64) | copy-start | bytes 28
  317.5 5.6 copy-start.40
  317.6 14.1 %slice-start = ((s8[8388608]{0:T(1024)(128)(4,1)}), s8[4194304]{0:T(1024)(128)(4,1)S(1)}, s32[]{:S(2)}) async-start(s8[8388608]{0:T(1024)(128)(4,1)} %bitcast.130), calls=%async_computation.2 | async-start | bytes 8388608
  323.1 4.9 copy-start.14
  323.1 8.6 %slice-start.1 = ((s8[8388608]{0:T(1024)(128)(4,1)}), s8[4194304]{0:T(1024)(128)(4,1)S(1)}, s32[]{:S(2)}) async-start(s8[8388608]{0:T(1024)(128)(4,1)} %bitcast.130), calls=%async_computation.3 | async-start | bytes 8388608
  350.1 4.9 copy-start.34
  572.1 6.2 copy-start.7
  578.3 28.8 %copy-start.25 = (f32[12,72,384]{2,1,0:T(8,128)S(1)}, f32[12,72,384]{2,1,0:T(8,128)}, u32[]{:S(2)}) copy-start(f32[12,72,384]{2,1,0:T(8,128)} %get-tuple-element.67) | copy-start | bytes 3981316
  611.6 8.3 %copy-start.6 = (f32[2,256,1152]{2,1,0:T(8,128)S(1)}, f32[2,256,1152]{2,1,0:T(8,128)}, u32[]{:S(2)}) copy-start(f32[2,256,1152]{2,1,0:T(8,128)} %copy-done.5) | copy-start | bytes 7077892
  (51 other events, 138.7 us)
Sparse Core Ops, SparseCore 0:
  10.4 137.1 all-gather.2
  149.8 92.3 all-gather.4

commit v4 on v3

--- a/solution.py
+++ b/solution.py
@@ -325,18 +325,16 @@
     lax.fori_loop(1, count, body, 0)
 
 
-GATHER_CHUNKS = 6
-
-
 def gather_steps(shard_ref, full_ref, own_sem, zs_sem, zr_sem, one_sem, two_sem, core_sem):
     narrow, wide = lax.axis_index("narrow"), lax.axis_index("wide")
     core, row, deep = wide % 2, (wide // 2) % 2, wide // 4
     core_peer = (narrow, wide + 1 - 2 * core)
     x_peer = (1 - narrow, wide)
     y_peer = (narrow, wide + 2 - 4 * row)
+    chunks = shard_ref.shape[1] // (2 * LANES)
 
     def span(chunk, half):
-        return pl.ds(pl.multiple_of((chunk + half * GATHER_CHUNKS) * LANES, LANES), LANES)
+        return pl.ds(pl.multiple_of((chunk + half * chunks) * LANES, LANES), LANES)
 
     def send(view, sems, chunk, number, peer):
         return pltpu.make_async_remote_copy(
@@ -384,17 +382,17 @@
         ]
 
     def begin():
-        for chunk in range(GATHER_CHUNKS):
+        for chunk in range(chunks):
             own(chunk).start()
             for copy in along_z(chunk):
                 copy.start()
 
     def run():
         stages = (lambda chunk: [own(chunk)] + along_z(chunk), one, two, across)
-        for turn in range(GATHER_CHUNKS + 3):
+        for turn in range(chunks + 3):
             for stage in (3, 2, 1, 0):
                 chunk = turn - stage
-                if 0 <= chunk < GATHER_CHUNKS:
+                if 0 <= chunk < chunks:
                     for copy in stages[stage](chunk):
                         copy.wait()
                     if stage < 3:
@@ -517,7 +515,7 @@
         operands.append(shard)
         shapes.append(jax.ShapeDtypeStruct((4, 2, 2) + shard.shape, jnp.bfloat16))
         out_specs.append(pl.BlockSpec(memory_space=pl.ANY))
-        n = GATHER_CHUNKS
+        n = shard.shape[1] // (2 * LANES)
         for dims in ((n,), (n, 3), (n, 3), (2, n, 1), (2, n, 2), (2, n, 2)):
             scratch.append(pltpu.SemaphoreType.DMA(dims))
     results = pl.pallas_call(
@@ -530,10 +528,13 @@
         name="front",
     )(*operands)
     if not with_weights:
-        return results + tuple(lax.all_gather(shard, "wide", axis=0, tiled=True) for shard in shards)
+        return tuple(results) + tuple(lax.all_gather(shard, "wide", axis=0, tiled=True) for shard in shards)
     full = results[2].reshape(wide_count * shard.shape[0], shard.shape[1])
-    cut = shards[0].shape[1]
-    return results[0], results[1], full[:, :cut], full[:, cut:]
+    weights, at = [], 0
+    for piece in shards:
+        weights.append(full[:, at : at + piece.shape[1]])
+        at += piece.shape[1]
+    return tuple(results[:2]) + tuple(weights)
 
 
 def tail(grad_modulation, bias_grads, gathered, ada_weight):
@@ -601,10 +602,11 @@
     wide_count = lax.axis_size("wide")
     live = (jnp.arange(slots) < image_counts[0]).astype(jnp.float32)[:, None, None]
     cond_act = jax.nn.silu(condition).astype(jnp.bfloat16)
-    gathered, mod_blocks, w_inproj, w_outproj = front(
+    gathered, mod_blocks, w_inproj, w_outproj, w_up = front(
         cond_act, (inproj_bias, outproj_bias, up_bias, down_bias), ada_weight, ada_bias,
-        (inproj_weight, outproj_weight),
-    )
+        (inproj_weight, outproj_weight, up_weight),
+    )
+    down_weight, mod_blocks = lax.optimization_barrier((down_weight, mod_blocks))
     modulation = (
         mod_blocks[:, :slots].transpose(1, 0, 2).reshape(slots, 6 * model_width).astype(jnp.float32)
     )
@@ -628,7 +630,6 @@
         perceptron_scale,
         perceptron_gate,
     ) = segment_list
-    w_up = lax.all_gather(up_weight, "wide", axis=0, tiled=True)
     w_down = lax.all_gather(down_weight, "wide", axis=0, tiled=True)
     input_rows = patches.astype(jnp.float32)
     normalized_first, inverse_deviation = normalize(input_rows)
@@ -666,6 +667,7 @@
     hidden = matmul_rows(second_in, w_up) + b_up.astype(jnp.float32)
     gelu_value, gelu_pull = jax.vjp(partial(jax.nn.gelu, approximate=True), hidden)
     activated = gelu_value.astype(jnp.bfloat16)
+    w_down, activated = lax.optimization_barrier((w_down, activated))
     mlp_out = (matmul_rows(activated, w_down) + b_down.astype(jnp.float32)).reshape(
         slots, seq_len, model_width
     )

time: 641 us -> 681 us (1.062)
  Pallas kernels: 363 us -> 396 us
  local copies, waits for them, and re-layouts: 115 us -> 122 us
    pallas_call x1, Pallas kernels: 161 us -> 196 us  [front(): pl.pallas_call(partial(front_kernel, narrow_count, wide_count, with_weigh...]
    unnamed x168 -> x156, local copies, waits for them, and re-layouts: 32.3 us -> 34.9 us
  transfers between devices with their start and end apart: 2 -> 1, of which waited for: 0 -> 1; matrix products, arithmetic and copies ran while one was open for 13% -> 13% of each run, Pallas kernels for 25% -> 0%
where the time goes in v4:
time: 681 us; the launch traced here: 671 us
  Pallas kernels  396 us (58%)
  local copies, waits for them, and re-layouts  122 us (18%)
  matrix products  89.7 us (13%)
  other arithmetic  43.6 us (6%)
  between operations  16 us (2%)
    pallas_call x1, Pallas kernels, front(): pl.pallas_call(partial(front_kernel, narrow_count, wide_count, with_weigh...  196 us
    pallas_call x1, Pallas kernels, reduce_weights(): pl.pallas_call(reduce_kernel, out_shape=jax.ShapeDtypeStruct((2 * n,) + u...  177 us
    dot_general x4, matrix products, matmul_back(): lax.dot_general(left, right, (((1,), (1,)), ((), ())), preferred_element_...  40 us
    dot_general x4, matrix products, matmul_rows(): return jnp.dot(left, right, preferred_element_type=jnp.float32)  36.1 us
    unnamed x156, local copies, waits for them, and re-layouts  34.9 us
    pallas_call x1, Pallas kernels, tail(): pl.pallas_call(partial(tail_kernel, narrow_count, wide_count), out_shape=...  23.1 us
  transfers between devices with their start and end apart: 1, of which 1 were waited for; matrix products, arithmetic and copies ran while one was open for 13% of the time, Pallas kernels for 0%

profile of v4, /device:TPU:0, one launch (start us, length us, event | category | flops | bytes accessed | tf_op | source)
XLA Modules:
  0.0 670.9 jit_solution(9269871140994694838)
XLA Ops:
  15.3 195.7 %front.1 = (bf16[32,8,1152]{2,1,0:T(8,128)(2,1)}, bf16[16,8,432]{2,1,0:T(8,128)(2,1)}, bf16[4,2,2,72,9216]{4,3,2,1,0:T(8,128)(2,1)}) custom-call(bf16[8,1152]{1,0:T(8,128)(2,1)} %maximum_maximum_fusion.refs_0_, bf16[1152,432]{1,0:T(8,128)(2,1)} %copy.48.refs_1_.weight_ref, bf16[1,432]{1,0:T(2,128)(2,1)} %broadcast_in_dim.12.refs_2_, ...), custom_call_target="tpu_custom_call" | custom-call | tf_op jit(solution)/shard_map/front/pallas_call | solution.py:521
  217.1 8.3 %add_convert_fusion = bf16[512,3456]{1,0:T(8,128)(2,1)S(1)} fusion(bf16[512,1152]{1,0:T(8,128)(2,1)S(1)} %bitcast.162, bf16[1152,9216]{1,0:T(8,128)(2,1)} %bitcast.169, f32[3456]{0:T(1024)S(1)} %pad_maximum_fusion.3), kind=kOutput, calls=%fused_computation.20 | convolution fusion | flops 4080402432 | bytes 12695040 | tf_op jit(solution)/shard_map/dot_general | solution.py:33
  226.8 4.7 reshape.315
  234.4 4.7 reshape.316
  242.1 6.0 reshape.317
  248.2 4.3 copy.55
  271.3 3.7 convolution_add_fusion.1
  285.9 13.8 %multiply_convert_fusion = (bf16[512,4608]{1,0:T(8,128)(2,1)}, f32[512,4608]{1,0:T(8,128)}) fusion(f32[4608]{0:T(1024)S(1)} %copy-done.56, bf16[512,1152]{1,0:T(8,128)(2,1)S(1)} %bitcast.164, bf16[1152,9216]{1,0:T(8,128)(2,1)} %bitcast.171), kind=kOutput, calls=%fused_computation.9 | convolution fusion | flops 5459410944 | bytes 25970688 | tf_op jit(solution)/shard_map/dot_general | solution.py:33
  299.7 4.2 all-gather.2.cloned.1.call-done
  303.9 16.3 %fusion.65 = (bf16[4608]{0:T(1024)(128)(2,1)}, bf16[512,4608]{1,0:T(8,128)(2,1)S(1)}) fusion(f32[512,4608]{1,0:T(8,128)} %get-tuple-element.99, f32[4608]{0:T(1024)} %reshape.313, bf16[512,1152]{1,0:T(8,128)(2,1)} %bitcast.153, bf16[4608,1152]{1,0:T(8,128)(2,1)} %all-gather.2.cloned.1.call-done), kind=kOutput, calls=%fused_computation.146 | convolution fusion | flops 5487717888 | bytes 25979904 | tf_op jit(solution)/shard_map/dot_general | solution.py:37
  320.1 11.0 %fusion.34 = (f32[512]{0:T(512)S(1)}, f32[512,1152]{1,0:T(8,128)S(1)}) fusion(f32[2,1152]{1,0:T(2,128)S(1)} %copy-done.42, bf16[512,4608]{1,0:T(8,128)(2,1)S(1)} %get-tuple-element.70, bf16[1152,9216]{1,0:T(8,128)(2,1)} %bitcast.172), kind=kOutput, calls=%fused_computation.51 | convolution fusion | flops 5436997120 | bytes 17705984 | tf_op jit(solution)/shard_map/dot_general | solution.py:37
  335.1 10.2 %convolution_add_fusion = f32[512,1152]{1,0:T(8,128)S(1)} fusion(bf16[512,4608]{1,0:T(8,128)(2,1)} %get-tuple-element.28, bf16[4608,1152]{1,0:T(8,128)(2,1)} %all-gather.2.cloned.1.call-done, f32[1152]{0:T(1024)} %reshape.314), kind=kOutput, calls=%fused_computation.29 | convolution fusion | flops 5436407808 | bytes 17699328 | tf_op jit(solution)/shard_map/dot_general | solution.py:33
  345.4 3.1 multiply_reduce_fusion.3
  352.0 3.6 convolution_convert_fusion
  355.6 4.7 reshape.318
  360.3 3.1 copy.61
  363.4 5.6 multiply_reduce_fusion
  369.0 4.9 multiply_convert_fusion.1
  386.7 9.1 %fusion.33 = (f32[512]{0:T(512)}, f32[512,1152]{1,0:T(8,128)S(1)}) fusion(f32[2,1152]{1,0:T(2,128)S(1)} %copy-done.41, bf16[512,3456]{0,1:T(8,128)(2,1)S(1)} %constant_dynamic-update-slice_fusion, bf16[1152,9216]{1,0:T(8,128)(2,1)} %bitcast.174), kind=kOutput, calls=%fused_computation.48 | convolution fusion | flops 4078042624 | bytes 13872128 | tf_op jit(solution)/shard_map/dot_general | solution.py:37
  395.9 4.0 reduce.4
  417.7 23.1 %tail.1 = (f32[1152,432]{1,0:T(8,128)}, f32[8,432]{1,0:T(8,128)}, f32[8,1152]{1,0:T(8,128)}) custom-call(bf16[16,8,432]{2,1,0:T(8,128)(2,1)} %pad_maximum_fusion.2.gift_ref, bf16[32,8,1152]{2,1,0:T(8,128)(2,1)} %get-tuple-element.26.all_ref, bf16[1152,432]{1,0:T(8,128)(2,1)} %copy.48.refs_1_.weight_ref), custom_call_target="tpu_custom_call" | custom-call | tf_op jit(solution)/shard_map/tail/pallas_call | solution.py:555
  442.8 6.7 copy.77
  462.3 3.8 pad_maximum_fusion.at_ref
  466.0 177.0 %reduce_weights.1 = f32[36,72,384]{2,1,0:T(8,128)} custom-call(bf16[7,2,576,512]{3,2,1,0:T(8,128)(2,1)} %pad_maximum_fusion.at_ref, bf16[512,10368]{1,0:T(8,128)(2,1)} %constant_dynamic-update-slice_fusion.9.b_ref), custom_call_target="tpu_custom_call" | custom-call | tf_op jit(solution)/shard_map/reduce_weights/pallas_call | solution.py:241
  (258 shorter events, 123.4 us)
Async XLA Ops:
  7.2 6.1 copy-start.38
  7.2 6.1 copy-start.39
  7.2 296.7 %all-gather.2.cloned.1.call-start = ((), (), s32[]{:S(2)}) async-start(), calls=%async_computation | async-start | bytes 11280384 | tf_op jit(solution)/shard_map/all_gather | solution.py:633
  15.3 198.4 %copy-start.1 = (bf16[2,256,1152]{2,1,0:T(8,128)(2,1)S(1)}, bf16[2,256,1152]{2,1,0:T(8,128)(2,1)}, u32[]{:S(2)}) copy-start(bf16[2,256,1152]{2,1,0:T(8,128)(2,1)} %param.14) | copy-start | bytes 3538948
  234.4 22.3 %copy-start.11 = (bf16[2,256,16,72]{1,3,2,0:T(8,128)(2,1)}, bf16[2,256,16,72]{1,3,2,0:T(8,128)(2,1)S(1)}, u32[]{:S(2)}) copy-start(bf16[2,256,16,72]{1,3,2,0:T(8,128)(2,1)S(1)} %copy.56) | copy-start | bytes 3538948
  242.1 10.3 %copy-start.13 = (bf16[2,256,16,72]{1,3,2,0:T(8,128)(2,1)}, bf16[2,256,16,72]{1,3,2,0:T(8,128)(2,1)S(1)}, u32[]{:S(2)}) copy-start(bf16[2,256,16,72]{1,3,2,0:T(8,128)(2,1)S(1)} %copy.54) | copy-start | bytes 3538948
  260.5 7.9 %copy-start.22 = (bf16[2,256,1152]{2,1,0:T(8,128)(2,1)S(1)}, bf16[2,256,1152]{2,1,0:T(8,128)(2,1)}, u32[]{:S(2)}) copy-start(bf16[2,256,1152]{2,1,0:T(8,128)(2,1)} %param.27) | copy-start | bytes 3538948
  262.0 12.9 %copy-start.19 = (bf16[144,8,2,256]{3,1,2,0:T(8,128)(2,1)}, bf16[144,8,2,256]{3,1,2,0:T(8,128)(2,1)S(1)}, u32[]{:S(2)}) copy-start(bf16[144,8,2,256]{3,1,2,0:T(8,128)(2,1)S(1)} %copy.105) | copy-start | bytes 3538948
  320.1 11.0 %copy-start.29 = (bf16[512,4608]{1,0:T(8,128)(2,1)}, bf16[512,4608]{1,0:T(8,128)(2,1)S(1)}, u32[]{:S(2)}) copy-start(bf16[512,4608]{1,0:T(8,128)(2,1)S(1)} %get-tuple-element.70) | copy-start | bytes 14155780
  320.1 11.0 %copy-start.52 = (f32[2,256]{1,0:T(2,128)S(1)}, f32[2,256]{1,0:T(2,128)}, u32[]{:S(2)}) copy-start(f32[2,256]{1,0:T(2,128)} %copy-done.51) | copy-start | bytes 6148
  335.1 10.3 %copy-start.4 = (f32[512,1152]{1,0:T(8,128)S(1)}, f32[512,1152]{1,0:T(8,128)}, u32[]{:S(2)}) copy-start(f32[512,1152]{1,0:T(8,128)} %copy-done.3) | copy-start | bytes 7077892
  335.1 10.3 %copy-start.10 = (f32[512,1152]{1,0:T(8,128)S(1)}, f32[512,1152]{1,0:T(8,128)}, u32[]{:S(2)}) copy-start(f32[512,1152]{1,0:T(8,128)} %copy-done.9) | copy-start | bytes 7077892
  335.1 10.3 %copy-start.23 = (bf16[2,256,1152]{2,1,0:T(8,128)(2,1)S(1)}, bf16[2,256,1152]{2,1,0:T(8,128)(2,1)}, u32[]{:S(2)}) copy-start(bf16[2,256,1152]{2,1,0:T(8,128)(2,1)} %param.27) | copy-start | bytes 3538948
  335.1 10.3 %copy-start.44 = (f32[2,1152]{1,0:T(2,128)S(1)}, f32[2,1152]{1,0:T(2,128)}, u32[]{:S(2)}) copy-start(f32[2,1152]{1,0:T(2,128)} %get-tuple-element.82) | copy-start | bytes 27652
  335.1 10.3 %copy-start.53 = (f32[2,256]{1,0:T(2,128)S(1)}, f32[2,256]{1,0:T(2,128)}, u32[]{:S(2)}) copy-start(f32[2,256]{1,0:T(2,128)} %copy-done.51) | copy-start | bytes 6148
  335.1 10.3 %copy-start.58 = (f32[2,256]{1,0:T(2,128)S(1)}, f32[2,256]{1,0:T(2,128)}, u32[]{:S(2)}) copy-start(f32[2,256]{1,0:T(2,128)} %broadcast_multiply_fusion.3) | copy-start | bytes 6148
  335.1 10.3 %copy-start.59 = (f32[2,256]{1,0:T(2,128)S(1)}, f32[2,256]{1,0:T(2,128)}, u32[]{:S(2)}) copy-start(f32[2,256]{1,0:T(2,128)} %div.40) | copy-start | bytes 6148
  335.1 10.3 %copy-start.61 = (f32[2]{0:T(128)S(1)}, f32[2]{0:T(128)}, u32[]{:S(2)}) copy-start(f32[2]{0:T(128)} %copy-done.60) | copy-start | bytes 28
  363.4 5.6 copy-start.37
  363.4 13.2 %slice-start = ((s8[8388608]{0:T(1024)(128)(4,1)}), s8[4194304]{0:T(1024)(128)(4,1)S(1)}, s32[]{:S(2)}) async-start(s8[8388608]{0:T(1024)(128)(4,1)} %bitcast.128), calls=%async_computation.1 | async-start | bytes 8388608
  369.0 7.6 %slice-start.1 = ((s8[8388608]{0:T(1024)(128)(4,1)}), s8[4194304]{0:T(1024)(128)(4,1)S(1)}, s32[]{:S(2)}) async-start(s8[8388608]{0:T(1024)(128)(4,1)} %bitcast.128), calls=%async_computation.2 | async-start | bytes 8388608
  395.9 11.2 %copy-start.7 = (f32[512,1152]{1,0:T(8,128)}, f32[512,1152]{1,0:T(8,128)S(1)}, u32[]{:S(2)}) copy-start(f32[512,1152]{1,0:T(8,128)S(1)} %get-tuple-element.105) | copy-start | bytes 7077892
  442.8 14.9 %slice-start.2 = ((s8[4718592]{0:T(1024)(128)(4,1)}), s8[524288]{0:T(1024)(128)(4,1)S(1)}, s32[]{:S(2)}) async-start(s8[4718592]{0:T(1024)(128)(4,1)} %bitcast.150), calls=%async_computation.3 | async-start | bytes 1048576
  449.5 8.2 %slice-start.3 = ((s8[4718592]{0:T(1024)(128)(4,1)}), s8[4194304]{0:T(1024)(128)(4,1)S(1)}, s32[]{:S(2)}) async-start(s8[4718592]{0:T(1024)(128)(4,1)} %bitcast.150), calls=%async_computation.4 | async-start | bytes 8388608
  (44 other events, 103.6 us)
Sparse Core Ops, SparseCore 0:
  211.2 92.6 all-gather.1

commit v5 on v4

--- a/solution.py
+++ b/solution.py
@@ -10,7 +10,7 @@
 
 HEADS = 16
 MESH = pl.DeviceIdType.MESH
-DEPTH = 2
+DEPTH = 4
 
 
 norm_eps = 1e-06
@@ -389,15 +389,17 @@
 
     def run():
         stages = (lambda chunk: [own(chunk)] + along_z(chunk), one, two, across)
-        for turn in range(chunks + 3):
-            for stage in (3, 2, 1, 0):
-                chunk = turn - stage
+        for turn in range(chunks + 4):
+            for stage in (2, 1, 0):
+                chunk = turn - 2 * stage
                 if 0 <= chunk < chunks:
                     for copy in stages[stage](chunk):
                         copy.wait()
-                    if stage < 3:
-                        for copy in stages[stage + 1](chunk):
-                            copy.start()
+                    for copy in stages[stage + 1](chunk):
+                        copy.start()
+        for chunk in range(chunks):
+            for copy in across(chunk):
+                copy.wait()
 
     return begin, run
 

time: 681 us -> 616 us (0.905)
  Pallas kernels: 396 us -> 335 us
    pallas_call x1, Pallas kernels: 196 us -> 140 us  [front(): pl.pallas_call(partial(front_kernel, narrow_count, wide_count, with_weigh...]
  transfers between devices with their start and end apart: 1 -> 1, of which waited for: 1 -> 0; matrix products, arithmetic and copies ran while one was open for 13% -> 14% of each run, Pallas kernels for 0% -> 0%
where the time goes in v5:
time: 616 us; the launch traced here: 606 us
  Pallas kernels  335 us (54%)
  local copies, waits for them, and re-layouts  122 us (20%)
  matrix products  90.3 us (15%)
  other arithmetic  43.6 us (7%)
  between operations  16 us (3%)
    pallas_call x1, Pallas kernels, reduce_weights(): pl.pallas_call(reduce_kernel, out_shape=jax.ShapeDtypeStruct((2 * n,) + u...  173 us
    pallas_call x1, Pallas kernels, front(): pl.pallas_call(partial(front_kernel, narrow_count, wide_count, with_weigh...  140 us
    dot_general x4, matrix products, matmul_back(): lax.dot_general(left, right, (((1,), (1,)), ((), ())), preferred_element_...  40 us
    dot_general x4, matrix products, matmul_rows(): return jnp.dot(left, right, preferred_element_type=jnp.float32)  36.6 us
    unnamed x156, local copies, waits for them, and re-layouts  34.9 us
    pallas_call x1, Pallas kernels, tail(): pl.pallas_call(partial(tail_kernel, narrow_count, wide_count), out_shape=...  22.2 us
  transfers between devices with their start and end apart: 1, of which 0 were waited for; matrix products, arithmetic and copies ran while one was open for 14% of the time, Pallas kernels for 0%

profile of v5, /device:TPU:0, one launch (start us, length us, event | category | flops | bytes accessed | tf_op | source)
XLA Modules:
  0.0 606.3 jit_solution(5885932337528150494)
XLA Ops:
  15.3 139.5 %front.1 = (bf16[32,8,1152]{2,1,0:T(8,128)(2,1)}, bf16[16,8,432]{2,1,0:T(8,128)(2,1)}, bf16[4,2,2,72,9216]{4,3,2,1,0:T(8,128)(2,1)}) custom-call(bf16[8,1152]{1,0:T(8,128)(2,1)} %maximum_maximum_fusion.refs_0_, bf16[1152,432]{1,0:T(8,128)(2,1)} %copy.48.refs_1_.weight_ref, bf16[1,432]{1,0:T(2,128)(2,1)} %broadcast_in_dim.12.refs_2_, ...), custom_call_target="tpu_custom_call" | custom-call | tf_op jit(solution)/shard_map/front/pallas_call | solution.py:523
  160.9 8.9 %add_convert_fusion = bf16[512,3456]{1,0:T(8,128)(2,1)S(1)} fusion(bf16[512,1152]{1,0:T(8,128)(2,1)S(1)} %bitcast.162, bf16[1152,9216]{1,0:T(8,128)(2,1)} %bitcast.169, f32[3456]{0:T(1024)S(1)} %pad_maximum_fusion.3), kind=kOutput, calls=%fused_computation.20 | convolution fusion | flops 4080402432 | bytes 12695040 | tf_op jit(solution)/shard_map/dot_general | solution.py:33
  171.1 4.7 reshape.315
  175.8 3.0 copy.56
  178.8 4.7 reshape.316
  186.5 6.0 reshape.317
  192.5 4.5 copy.55
  215.8 3.6 convolution_add_fusion.1
  230.4 13.8 %multiply_convert_fusion = (bf16[512,4608]{1,0:T(8,128)(2,1)}, f32[512,4608]{1,0:T(8,128)}) fusion(f32[4608]{0:T(1024)S(1)} %copy-done.56, bf16[512,1152]{1,0:T(8,128)(2,1)S(1)} %bitcast.164, bf16[1152,9216]{1,0:T(8,128)(2,1)} %bitcast.171), kind=kOutput, calls=%fused_computation.9 | convolution fusion | flops 5459410944 | bytes 25970688 | tf_op jit(solution)/shard_map/dot_general | solution.py:33
  244.2 16.3 %fusion.65 = (bf16[4608]{0:T(1024)(128)(2,1)}, bf16[512,4608]{1,0:T(8,128)(2,1)S(1)}) fusion(f32[512,4608]{1,0:T(8,128)} %get-tuple-element.99, f32[4608]{0:T(1024)} %reshape.313, bf16[512,1152]{1,0:T(8,128)(2,1)} %bitcast.153, bf16[4608,1152]{1,0:T(8,128)(2,1)} %all-gather.2.cloned.1.call-done), kind=kOutput, calls=%fused_computation.146 | convolution fusion | flops 5487717888 | bytes 25979904 | tf_op jit(solution)/shard_map/dot_general | solution.py:37
  260.5 11.0 %fusion.34 = (f32[512]{0:T(512)S(1)}, f32[512,1152]{1,0:T(8,128)S(1)}) fusion(f32[2,1152]{1,0:T(2,128)S(1)} %copy-done.42, bf16[512,4608]{1,0:T(8,128)(2,1)S(1)} %get-tuple-element.70, bf16[1152,9216]{1,0:T(8,128)(2,1)} %bitcast.172), kind=kOutput, calls=%fused_computation.51 | convolution fusion | flops 5436997120 | bytes 17705984 | tf_op jit(solution)/shard_map/dot_general | solution.py:37
  275.5 10.2 %convolution_add_fusion = f32[512,1152]{1,0:T(8,128)S(1)} fusion(bf16[512,4608]{1,0:T(8,128)(2,1)} %get-tuple-element.28, bf16[4608,1152]{1,0:T(8,128)(2,1)} %all-gather.2.cloned.1.call-done, f32[1152]{0:T(1024)} %reshape.314), kind=kOutput, calls=%fused_computation.29 | convolution fusion | flops 5436407808 | bytes 17699328 | tf_op jit(solution)/shard_map/dot_general | solution.py:33
  285.8 3.1 multiply_reduce_fusion.3
  292.4 3.6 convolution_convert_fusion
  296.0 4.7 reshape.318
  300.7 3.1 copy.61
  303.8 5.6 multiply_reduce_fusion
  309.4 4.9 multiply_convert_fusion.1
  327.1 9.1 %fusion.33 = (f32[512]{0:T(512)}, f32[512,1152]{1,0:T(8,128)S(1)}) fusion(f32[2,1152]{1,0:T(2,128)S(1)} %copy-done.41, bf16[512,3456]{0,1:T(8,128)(2,1)S(1)} %constant_dynamic-update-slice_fusion, bf16[1152,9216]{1,0:T(8,128)(2,1)} %bitcast.174), kind=kOutput, calls=%fused_computation.48 | convolution fusion | flops 4078042624 | bytes 13872128 | tf_op jit(solution)/shard_map/dot_general | solution.py:37
  336.2 4.0 reduce.4
  358.1 22.2 %tail.1 = (f32[1152,432]{1,0:T(8,128)}, f32[8,432]{1,0:T(8,128)}, f32[8,1152]{1,0:T(8,128)}) custom-call(bf16[16,8,432]{2,1,0:T(8,128)(2,1)} %pad_maximum_fusion.2.gift_ref, bf16[32,8,1152]{2,1,0:T(8,128)(2,1)} %get-tuple-element.26.all_ref, bf16[1152,432]{1,0:T(8,128)(2,1)} %copy.48.refs_1_.weight_ref), custom_call_target="tpu_custom_call" | custom-call | tf_op jit(solution)/shard_map/tail/pallas_call | solution.py:557
  382.3 6.7 %copy.77 = bf16[4608,512]{1,0:T(8,128)(2,1)} copy(bf16[4608,512]{0,1:T(8,128)(2,1)} %bitcast.152) | data formatting | bytes 9437184 | tf_op jit(solution)/shard_map/transpose | solution.py:278
  401.8 3.8 pad_maximum_fusion.at_ref
  405.5 172.9 %reduce_weights.1 = f32[36,72,384]{2,1,0:T(8,128)} custom-call(bf16[7,2,576,512]{3,2,1,0:T(8,128)(2,1)} %pad_maximum_fusion.at_ref, bf16[512,10368]{1,0:T(8,128)(2,1)} %constant_dynamic-update-slice_fusion.9.b_ref), custom_call_target="tpu_custom_call" | custom-call | tf_op jit(solution)/shard_map/reduce_weights/pallas_call | solution.py:241
  (258 shorter events, 120.4 us)
Async XLA Ops:
  7.2 6.1 %copy-start.38 = (bf16[72,4608]{1,0:T(8,128)(2,1)S(1)}, bf16[72,4608]{1,0:T(8,128)(2,1)}, u32[]{:S(2)}) copy-start(bf16[72,4608]{1,0:T(8,128)(2,1)} %param.23) | copy-start | bytes 1990660
  7.2 6.1 %copy-start.39 = (bf16[72,3456]{1,0:T(8,128)(2,1)S(1)}, bf16[72,3456]{1,0:T(8,128)(2,1)}, u32[]{:S(2)}) copy-start(bf16[72,3456]{1,0:T(8,128)(2,1)} %param.19) | copy-start | bytes 1492996
  7.2 237.0 %all-gather.2.cloned.1.call-start = ((), (), s32[]{:S(2)}) async-start(), calls=%async_computation | async-start | bytes 11280384 | tf_op jit(solution)/shard_map/all_gather | solution.py:635
  15.3 142.2 %copy-start.1 = (bf16[2,256,1152]{2,1,0:T(8,128)(2,1)S(1)}, bf16[2,256,1152]{2,1,0:T(8,128)(2,1)}, u32[]{:S(2)}) copy-start(bf16[2,256,1152]{2,1,0:T(8,128)(2,1)} %param.14) | copy-start | bytes 3538948
  178.8 22.4 %copy-start.11 = (bf16[2,256,16,72]{1,3,2,0:T(8,128)(2,1)}, bf16[2,256,16,72]{1,3,2,0:T(8,128)(2,1)S(1)}, u32[]{:S(2)}) copy-start(bf16[2,256,16,72]{1,3,2,0:T(8,128)(2,1)S(1)} %copy.56) | copy-start | bytes 3538948
  186.5 10.5 %copy-start.13 = (bf16[2,256,16,72]{1,3,2,0:T(8,128)(2,1)}, bf16[2,256,16,72]{1,3,2,0:T(8,128)(2,1)S(1)}, u32[]{:S(2)}) copy-start(bf16[2,256,16,72]{1,3,2,0:T(8,128)(2,1)S(1)} %copy.54) | copy-start | bytes 3538948
  205.1 7.9 %copy-start.22 = (bf16[2,256,1152]{2,1,0:T(8,128)(2,1)S(1)}, bf16[2,256,1152]{2,1,0:T(8,128)(2,1)}, u32[]{:S(2)}) copy-start(bf16[2,256,1152]{2,1,0:T(8,128)(2,1)} %param.27) | copy-start | bytes 3538948
  206.6 12.9 %copy-start.19 = (bf16[144,8,2,256]{3,1,2,0:T(8,128)(2,1)}, bf16[144,8,2,256]{3,1,2,0:T(8,128)(2,1)S(1)}, u32[]{:S(2)}) copy-start(bf16[144,8,2,256]{3,1,2,0:T(8,128)(2,1)S(1)} %copy.105) | copy-start | bytes 3538948
  260.5 11.0 %copy-start.29 = (bf16[512,4608]{1,0:T(8,128)(2,1)}, bf16[512,4608]{1,0:T(8,128)(2,1)S(1)}, u32[]{:S(2)}) copy-start(bf16[512,4608]{1,0:T(8,128)(2,1)S(1)} %get-tuple-element.70) | copy-start | bytes 14155780
  260.5 11.0 %copy-start.52 = (f32[2,256]{1,0:T(2,128)S(1)}, f32[2,256]{1,0:T(2,128)}, u32[]{:S(2)}) copy-start(f32[2,256]{1,0:T(2,128)} %copy-done.51) | copy-start | bytes 6148
  275.4 10.3 %copy-start.4 = (f32[512,1152]{1,0:T(8,128)S(1)}, f32[512,1152]{1,0:T(8,128)}, u32[]{:S(2)}) copy-start(f32[512,1152]{1,0:T(8,128)} %copy-done.3) | copy-start | bytes 7077892
  275.5 10.3 %copy-start.10 = (f32[512,1152]{1,0:T(8,128)S(1)}, f32[512,1152]{1,0:T(8,128)}, u32[]{:S(2)}) copy-start(f32[512,1152]{1,0:T(8,128)} %copy-done.9) | copy-start | bytes 7077892
  275.5 10.3 %copy-start.23 = (bf16[2,256,1152]{2,1,0:T(8,128)(2,1)S(1)}, bf16[2,256,1152]{2,1,0:T(8,128)(2,1)}, u32[]{:S(2)}) copy-start(bf16[2,256,1152]{2,1,0:T(8,128)(2,1)} %param.27) | copy-start | bytes 3538948
  275.5 10.3 %copy-start.44 = (f32[2,1152]{1,0:T(2,128)S(1)}, f32[2,1152]{1,0:T(2,128)}, u32[]{:S(2)}) copy-start(f32[2,1152]{1,0:T(2,128)} %get-tuple-element.82) | copy-start | bytes 27652
  275.5 10.3 %copy-start.53 = (f32[2,256]{1,0:T(2,128)S(1)}, f32[2,256]{1,0:T(2,128)}, u32[]{:S(2)}) copy-start(f32[2,256]{1,0:T(2,128)} %copy-done.51) | copy-start | bytes 6148
  275.5 10.3 %copy-start.58 = (f32[2,256]{1,0:T(2,128)S(1)}, f32[2,256]{1,0:T(2,128)}, u32[]{:S(2)}) copy-start(f32[2,256]{1,0:T(2,128)} %broadcast_multiply_fusion.3) | copy-start | bytes 6148
  275.5 10.3 %copy-start.59 = (f32[2,256]{1,0:T(2,128)S(1)}, f32[2,256]{1,0:T(2,128)}, u32[]{:S(2)}) copy-start(f32[2,256]{1,0:T(2,128)} %div.40) | copy-start | bytes 6148
  275.5 10.3 %copy-start.61 = (f32[2]{0:T(128)S(1)}, f32[2]{0:T(128)}, u32[]{:S(2)}) copy-start(f32[2]{0:T(128)} %copy-done.60) | copy-start | bytes 28
  303.8 5.6 copy-start.37
  303.8 13.2 %slice-start = ((s8[8388608]{0:T(1024)(128)(4,1)}), s8[4194304]{0:T(1024)(128)(4,1)S(1)}, s32[]{:S(2)}) async-start(s8[8388608]{0:T(1024)(128)(4,1)} %bitcast.128), calls=%async_computation.1 | async-start | bytes 8388608
  309.4 7.6 %slice-start.1 = ((s8[8388608]{0:T(1024)(128)(4,1)}), s8[4194304]{0:T(1024)(128)(4,1)S(1)}, s32[]{:S(2)}) async-start(s8[8388608]{0:T(1024)(128)(4,1)} %bitcast.128), calls=%async_computation.2 | async-start | bytes 8388608
  336.2 11.2 %copy-start.7 = (f32[512,1152]{1,0:T(8,128)}, f32[512,1152]{1,0:T(8,128)S(1)}, u32[]{:S(2)}) copy-start(f32[512,1152]{1,0:T(8,128)S(1)} %get-tuple-element.105) | copy-start | bytes 7077892
  382.3 14.9 %slice-start.2 = ((s8[4718592]{0:T(1024)(128)(4,1)}), s8[524288]{0:T(1024)(128)(4,1)S(1)}, s32[]{:S(2)}) async-start(s8[4718592]{0:T(1024)(128)(4,1)} %bitcast.150), calls=%async_computation.3 | async-start | bytes 1048576
  389.0 8.2 %slice-start.3 = ((s8[4718592]{0:T(1024)(128)(4,1)}), s8[4194304]{0:T(1024)(128)(4,1)S(1)}, s32[]{:S(2)}) async-start(s8[4718592]{0:T(1024)(128)(4,1)} %bitcast.150), calls=%async_computation.4 | async-start | bytes 8388608
  (44 other events, 103.6 us)
Sparse Core Ops, SparseCore 0:
  155.0 88.2 all-gather.1

commit v6 on v5

--- a/solution.py
+++ b/solution.py
@@ -581,6 +581,69 @@
     return ada, misc[:slots].sum(axis=0), cond[:slots], grads
 
 
+def head_parts(ref, head, width, count):
+    at = head * width
+    span = width * HEADS
+    return [ref[0, :, number * span + at : number * span + at + width] for number in range(count)]
+
+
+def attend_kernel(projected_ref, out_ref, lse_ref):
+    width = out_ref.shape[2] // HEADS
+    scale = width ** (-0.5)
+    for head in range(HEADS):
+        query, key, value = head_parts(projected_ref, head, width, 3)
+        scores = matmul_back(query, key) * scale
+        top = jnp.max(scores, axis=-1, keepdims=True)
+        lse = top + jnp.log(jnp.sum(jnp.exp(scores - top), axis=-1, keepdims=True))
+        probs = jnp.exp(scores - lse).astype(jnp.bfloat16)
+        out_ref[0, :, head * width : head * width + width] = matmul_rows(probs, value).astype(
+            jnp.bfloat16
+        )
+        lse_ref[0, :, head : head + 1] = lse
+
+
+def attend_back_kernel(projected_ref, grad_ref, lse_ref, out_ref):
+    model_width = grad_ref.shape[2]
+    width = model_width // HEADS
+    scale = width ** (-0.5)
+    for head in range(HEADS):
+        query, key, value = head_parts(projected_ref, head, width, 3)
+        (grad,) = head_parts(grad_ref, head, width, 1)
+        scores = matmul_back(query, key) * scale
+        probs = jnp.exp(scores - lse_ref[0, :, head : head + 1])
+        grad_value = matmul_outer(probs.astype(jnp.bfloat16), grad)
+        grad_probs = matmul_back(grad, value)
+        row_dot = jnp.sum(grad_probs * probs, axis=-1, keepdims=True)
+        grad_scores = (probs * (grad_probs - row_dot)).astype(jnp.bfloat16)
+        grad_query = matmul_rows(grad_scores, key) * scale
+        grad_key = matmul_outer(grad_scores, query) * scale
+        for number, part in enumerate((grad_query, grad_key, grad_value)):
+            at = number * model_width + head * width
+            out_ref[0, :, at : at + width] = part.astype(jnp.bfloat16)
+
+
+def by_image(shape):
+    return pl.BlockSpec((1,) + shape[1:], lambda image: (image, 0, 0))
+
+
+def attend_call(kernel, operands, shapes, name):
+    slots, seq_len = operands[0].shape[:2]
+    work = slots * seq_len * seq_len
+    return pl.pallas_call(
+        kernel,
+        grid=(slots,),
+        out_shape=shapes,
+        in_specs=[by_image(operand.shape) for operand in operands],
+        out_specs=jax.tree.map(lambda shape: by_image(shape.shape), shapes),
+        cost_estimate=pl.CostEstimate(
+            flops=8 * work * operands[0].shape[2] // 3,
+            bytes_accessed=sum(operand.size * 2 for operand in operands) * 2,
+            transcendentals=work * HEADS,
+        ),
+        name=name,
+    )(*operands)
+
+
 def per_device(
     patches,
     condition,
@@ -598,8 +661,6 @@
     cotangent,
 ):
     slots, seq_len, model_width = patches.shape
-    head_dim = model_width // HEADS
-    scale_qk = head_dim ** (-0.5)
     row_total = slots * seq_len
     wide_count = lax.axis_size("wide")
     live = (jnp.arange(slots) < image_counts[0]).astype(jnp.float32)[:, None, None]
@@ -645,17 +706,17 @@
         [proj_bias[:model_width], jnp.zeros((model_width,), jnp.float32), proj_bias[model_width:]]
     )
     projected = (matmul_rows(first_input, w_inproj) + full_bias).astype(jnp.bfloat16)
-    query_rows = projected[:, :model_width].reshape(slots, seq_len, HEADS, head_dim)
-    key_rows = projected[:, model_width : 2 * model_width].reshape(slots, seq_len, HEADS, head_dim)
-    value_rows = projected[:, 2 * model_width :].reshape(slots, seq_len, HEADS, head_dim)
-    scores = (
-        jnp.einsum("sqhe,skhe->shqk", query_rows, key_rows, preferred_element_type=jnp.float32)
-        * scale_qk
-    )
-    log_total = jax.nn.logsumexp(scores, axis=-1, keepdims=True)
-    probs = jnp.exp(scores - log_total).astype(jnp.bfloat16)
-    attended = jnp.einsum("shqk,skhe->sqhe", probs, value_rows, preferred_element_type=jnp.float32)
-    attended = attended.astype(jnp.bfloat16).reshape(row_total, model_width)
+    projected = projected.reshape(slots, seq_len, 3 * model_width)
+    attended, log_total = attend_call(
+        attend_kernel,
+        (projected,),
+        (
+            jax.ShapeDtypeStruct((slots, seq_len, model_width), jnp.bfloat16),
+            jax.ShapeDtypeStruct((slots, seq_len, HEADS), jnp.float32),
+        ),
+        "attend",
+    )
+    attended = attended.reshape(row_total, model_width)
     residual_branch = (matmul_rows(attended, w_outproj) + b_outproj.astype(jnp.float32)).reshape(
         slots, seq_len, model_width
     )
@@ -696,40 +757,14 @@
     grad_attended = (
         matmul_back(residual_branch_gradient, wb_outproj)
         .astype(jnp.bfloat16)
-        .reshape(slots, seq_len, HEADS, head_dim)
-    )
-    scores_again = (
-        jnp.einsum("sqhe,skhe->shqk", query_rows, key_rows, preferred_element_type=jnp.float32)
-        * scale_qk
-    )
-    probs_full = jnp.exp(scores_again - log_total)
-    grad_values = jnp.einsum(
-        "shqk,sqhe->skhe",
-        probs_full.astype(jnp.bfloat16),
-        grad_attended,
-        preferred_element_type=jnp.float32,
-    )
-    grad_probs = jnp.einsum(
-        "sqhe,skhe->shqk", grad_attended, value_rows, preferred_element_type=jnp.float32
-    )
-    row_dot = jnp.sum(grad_probs * probs_full, axis=-1, keepdims=True)
-    grad_scores = (probs_full * (grad_probs - row_dot)).astype(jnp.bfloat16)
-    grad_queries = (
-        jnp.einsum("shqk,skhe->sqhe", grad_scores, key_rows, preferred_element_type=jnp.float32)
-        * scale_qk
-    )
-    grad_keys = (
-        jnp.einsum("shqk,sqhe->skhe", grad_scores, query_rows, preferred_element_type=jnp.float32)
-        * scale_qk
-    )
-    grad_projected = jnp.concatenate(
-        [
-            grad_queries.reshape(row_total, model_width),
-            grad_keys.reshape(row_total, model_width),
-            grad_values.reshape(row_total, model_width),
-        ],
-        axis=1,
-    ).astype(jnp.bfloat16)
+        .reshape(slots, seq_len, model_width)
+    )
+    grad_projected = attend_call(
+        attend_back_kernel,
+        (projected, grad_attended, log_total),
+        jax.ShapeDtypeStruct((slots, seq_len, 3 * model_width), jnp.bfloat16),
+        "attend_back",
+    ).reshape(row_total, 3 * model_width)
     proj_sums = jnp.sum(grad_projected.astype(jnp.float32), axis=0)
     grad_inproj_bias = jnp.concatenate([proj_sums[:model_width], proj_sums[2 * model_width :]])
     first_gradient = matmul_back(grad_projected, wb_inproj).reshape(slots, seq_len, model_width)

time: 616 us -> 608 us (0.987)
  local copies, waits for them, and re-layouts: 122 us -> 66.7 us
  Pallas kernels: 335 us -> 383 us
  waiting for transfers between devices: 0.02 us -> 16.7 us
  matrix products: 90.3 us -> 81.2 us
    pallas_call x0 -> x2, Pallas kernels: none -> 50.1 us  [attend_call(): pl.pallas_call(kernel, grid=(slots,), out_shape=shapes, in_specs=[by_imag...]
    reshape x11 -> x1, local copies, waits for them, and re-layouts: 40.7 us -> 2.66 us  [per_device(): attended = attended.reshape(row_total, model_width)]
    all_gather x1, waiting for transfers between devices: 0.01 us -> 16.6 us  [per_device(): w_down = lax.all_gather(down_weight, 'wide', axis=0, tiled=True)]
    unnamed x156 -> x105, local copies, waits for them, and re-layouts: 34.9 us -> 19.2 us
    dot_general x6 -> x0, matrix products: 13.6 us -> none  [the longest x1 5.57 us: per_device(): jnp.einsum('sqhe,skhe->shqk', grad_attended, value_rows, preferred_elemen...]
    concatenate x0 -> x1, other arithmetic: none -> 8.11 us  [weight_grads(): jnp.concatenate([grad_projected, grad_branch, grad_hidden, grad_mlp], axi...]
  transfers between devices with their start and end apart: 1 -> 1, of which waited for: 0 -> 1; matrix products, arithmetic and copies ran while one was open for 14% -> 8% of each run, Pallas kernels for 0% -> 3%
where the time goes in v6:
time: 608 us; the launch traced here: 601 us
  Pallas kernels  383 us (63%)
  matrix products  81.2 us (13%)
  local copies, waits for them, and re-layouts  66.7 us (11%)
  other arithmetic  37.5 us (6%)
  waiting for transfers between devices  16.7 us (3%)
  between operations  15.4 us (3%)
    pallas_call x1, Pallas kernels, reduce_weights(): pl.pallas_call(reduce_kernel, out_shape=jax.ShapeDtypeStruct((2 * n,) + u...  173 us
    pallas_call x1, Pallas kernels, front(): pl.pallas_call(partial(front_kernel, narrow_count, wide_count, with_weigh...  140 us
    pallas_call x2, Pallas kernels, attend_call(): pl.pallas_call(kernel, grid=(slots,), out_shape=shapes, in_specs=[by_imag...  50.1 us
    dot_general x4, matrix products, matmul_back(): lax.dot_general(left, right, (((1,), (1,)), ((), ())), preferred_element_...  43.8 us
    dot_general x4, matrix products, matmul_rows(): return jnp.dot(left, right, preferred_element_type=jnp.float32)  37.4 us
    pallas_call x1, Pallas kernels, tail(): pl.pallas_call(partial(tail_kernel, narrow_count, wide_count), out_shape=...  20.7 us
    unnamed x105, local copies, waits for them, and re-layouts  19.2 us
    all_gather x1, waiting for transfers between devices, per_device(): w_down = lax.all_gather(down_weight, 'wide', axis=0, tiled=True)  16.6 us
  transfers between devices with their start and end apart: 1, of which 1 were waited for; matrix products, arithmetic and copies ran while one was open for 8% of the time, Pallas kernels for 3%

profile of v6, /device:TPU:0, one launch (start us, length us, event | category | flops | bytes accessed | tf_op | source)
XLA Modules:
  0.0 600.9 jit_solution(4092663040977233033)
XLA Ops:
  8.8 2.4 copy.33.refs_1_.weight_ref
  15.3 139.6 %front.1 = (bf16[32,8,1152]{2,1,0:T(8,128)(2,1)}, bf16[16,8,432]{2,1,0:T(8,128)(2,1)}, bf16[4,2,2,72,9216]{4,3,2,1,0:T(8,128)(2,1)}) custom-call(bf16[8,1152]{1,0:T(8,128)(2,1)} %maximum_maximum_fusion.refs_0_, bf16[1152,432]{1,0:T(8,128)(2,1)} %copy.33.refs_1_.weight_ref, bf16[1,432]{1,0:T(2,128)(2,1)} %broadcast_in_dim.10.refs_2_, ...), custom_call_target="tpu_custom_call" | custom-call | tf_op jit(solution)/shard_map/front/pallas_call | solution.py:523
  165.4 9.6 %add_convert_fusion = bf16[512,3456]{1,0:T(8,128)(2,1)} fusion(bf16[512,1152]{1,0:T(8,128)(2,1)S(1)} %bitcast.105, bf16[1152,9216]{1,0:T(8,128)(2,1)} %bitcast.125, f32[3456]{0:T(1024)S(1)} %pad_maximum_fusion.4), kind=kOutput, calls=%fused_computation.18 | convolution fusion | flops 4080402432 | bytes 12695040 | tf_op jit(solution)/shard_map/dot_general | solution.py:33
  175.0 20.9 %attend.1 = (bf16[2,256,1152]{2,1,0:T(8,128)(2,1)}, f32[2,256,16]{2,1,0:T(8,128)}) custom-call(bf16[2,256,3456]{2,1,0:T(8,128)(2,1)} %bitcast.112), custom_call_target="tpu_custom_call" | custom-call | flops 1207959552 | bytes 7077888 | tf_op jit(solution)/shard_map/attend/pallas_call | solution.py:632
  195.9 2.7 copy.39
  198.6 3.7 convolution_add_fusion.1
  205.8 2.5 copy.41
  208.3 2.5 copy.42
  213.0 13.7 %multiply_convert_fusion = (bf16[512,4608]{1,0:T(8,128)(2,1)}, f32[512,4608]{1,0:T(8,128)}) fusion(f32[4608]{0:T(1024)S(1)} %copy-done.39, bf16[512,1152]{1,0:T(8,128)(2,1)S(1)} %bitcast.107, bf16[1152,9216]{1,0:T(8,128)(2,1)} %bitcast.127), kind=kOutput, calls=%fused_computation.10 | convolution fusion | flops 5459410944 | bytes 25970688 | tf_op jit(solution)/shard_map/dot_general | solution.py:33
  226.7 16.6 %all-gather.2.cloned.1.call-done = bf16[4608,1152]{1,0:T(8,128)(2,1)} async-done(((bf16[288,1152]{1,0:T(8,128)(2,1)}), bf16[4608,1152]{1,0:T(8,128)(2,1)}) %all-gather.2.cloned.1.call-update) | async-done | bytes 10616848 | tf_op jit(solution)/shard_map/all_gather | solution.py:696
  243.4 16.0 %fusion.56 = (bf16[4608]{0:T(1024)(128)(2,1)}, bf16[512,4608]{1,0:T(8,128)(2,1)S(1)}) fusion(f32[512,4608]{1,0:T(8,128)} %get-tuple-element.99, f32[4608]{0:T(1024)} %reshape.269, bf16[512,1152]{1,0:T(8,128)(2,1)S(1)} %bitcast.110, bf16[4608,1152]{1,0:T(8,128)(2,1)} %all-gather.2.cloned.1.call-done), kind=kOutput, calls=%fused_computation.119 | convolution fusion | flops 5487717888 | bytes 25979904 | tf_op jit(solution)/shard_map/dot_general | solution.py:37
  259.4 11.0 %fusion.33 = (f32[512]{0:T(512)S(1)}, f32[512,1152]{1,0:T(8,128)S(1)}) fusion(f32[2,1152]{1,0:T(2,128)S(1)} %get-tuple-element.86, bf16[512,4608]{1,0:T(8,128)(2,1)S(1)} %get-tuple-element.75, bf16[1152,9216]{1,0:T(8,128)(2,1)} %bitcast.128), kind=kOutput, calls=%fused_computation.44 | convolution fusion | flops 5436997120 | bytes 17705984 | tf_op jit(solution)/shard_map/dot_general | solution.py:37
  271.9 10.5 %convolution_add_fusion = f32[512,1152]{1,0:T(8,128)S(1)} fusion(bf16[512,4608]{1,0:T(8,128)(2,1)} %get-tuple-element.31, bf16[4608,1152]{1,0:T(8,128)(2,1)} %all-gather.2.cloned.1.call-done, f32[1152]{0:T(1024)S(1)} %copy-done.42), kind=kOutput, calls=%fused_computation.25 | convolution fusion | flops 5436407808 | bytes 17699328 | tf_op jit(solution)/shard_map/dot_general | solution.py:33
  282.5 3.1 multiply_reduce_fusion.1
  286.8 5.1 convolution_convert_fusion
  291.9 29.2 %attend_back.1 = bf16[2,256,3456]{2,1,0:T(8,128)(2,1)} custom-call(bf16[2,256,3456]{2,1,0:T(8,128)(2,1)} %bitcast.113, bf16[2,256,1152]{2,1,0:T(8,128)(2,1)} %bitcast.118, f32[2,256,16]{2,1,0:T(8,128)} %get-tuple-element.33.lse_ref), custom_call_target="tpu_custom_call" | custom-call | flops 1207959552 | bytes 9469952 | tf_op jit(solution)/shard_map/attend_back/pallas_call | solution.py:632
  321.1 11.8 %fusion.31 = (bf16[2,1152]{1,0:T(2,128)(2,1)}, f32[2,256]{1,0:T(2,128)}, f32[2,256]{1,0:T(2,128)}, bf16[2,1152]{1,0:T(2,128)(2,1)}, f32[2,256,1152]{2,1,0:T(8,128)}) fusion(bf16[2,256,1152]{2,1,0:T(8,128)(2,1)} %param.14, f32[2,256]{1,0:T(2,128)} %copy-done.40, f32[2,256]{1,0:T(2,128)S(1)} %copy-done.38, f32[2,1152]{1,0:T(2,128)S(1)} %copy-done.29, ...), kind=kOutput, calls=%fused_computation.41 | convolution fusion | flops 4082756096 | bytes 15067136 | tf_op jit(solution)/shard_map/dot_general | solution.py:37
  355.3 20.7 %tail.1 = (f32[1152,432]{1,0:T(8,128)}, f32[8,432]{1,0:T(8,128)}, f32[8,1152]{1,0:T(8,128)}) custom-call(bf16[16,8,432]{2,1,0:T(8,128)(2,1)} %pad_maximum_fusion.3.gift_ref, bf16[32,8,1152]{2,1,0:T(8,128)(2,1)} %get-tuple-element.28.all_ref, bf16[1152,432]{1,0:T(8,128)(2,1)} %copy.33.refs_1_.weight_ref), custom_call_target="tpu_custom_call" | custom-call | tf_op jit(solution)/shard_map/tail/pallas_call | solution.py:557
  378.6 6.7 %copy.43 = bf16[4608,512]{1,0:T(8,128)(2,1)} copy(bf16[4608,512]{0,1:T(8,128)(2,1)} %bitcast.100) | data formatting | bytes 9437184 | tf_op jit(solution)/shard_map/transpose | solution.py:278
  385.3 2.9 copy.44
  388.3 8.1 %pad_maximum_fusion.b_ref = bf16[512,10368]{1,0:T(8,128)(2,1)} fusion(bf16[512,1152]{1,0:T(8,128)(2,1)S(1)} %bitcast.111, bf16[512,4608]{1,0:T(8,128)(2,1)} %copy-done.17, bf16[512,1152]{1,0:T(8,128)(2,1)S(1)} %bitcast.109, bf16[512,3456]{1,0:T(8,128)(2,1)S(1)} %bitcast.90), kind=kLoop, calls=%fused_computation.2 | loop fusion | flops 42467328 | bytes 21233664 | tf_op jit(solution)/shard_map/concatenate | solution.py:286
  396.5 3.8 pad_maximum_fusion.1.at_ref
  400.2 173.0 %reduce_weights.1 = f32[36,72,384]{2,1,0:T(8,128)} custom-call(bf16[7,2,576,512]{3,2,1,0:T(8,128)(2,1)} %pad_maximum_fusion.1.at_ref, bf16[512,10368]{1,0:T(8,128)(2,1)} %pad_maximum_fusion.b_ref), custom_call_target="tpu_custom_call" | custom-call | tf_op jit(solution)/shard_map/reduce_weights/pallas_call | solution.py:241
  581.7 2.9 copy.49
  (178 shorter events, 66.8 us)
Async XLA Ops:
  7.2 6.1 %copy-start.24 = (bf16[72,4608]{1,0:T(8,128)(2,1)S(1)}, bf16[72,4608]{1,0:T(8,128)(2,1)}, u32[]{:S(2)}) copy-start(bf16[72,4608]{1,0:T(8,128)(2,1)} %param.23) | copy-start | bytes 1990660
  7.2 6.1 %copy-start.25 = (bf16[72,3456]{1,0:T(8,128)(2,1)S(1)}, bf16[72,3456]{1,0:T(8,128)(2,1)}, u32[]{:S(2)}) copy-start(bf16[72,3456]{1,0:T(8,128)(2,1)} %param.19) | copy-start | bytes 1492996
  7.2 236.2 %all-gather.2.cloned.1.call-start = ((), (), s32[]{:S(2)}) async-start(), calls=%async_computation | async-start | bytes 11280384 | tf_op jit(solution)/shard_map/all_gather | solution.py:696
  15.3 145.2 %copy-start.9 = (bf16[2,256,1152]{2,1,0:T(8,128)(2,1)S(1)}, bf16[2,256,1152]{2,1,0:T(8,128)(2,1)}, u32[]{:S(2)}) copy-start(bf16[2,256,1152]{2,1,0:T(8,128)(2,1)} %param.27) | copy-start | bytes 3538948
  154.9 7.8 %copy-start.1 = (bf16[2,256,1152]{2,1,0:T(8,128)(2,1)S(1)}, bf16[2,256,1152]{2,1,0:T(8,128)(2,1)}, u32[]{:S(2)}) copy-start(bf16[2,256,1152]{2,1,0:T(8,128)(2,1)} %param.14) | copy-start | bytes 3538948
  198.6 3.7 copy-start.30
  205.8 5.0 copy-start.15
  208.3 3.6 copy-start.14
  213.0 30.3 %copy-start.20 = (bf16[2,256,1152]{2,1,0:T(8,128)(2,1)S(1)}, bf16[2,256,1152]{2,1,0:T(8,128)(2,1)}, u32[]{:S(2)}) copy-start(bf16[2,256,1152]{2,1,0:T(8,128)(2,1)} %get-tuple-element.77) | copy-start | bytes 3538948
  259.4 11.0 %copy-start.17 = (bf16[512,4608]{1,0:T(8,128)(2,1)}, bf16[512,4608]{1,0:T(8,128)(2,1)S(1)}, u32[]{:S(2)}) copy-start(bf16[512,4608]{1,0:T(8,128)(2,1)S(1)} %get-tuple-element.75) | copy-start | bytes 14155780
  259.4 11.0 %copy-start.36 = (f32[2,256]{1,0:T(2,128)S(1)}, f32[2,256]{1,0:T(2,128)}, u32[]{:S(2)}) copy-start(f32[2,256]{1,0:T(2,128)} %copy-done.35) | copy-start | bytes 6148
  271.9 10.6 %copy-start.6 = (f32[512,1152]{1,0:T(8,128)S(1)}, f32[512,1152]{1,0:T(8,128)}, u32[]{:S(2)}) copy-start(f32[512,1152]{1,0:T(8,128)} %copy-done.5) | copy-start | bytes 7077892
  271.9 10.6 %copy-start.8 = (f32[512,1152]{1,0:T(8,128)S(1)}, f32[512,1152]{1,0:T(8,128)}, u32[]{:S(2)}) copy-start(f32[512,1152]{1,0:T(8,128)} %copy-done.7) | copy-start | bytes 7077892
  271.9 10.6 %copy-start.10 = (bf16[2,256,1152]{2,1,0:T(8,128)(2,1)S(1)}, bf16[2,256,1152]{2,1,0:T(8,128)(2,1)}, u32[]{:S(2)}) copy-start(bf16[2,256,1152]{2,1,0:T(8,128)(2,1)} %param.27) | copy-start | bytes 3538948
  271.9 10.6 %copy-start.27 = (f32[2,1152]{1,0:T(2,128)S(1)}, f32[2,1152]{1,0:T(2,128)}, u32[]{:S(2)}) copy-start(f32[2,1152]{1,0:T(2,128)} %copy-done.26) | copy-start | bytes 27652
  271.9 10.6 %copy-start.44 = (f32[2]{0:T(128)S(1)}, f32[2]{0:T(128)}, u32[]{:S(2)}) copy-start(f32[2]{0:T(128)} %copy-done.43) | copy-start | bytes 28
  285.7 6.2 %copy-start.3 = (f32[2,256,1152]{2,1,0:T(8,128)}, f32[2,256,1152]{2,1,0:T(8,128)S(1)}, u32[]{:S(2)}) copy-start(f32[2,256,1152]{2,1,0:T(8,128)S(1)} %get-tuple-element.71) | copy-start | bytes 7077892
  286.8 5.1 copy-start.18
  291.9 29.2 %copy-start.29 = (f32[2,1152]{1,0:T(2,128)S(1)}, f32[2,1152]{1,0:T(2,128)}, u32[]{:S(2)}) copy-start(f32[2,1152]{1,0:T(2,128)} %copy-done.28) | copy-start | bytes 27652
  291.9 29.2 %copy-start.38 = (f32[2,256]{1,0:T(2,128)S(1)}, f32[2,256]{1,0:T(2,128)}, u32[]{:S(2)}) copy-start(f32[2,256]{1,0:T(2,128)} %copy-done.37) | copy-start | bytes 6148
  321.1 11.8 %copy-start = (bf16[2,256,3456]{2,1,0:T(8,128)(2,1)S(1)}, bf16[2,256,3456]{2,1,0:T(8,128)(2,1)}, u32[]{:S(2)}) copy-start(bf16[2,256,3456]{2,1,0:T(8,128)(2,1)} %attend_back.1) | copy-start | bytes 10616836
  388.3 8.1 %copy-start.11 = (bf16[1,2,8,72,512]{4,3,2,1,0:T(8,128)(2,1)S(1)}, bf16[1,2,8,72,512]{4,3,2,1,0:T(8,128)(2,1)}, u32[]{:S(2)}) copy-start(bf16[1,2,8,72,512]{4,3,2,1,0:T(8,128)(2,1)} %copy.42) | copy-start | bytes 3538948
  388.3 8.1 %copy-start.12 = (bf16[1,2,8,72,512]{4,3,2,1,0:T(8,128)(2,1)S(1)}, bf16[1,2,8,72,512]{4,3,2,1,0:T(8,128)(2,1)}, u32[]{:S(2)}) copy-start(bf16[1,2,8,72,512]{4,3,2,1,0:T(8,128)(2,1)} %copy.40) | copy-start | bytes 3538948
  388.3 8.1 %copy-start.13 = (bf16[1,2,8,72,512]{4,3,2,1,0:T(8,128)(2,1)S(1)}, bf16[1,2,8,72,512]{4,3,2,1,0:T(8,128)(2,1)}, u32[]{:S(2)}) copy-start(bf16[1,2,8,72,512]{4,3,2,1,0:T(8,128)(2,1)} %copy.38) | copy-start | bytes 3538948
  (24 other events, 56.7 us)
Sparse Core Ops, SparseCore 0:
  155.1 88.2 all-gather.1

commit v7 on v6

--- a/solution.py
+++ b/solution.py
@@ -60,9 +60,9 @@
 
 
 def reduce_kernel(
-    at_ref, b_ref, out_ref,
-    bbuf, gbuf, sbuf, tbuf, ubuf, fbuf, core_in, one_in, two_in, z_in, far_in,
-    bsem, core_sem, one_sem, two_sem, zs_sem, zr_sem, far_sem,
+    a_in, a_out, a_up, a_down, b_in, b_out, b_up, b_down, out_ref,
+    abuf, bbuf, gbuf, sbuf, tbuf, ubuf, fbuf, core_in, one_in, two_in, z_in, far_in,
+    asem, bsem, core_sem, one_sem, two_sem, zs_sem, zr_sem, far_sem,
 ):
     narrow = lax.axis_index("narrow")
     wide = lax.axis_index("wide")
@@ -79,13 +79,30 @@
         pl.semaphore_signal(barrier, inc=1, device_id=peer, device_id_type=MESH)
     pl.semaphore_wait(barrier, 6)
 
+    def copies(left, right, column, half):
+        column = pl.multiple_of(column * LANES, LANES)
+        return (
+            pltpu.make_async_copy(left, abuf.at[half], asem.at[half]),
+            pltpu.make_async_copy(right.at[:, pl.ds(column, LANES)], bbuf.at[half], bsem.at[half]),
+        )
+
     def fetch(chunk, half):
         number = chunk + half * PER_HALF
-        column = number - 3 * ((number - 24) // 3) * (number // 24)
-        column = pl.multiple_of(column * LANES, LANES)
-        return pltpu.make_async_copy(
-            b_ref.at[:, pl.ds(column, LANES)], bbuf.at[half], bsem.at[half]
-        )
+        regions = ((0, 9, a_in, b_in), (9, 12, a_out, b_out), (12, 24, a_up, b_up))
+        for lower, upper, left, right in regions:
+            if half * PER_HALF < upper and lower < (half + 1) * PER_HALF:
+
+                @pl.when(jnp.logical_and(number >= lower, number < upper))
+                def _(lower=lower, left=left, right=right):
+                    for copy in copies(left.at[0], right, number - lower, half):
+                        copy.start()
+
+        if half:
+
+            @pl.when(number >= 24)
+            def _():
+                for copy in copies(a_down.at[(number - 24) // 3], b_down, (number - 24) % 3, half):
+                    copy.start()
 
     def send(src, dst, sems, chunk, peer):
         return pltpu.make_async_remote_copy(
@@ -127,23 +144,18 @@
 
     def make(chunk):
         for half in range(2):
-            number = chunk + half * PER_HALF
-            which = (
-                jnp.where(number >= 9, 1, 0) + jnp.where(number >= 12, 1, 0)
-                + jnp.where(number >= 24, 1, 0) + jnp.where(number >= 27, 1, 0)
-                + jnp.where(number >= 30, 1, 0) + jnp.where(number >= 33, 1, 0)
-            )
-            fetch(chunk, half).wait()
+            for copy in copies(a_in.at[0], b_in, 0, half):
+                copy.wait()
             for side in range(2):
                 product = jnp.dot(
-                    at_ref[which, side], bbuf[half], preferred_element_type=jnp.float32
+                    abuf[half, side], bbuf[half], preferred_element_type=jnp.float32
                 )
                 for unit in range(8):
                     gbuf[side, half, unit] = product[unit * 72 : unit * 72 + 72].astype(jnp.bfloat16)
 
             @pl.when(chunk + 1 < PER_HALF)
             def _():
-                fetch(chunk + 1, half).start()
+                fetch(chunk + 1, half)
 
         core_copy(chunk).start()
 
@@ -202,7 +214,7 @@
         far_copy(chunk).start()
 
     for half in range(2):
-        fetch(0, half).start()
+        fetch(0, half)
 
     def turn(step, carry):
         for parity in range(2):
@@ -233,7 +245,7 @@
     lax.fori_loop(0, PER_HALF, finish, 0)
 
 
-def reduce_weights(transposed, right):
+def reduce_weights(*operands):
     bf = jnp.bfloat16
     dma = pltpu.SemaphoreType.DMA
     unit = (72, LANES)
@@ -241,13 +253,11 @@
     return pl.pallas_call(
         reduce_kernel,
         out_shape=jax.ShapeDtypeStruct((2 * n,) + unit, jnp.float32),
-        in_specs=[
-            pl.BlockSpec(memory_space=pltpu.VMEM),
-            pl.BlockSpec(memory_space=pl.ANY),
-        ],
+        in_specs=[pl.BlockSpec(memory_space=pl.ANY)] * 8,
         out_specs=pl.BlockSpec(memory_space=pltpu.VMEM),
         scratch_shapes=[
-            pltpu.VMEM((2, 512, LANES), bf),
+            pltpu.VMEM((2,) + operands[0].shape[1:], bf),
+            pltpu.VMEM((2, operands[4].shape[0], LANES), bf),
             pltpu.VMEM((2, 2, 8) + unit, bf),
             pltpu.VMEM((DEPTH, 2, 2, 4) + unit, bf),
             pltpu.VMEM((DEPTH, 2, 4) + unit, bf),
@@ -258,6 +268,7 @@
             pltpu.VMEM((n, 4) + unit, bf),
             pltpu.VMEM((n, 3) + unit, bf),
             pltpu.VMEM((n,) + unit, bf),
+            dma((2,)),
             dma((2,)),
             dma((2, n)),
             dma((2, n)),
@@ -270,7 +281,7 @@
             collective_id=1, has_side_effects=True, vmem_limit_bytes=66_000_000
         ),
         name="reduce_weights",
-    )(transposed, right)
+    )(*operands)
 
 
 def by_holder(left, parts):
@@ -280,11 +291,10 @@
 
 
 def weight_grads(first_input, attended, second_in, activated, grad_projected, grad_branch, grad_hidden, grad_mlp):
-    transposed = jnp.concatenate(
-        [by_holder(first_input, 1), by_holder(attended, 1), by_holder(second_in, 1), by_holder(activated, 4)]
-    )
-    right = jnp.concatenate([grad_projected, grad_branch, grad_hidden, grad_mlp], axis=1)
-    done = reduce_weights(transposed, right)
+    done = reduce_weights(
+        by_holder(first_input, 1), by_holder(attended, 1), by_holder(second_in, 1),
+        by_holder(activated, 4), grad_projected, grad_branch, grad_hidden, grad_mlp,
+    )
 
     def flat(lower, upper):
         return done[lower:upper].transpose(1, 0, 2).reshape(72, (upper - lower) * LANES)
@@ -445,14 +455,29 @@
     loop(wide_count, lambda step: deal(step).wait())
 
 
-def tail_kernel(
-    narrow_count, wide_count, gift_ref, all_ref, weight_ref, ada_ref, misc_ref, cond_ref,
-    gifts, part, shares, send_sem, recv_sem, send_two, recv_two,
-):
+def tail_kernel(narrow_count, wide_count, *refs):
+    mod_refs, (in_ref, out_ref, up_ref, down_ref, all_ref, weight_ref) = refs[:6], refs[6:12]
+    ada_ref, misc_ref, cond_ref, wide_mod, layout, gift_ref = refs[12:18]
+    gifts, part, shares, send_sem, recv_sem, send_two, recv_two = refs[18:]
     total = narrow_count * wide_count
     narrow, wide = lax.axis_index("narrow"), lax.axis_index("wide")
     me = narrow * wide_count + wide
     base = narrow * wide_count
+    slots, model_width = mod_refs[0].shape
+    columns = layout.shape[2]
+    for number, ref in enumerate(mod_refs):
+        wide_mod[:slots, number * model_width : (number + 1) * model_width] = ref[...]
+    layout[...] = jnp.zeros_like(layout)
+    for holder in range(wide_count):
+        layout[holder, :slots] = wide_mod[:slots, holder * columns : (holder + 1) * columns]
+        span = 2 * model_width // wide_count
+        at = holder * span
+        at = at if at < model_width else at + model_width
+        layout[holder, 4:5, :span] = in_ref[:, at : at + span]
+        for row, ref in ((5, out_ref), (6, up_ref), (7, down_ref)):
+            span = ref.shape[1] // wide_count
+            layout[holder, row : row + 1, :span] = ref[:, holder * span : (holder + 1) * span]
+    gift_ref[...] = layout[...].astype(jnp.bfloat16)
     meet(total, me, wide_count)
 
     def spread(step):
@@ -539,21 +564,12 @@
     return tuple(results[:2]) + tuple(weights)
 
 
-def tail(grad_modulation, bias_grads, gathered, ada_weight):
+def tail(mod_grads, bias_sums, gathered, ada_weight):
     narrow_count, wide_count = lax.axis_size("narrow"), lax.axis_size("wide")
     total = narrow_count * wide_count
-    slots = grad_modulation.shape[0]
+    slots = mod_grads[0].shape[0]
     model_width, columns = ada_weight.shape
-    blocks = grad_modulation.reshape(slots, wide_count, columns).transpose(1, 0, 2)
-    held = jnp.concatenate(
-        [grad.reshape(wide_count, -1) for grad in bias_grads], axis=1
-    ).astype(jnp.bfloat16)
-    lines = -(-held.shape[1] // columns)
-    held_rows = jnp.pad(held, ((0, 0), (0, lines * columns - held.shape[1])))
-    held_rows = held_rows.reshape(wide_count, lines, columns)
-    gap = jnp.zeros((wide_count, 4 - slots, columns), jnp.bfloat16)
-    end = jnp.zeros((wide_count, 4 - lines, columns), jnp.bfloat16)
-    gift = jnp.concatenate([blocks, gap, held_rows, end], axis=1)
+    operands = list(mod_grads) + [sums[None] for sums in bias_sums] + [gathered, ada_weight]
     ada, misc, cond = pl.pallas_call(
         partial(tail_kernel, narrow_count, wide_count),
         out_shape=(
@@ -561,9 +577,12 @@
             jax.ShapeDtypeStruct((8, columns), jnp.float32),
             jax.ShapeDtypeStruct((8, model_width), jnp.float32),
         ),
-        in_specs=in_vmem(3),
+        in_specs=in_vmem(len(operands)),
         out_specs=tuple(in_vmem(3)),
         scratch_shapes=[
+            pltpu.VMEM((8, 6 * model_width), jnp.float32),
+            pltpu.VMEM((wide_count, 8, columns), jnp.float32),
+            pltpu.VMEM((wide_count, 8, columns), jnp.bfloat16),
             pltpu.VMEM((total, 8, columns), jnp.bfloat16),
             pltpu.VMEM((wide_count, 8, model_width), jnp.bfloat16),
             pltpu.VMEM((wide_count, 8, model_width), jnp.bfloat16),
@@ -571,13 +590,9 @@
         + dmas(total, total, wide_count, wide_count),
         compiler_params=pltpu.CompilerParams(collective_id=3, has_side_effects=True),
         name="tail",
-    )(gift, gathered, ada_weight)
-    flat = misc[4:].reshape(-1)
-    grads, at = [], 0
-    for grad in bias_grads:
-        width = grad.shape[0] // wide_count
-        grads.append(flat[at : at + width])
-        at += width
+    )(*operands)
+    spans = [2 * model_width // wide_count] + [sums.shape[0] // wide_count for sums in bias_sums[1:]]
+    grads = [misc[4 + number, :span] for number, span in enumerate(spans)]
     return ada, misc[:slots].sum(axis=0), cond[:slots], grads
 
 
@@ -766,7 +781,6 @@
         "attend_back",
     ).reshape(row_total, 3 * model_width)
     proj_sums = jnp.sum(grad_projected.astype(jnp.float32), axis=0)
-    grad_inproj_bias = jnp.concatenate([proj_sums[:model_width], proj_sums[2 * model_width :]])
     first_gradient = matmul_back(grad_projected, wb_inproj).reshape(slots, seq_len, model_width)
     selfattn_scale_gradient = jnp.sum(first_gradient * normalized_first, axis=1)
     selfattn_offset_gradient = jnp.sum(first_gradient, axis=1)
@@ -776,20 +790,17 @@
             normalized_first, inverse_deviation, first_gradient * (1.0 + selfattn_scale)
         )
     ).astype(jnp.bfloat16)
-    grad_modulation = jnp.concatenate(
-        [
-            selfattn_offset_gradient,
-            selfattn_scale_gradient,
-            selfattn_gate_gradient,
-            grad_shift_mlp,
-            grad_scale_mlp,
-            grad_gate_mlp,
-        ],
-        axis=1,
-    ).astype(jnp.bfloat16)
+    mod_grads = (
+        selfattn_offset_gradient,
+        selfattn_scale_gradient,
+        selfattn_gate_gradient,
+        grad_shift_mlp,
+        grad_scale_mlp,
+        grad_gate_mlp,
+    )
     grad_ada_weight, grad_ada_bias, grad_cond_act, bias_shares = tail(
-        grad_modulation,
-        (grad_inproj_bias, grad_outproj_bias, grad_up_bias, grad_down_bias),
+        mod_grads,
+        (proj_sums, grad_outproj_bias, grad_up_bias, grad_down_bias),
         gathered,
         ada_weight,
     )

time: 608 us -> 576 us (0.947)
  local copies, waits for them, and re-layouts: 66.7 us -> 49.2 us
  other arithmetic: 37.5 us -> 26 us
    concatenate x4 -> x0, other arithmetic: 14.9 us -> none  [the longest x1 8.11 us: weight_grads(): jnp.concatenate([grad_projected, grad_branch, grad_hidden, grad_mlp], axi...]
    unnamed x105 -> x86, local copies, waits for them, and re-layouts: 19.2 us -> 9.14 us
  transfers between devices with their start and end apart: 1 -> 1, of which waited for: 1 -> 1; matrix products, arithmetic and copies ran while one was open for 8% -> 9% of each run, Pallas kernels for 3% -> 4%
where the time goes in v7:
time: 576 us; the launch traced here: 569 us
  Pallas kernels  381 us (66%)
  matrix products  80.4 us (14%)
  local copies, waits for them, and re-layouts  49.2 us (9%)
  other arithmetic  26 us (5%)
  waiting for transfers between devices  16.2 us (3%)
  between operations  15.7 us (3%)
    pallas_call x1, Pallas kernels, reduce_weights(): pl.pallas_call(reduce_kernel, out_shape=jax.ShapeDtypeStruct((2 * n,) + u...  170 us
    pallas_call x1, Pallas kernels, front(): pl.pallas_call(partial(front_kernel, narrow_count, wide_count, with_weigh...  140 us
    pallas_call x2, Pallas kernels, attend_call(): pl.pallas_call(kernel, grid=(slots,), out_shape=shapes, in_specs=[by_imag...  50.1 us
    dot_general x4, matrix products, matmul_back(): lax.dot_general(left, right, (((1,), (1,)), ((), ())), preferred_element_...  44.1 us
    dot_general x4, matrix products, matmul_rows(): return jnp.dot(left, right, preferred_element_type=jnp.float32)  36.4 us
    pallas_call x1, Pallas kernels, tail(): pl.pallas_call(partial(tail_kernel, narrow_count, wide_count), out_shape=...  21.4 us
    all_gather x1, waiting for transfers between devices, per_device(): w_down = lax.all_gather(down_weight, 'wide', axis=0, tiled=True)  16.2 us
  transfers between devices with their start and end apart: 1, of which 1 were waited for; matrix products, arithmetic and copies ran while one was open for 9% of the time, Pallas kernels for 4%

profile of v7, /device:TPU:0, one launch (start us, length us, event | category | flops | bytes accessed | tf_op | source)
XLA Modules:
  0.0 568.5 jit_solution(4164111539430236621)
XLA Ops:
  10.1 2.4 copy.33.refs_1_.refs_11_
  13.3 2.1 pad_maximum_fusion.refs_3_
  15.3 139.5 %front.1 = (bf16[32,8,1152]{2,1,0:T(8,128)(2,1)}, bf16[16,8,432]{2,1,0:T(8,128)(2,1)}, bf16[4,2,2,72,9216]{4,3,2,1,0:T(8,128)(2,1)}) custom-call(bf16[8,1152]{1,0:T(8,128)(2,1)} %maximum_maximum_fusion.refs_0_, bf16[1152,432]{1,0:T(8,128)(2,1)} %copy.33.refs_1_.refs_11_, bf16[1,432]{1,0:T(2,128)(2,1)} %broadcast_in_dim.18.refs_2_, ...), custom_call_target="tpu_custom_call" | custom-call | tf_op jit(solution)/shard_map/front/pallas_call | solution.py:548
  163.0 2.8 convert_reduce_fusion.3
  168.2 9.6 %add_convert_fusion = bf16[512,3456]{1,0:T(8,128)(2,1)} fusion(bf16[512,1152]{1,0:T(8,128)(2,1)S(1)} %bitcast.111, bf16[1152,9216]{1,0:T(8,128)(2,1)} %bitcast.127, f32[3456]{0:T(1024)S(1)} %pad_maximum_fusion.1), kind=kOutput, calls=%fused_computation.18 | convolution fusion | flops 4080402432 | bytes 12695040 | tf_op jit(solution)/shard_map/dot_general | solution.py:33
  177.8 20.9 %attend.1 = (bf16[2,256,1152]{2,1,0:T(8,128)(2,1)}, f32[2,256,16]{2,1,0:T(8,128)}) custom-call(bf16[2,256,3456]{2,1,0:T(8,128)(2,1)} %bitcast.114), custom_call_target="tpu_custom_call" | custom-call | flops 1207959552 | bytes 7077888 | tf_op jit(solution)/shard_map/attend/pallas_call | solution.py:647
  201.6 3.6 convolution_add_fusion.1
  208.8 2.4 copy.40
  211.1 2.5 copy.41
  213.6 13.5 %multiply_convert_fusion = (bf16[512,4608]{1,0:T(8,128)(2,1)}, f32[512,4608]{1,0:T(8,128)}) fusion(f32[4608]{0:T(1024)S(1)} %copy-done.31, bf16[512,1152]{1,0:T(8,128)(2,1)S(1)} %bitcast.113, bf16[1152,9216]{1,0:T(8,128)(2,1)} %bitcast.129), kind=kOutput, calls=%fused_computation.10 | convolution fusion | flops 5459410944 | bytes 25970688 | tf_op jit(solution)/shard_map/dot_general | solution.py:33
  227.2 16.2 %all-gather.2.cloned.1.call-done = bf16[4608,1152]{1,0:T(8,128)(2,1)} async-done(((bf16[288,1152]{1,0:T(8,128)(2,1)}), bf16[4608,1152]{1,0:T(8,128)(2,1)}) %all-gather.2.cloned.1.call-update) | async-done | bytes 10616848 | tf_op jit(solution)/shard_map/all_gather | solution.py:711
  243.4 16.4 %convert_reduce_fusion = (f32[4608]{0:T(1024)}, bf16[512,4608]{1,0:T(8,128)(2,1)S(1)}) fusion(f32[512,4608]{1,0:T(8,128)} %get-tuple-element.98, f32[4608]{0:T(1024)} %reshape.224, bf16[512,1152]{1,0:T(8,128)(2,1)} %bitcast.104, bf16[4608,1152]{1,0:T(8,128)(2,1)} %all-gather.2.cloned.1.call-done), kind=kOutput, calls=%fused_computation.9 | convolution fusion | flops 5490077184 | bytes 25989120 | tf_op jit(solution)/shard_map/dot_general | solution.py:37
  259.7 12.4 %fusion.33 = (f32[512]{0:T(512)S(1)}, f32[512,1152]{1,0:T(8,128)}) fusion(f32[2,1152]{1,0:T(2,128)S(1)} %get-tuple-element.87, bf16[512,4608]{1,0:T(8,128)(2,1)S(1)} %get-tuple-element.73.b_up, bf16[1152,9216]{1,0:T(8,128)(2,1)} %bitcast.130), kind=kOutput, calls=%fused_computation.44 | convolution fusion | flops 5436997120 | bytes 17705984 | tf_op jit(solution)/shard_map/dot_general | solution.py:37
  273.9 4.0 fusion.34
  278.0 9.6 %convolution_add_fusion = f32[512,1152]{1,0:T(8,128)S(1)} fusion(bf16[512,4608]{1,0:T(8,128)(2,1)S(1)} %copy-done.9, bf16[4608,1152]{1,0:T(8,128)(2,1)} %all-gather.2.cloned.1.call-done, f32[1152]{0:T(1024)S(1)} %copy-done.36), kind=kOutput, calls=%fused_computation.25 | convolution fusion | flops 5436407808 | bytes 17699328 | tf_op jit(solution)/shard_map/dot_general | solution.py:33
  287.7 3.6 convert_reduce_fusion.4
  291.3 5.1 convolution_convert_fusion
  296.4 29.2 %attend_back.1 = bf16[2,256,3456]{2,1,0:T(8,128)(2,1)} custom-call(bf16[2,256,3456]{2,1,0:T(8,128)(2,1)} %bitcast.115, bf16[2,256,1152]{2,1,0:T(8,128)(2,1)} %bitcast.120, f32[2,256,16]{2,1,0:T(8,128)} %get-tuple-element.33.lse_ref), custom_call_target="tpu_custom_call" | custom-call | flops 1207959552 | bytes 9469952 | tf_op jit(solution)/shard_map/attend_back/pallas_call | solution.py:647
  325.7 10.3 %fusion.31 = (f32[2,1152]{1,0:T(2,128)}, f32[2,256]{1,0:T(2,128)S(1)}, f32[2,256]{1,0:T(2,128)S(1)}, f32[2,1152]{1,0:T(2,128)}, f32[2,256,1152]{2,1,0:T(8,128)S(1)}) fusion(bf16[2,256,1152]{2,1,0:T(8,128)(2,1)S(1)} %copy-done.1, f32[2,256]{1,0:T(2,128)S(1)} %copy-done.34, f32[2,256]{1,0:T(2,128)S(1)} %copy-done.25, f32[2,1152]{1,0:T(2,128)S(1)} %copy-done.17, ...), kind=kOutput, calls=%fused_computation.41 | convolution fusion | flops 4082756096 | bytes 15076352 | tf_op jit(solution)/shard_map/dot_general | solution.py:37
  338.5 2.6 multiply_reduce_fusion.1
  341.2 21.4 %tail.1 = (f32[1152,432]{1,0:T(8,128)}, f32[8,432]{1,0:T(8,128)}, f32[8,1152]{1,0:T(8,128)}) custom-call(f32[2,1152]{1,0:T(2,128)} %get-tuple-element.69.refs_0_, f32[2,1152]{1,0:T(2,128)} %get-tuple-element.63.refs_1_, f32[2,1152]{1,0:T(2,128)} %get-tuple-element.82.refs_2_, f32[2,1152]{1,0:T(2,128)} %get-tuple-element.68.refs_3_, ...), custom_call_target="tpu_custom_call" | custom-call | tf_op jit(solution)/shard_map/tail/pallas_call | solution.py:573
  367.7 6.6 %copy.42 = bf16[4608,512]{1,0:T(8,128)(2,1)} copy(bf16[4608,512]{0,1:T(8,128)(2,1)} %bitcast.106) | data formatting | bytes 9437184 | tf_op jit(solution)/shard_map/transpose | solution.py:289
  374.3 4.9 copy.43
  379.2 170.0 %reduce_weights.1 = f32[36,72,384]{2,1,0:T(8,128)} custom-call(bf16[1,2,576,512]{3,2,1,0:T(8,128)(2,1)} %bitcast.101, bf16[1,2,576,512]{3,2,1,0:T(8,128)(2,1)} %bitcast.102, bf16[1,2,576,512]{3,2,1,0:T(8,128)(2,1)} %bitcast.103, bf16[4,2,576,512]{3,2,1,0:T(8,128)(2,1)} %bitcast.95, bf16[512,3456]{1,0:T(8,128)(2,1)} %bitcast.92, bf16[512,1152]{1,0:T(8,128)(2,1)} %bitcast.100, ...), custom_call_target="tpu_custom_call" | custom-call | tf_op jit(solution)/shard_map/reduce_weights/pallas_call | solution.py:253
  (145 shorter events, 41.3 us)
Async XLA Ops:
  7.2 6.1 %copy-start.14 = (bf16[72,4608]{1,0:T(8,128)(2,1)S(1)}, bf16[72,4608]{1,0:T(8,128)(2,1)}, u32[]{:S(2)}) copy-start(bf16[72,4608]{1,0:T(8,128)(2,1)} %param.23) | copy-start | bytes 1990660
  7.2 6.1 %copy-start.15 = (bf16[72,3456]{1,0:T(8,128)(2,1)S(1)}, bf16[72,3456]{1,0:T(8,128)(2,1)}, u32[]{:S(2)}) copy-start(bf16[72,3456]{1,0:T(8,128)(2,1)} %param.19) | copy-start | bytes 1492996
  7.2 236.2 %all-gather.2.cloned.1.call-start = ((), (), s32[]{:S(2)}) async-start(), calls=%async_computation | async-start | bytes 11280384 | tf_op jit(solution)/shard_map/all_gather | solution.py:711
  15.3 146.3 %copy-start.1 = (bf16[2,256,1152]{2,1,0:T(8,128)(2,1)S(1)}, bf16[2,256,1152]{2,1,0:T(8,128)(2,1)}, u32[]{:S(2)}) copy-start(bf16[2,256,1152]{2,1,0:T(8,128)(2,1)} %param.14) | copy-start | bytes 3538948
  154.9 8.1 %copy-start.7 = (bf16[2,256,1152]{2,1,0:T(8,128)(2,1)S(1)}, bf16[2,256,1152]{2,1,0:T(8,128)(2,1)}, u32[]{:S(2)}) copy-start(bf16[2,256,1152]{2,1,0:T(8,128)(2,1)} %param.27) | copy-start | bytes 3538948
  161.7 4.2 copy-start.38
  161.9 3.9 copy-start.24
  201.6 3.6 copy-start.20
  259.7 12.4 %copy-start.11 = (bf16[512,4608]{1,0:T(8,128)(2,1)}, bf16[512,4608]{1,0:T(8,128)(2,1)S(1)}, u32[]{:S(2)}) copy-start(bf16[512,4608]{1,0:T(8,128)(2,1)S(1)} %get-tuple-element.73.b_up) | copy-start | bytes 14155780
  273.9 4.0 copy-start.9
  273.9 4.0 copy-start.36
  277.9 9.7 %copy-start.2 = (f32[512,1152]{1,0:T(8,128)S(1)}, f32[512,1152]{1,0:T(8,128)}, u32[]{:S(2)}) copy-start(f32[512,1152]{1,0:T(8,128)} %get-tuple-element.100) | copy-start | bytes 7077892
  277.9 9.7 %copy-start.8 = (bf16[2,256,1152]{2,1,0:T(8,128)(2,1)S(1)}, bf16[2,256,1152]{2,1,0:T(8,128)(2,1)}, u32[]{:S(2)}) copy-start(bf16[2,256,1152]{2,1,0:T(8,128)(2,1)} %param.27) | copy-start | bytes 3538948
  277.9 9.7 %copy-start.19 = (f32[2,1152]{1,0:T(2,128)S(1)}, f32[2,1152]{1,0:T(2,128)}, u32[]{:S(2)}) copy-start(f32[2,1152]{1,0:T(2,128)} %copy-done.18) | copy-start | bytes 27652
  277.9 9.7 %copy-start.21 = (f32[2,1152]{1,0:T(2,128)S(1)}, f32[2,1152]{1,0:T(2,128)}, u32[]{:S(2)}) copy-start(f32[2,1152]{1,0:T(2,128)} %get-tuple-element.90) | copy-start | bytes 27652
  278.0 9.7 %copy-start.30 = (f32[2,256]{1,0:T(2,128)S(1)}, f32[2,256]{1,0:T(2,128)}, u32[]{:S(2)}) copy-start(f32[2,256]{1,0:T(2,128)} %copy-done.29) | copy-start | bytes 6148
  278.0 9.7 %copy-start.35 = (f32[2,256]{1,0:T(2,128)S(1)}, f32[2,256]{1,0:T(2,128)}, u32[]{:S(2)}) copy-start(f32[2,256]{1,0:T(2,128)} %div.38) | copy-start | bytes 6148
  278.0 9.7 %copy-start.39 = (f32[2]{0:T(128)S(1)}, f32[2]{0:T(128)}, u32[]{:S(2)}) copy-start(f32[2]{0:T(128)} %copy-done.38) | copy-start | bytes 28
  291.3 5.1 copy-start.6
  296.4 29.3 %copy-start.17 = (f32[2,1152]{1,0:T(2,128)S(1)}, f32[2,1152]{1,0:T(2,128)}, u32[]{:S(2)}) copy-start(f32[2,1152]{1,0:T(2,128)} %copy-done.16) | copy-start | bytes 27652
  296.4 29.3 %copy-start.25 = (f32[2,256]{1,0:T(2,128)S(1)}, f32[2,256]{1,0:T(2,128)}, u32[]{:S(2)}) copy-start(f32[2,256]{1,0:T(2,128)} %copy-done.24) | copy-start | bytes 6148
  296.4 29.3 %copy-start.34 = (f32[2,256]{1,0:T(2,128)S(1)}, f32[2,256]{1,0:T(2,128)}, u32[]{:S(2)}) copy-start(f32[2,256]{1,0:T(2,128)} %copy-done.33) | copy-start | bytes 6148
  325.7 10.3 %copy-start = (bf16[2,256,3456]{2,1,0:T(8,128)(2,1)S(1)}, bf16[2,256,3456]{2,1,0:T(8,128)(2,1)}, u32[]{:S(2)}) copy-start(bf16[2,256,3456]{2,1,0:T(8,128)(2,1)} %attend_back.1) | copy-start | bytes 10616836
  325.7 12.8 %copy-start.5 = (f32[2,256,1152]{2,1,0:T(8,128)S(1)}, f32[2,256,1152]{2,1,0:T(8,128)}, u32[]{:S(2)}) copy-start(f32[2,256,1152]{2,1,0:T(8,128)} %get-tuple-element.76) | copy-start | bytes 7077892
  (17 other events, 33.9 us)
Sparse Core Ops, SparseCore 0:
  155.1 88.2 all-gather.1

commit v8 on v7

--- a/solution.py
+++ b/solution.py
@@ -60,7 +60,7 @@
 
 
 def reduce_kernel(
-    a_in, a_out, a_up, a_down, b_in, b_out, b_up, b_down, out_ref,
+    projected_ref, grad_ref, lse_ref, a_in, a_out, a_up, a_down, b_out, b_up, b_down, out_ref, b_in,
     abuf, bbuf, gbuf, sbuf, tbuf, ubuf, fbuf, core_in, one_in, two_in, z_in, far_in,
     asem, bsem, core_sem, one_sem, two_sem, zs_sem, zr_sem, far_sem,
 ):
@@ -87,21 +87,19 @@
         )
 
     def fetch(chunk, half):
-        number = chunk + half * PER_HALF
-        regions = ((0, 9, a_in, b_in), (9, 12, a_out, b_out), (12, 24, a_up, b_up))
-        for lower, upper, left, right in regions:
-            if half * PER_HALF < upper and lower < (half + 1) * PER_HALF:
-
-                @pl.when(jnp.logical_and(number >= lower, number < upper))
-                def _(lower=lower, left=left, right=right):
-                    for copy in copies(left.at[0], right, number - lower, half):
-                        copy.start()
-
         if half:
-
-            @pl.when(number >= 24)
-            def _():
-                for copy in copies(a_down.at[(number - 24) // 3], b_down, (number - 24) % 3, half):
+            regions = ((0, 12, None, b_down, 0), (12, 18, a_in, b_in, 3))
+        else:
+            regions = ((0, 12, a_up, b_up, 0), (12, 15, a_out, b_out, 0), (15, 18, a_in, b_in, 0))
+        for lower, upper, left, right, offset in regions:
+
+            @pl.when(jnp.logical_and(chunk >= lower, chunk < upper))
+            def _(lower=lower, left=left, right=right, offset=offset):
+                if left is None:
+                    pieces = copies(a_down.at[chunk // 3], right, chunk % 3, half)
+                else:
+                    pieces = copies(left.at[0], right, chunk - lower + offset, half)
+                for copy in pieces:
                     copy.start()
 
     def send(src, dst, sems, chunk, peer):
@@ -144,7 +142,7 @@
 
     def make(chunk):
         for half in range(2):
-            for copy in copies(a_in.at[0], b_in, 0, half):
+            for copy in copies(a_in.at[0], b_up, 0, half):
                 copy.wait()
             for side in range(2):
                 product = jnp.dot(
@@ -216,26 +214,47 @@
     for half in range(2):
         fetch(0, half)
 
-    def turn(step, carry):
-        for parity in range(2):
-            now = step * 2 + parity
-            for lag, action, fixed in (
-                (1 + 3 * DEPTH, third, False),
-                (1 + 2 * DEPTH, second, True),
-                (1 + DEPTH, first, True),
-                (1, pair, True),
-                (0, make, False),
-            ):
-                chunk = now - lag
-                even = (parity - lag) % 2 == 0
-
-                @pl.when(jnp.logical_and(chunk >= 0, chunk < PER_HALF))
-                def _(action=action, fixed=fixed, chunk=chunk, even=even):
-                    action(chunk, even) if fixed else action(chunk)
+    def turn(now, carry):
+        for lag, action, fixed in (
+            (1 + 3 * DEPTH, third, False),
+            (1 + 2 * DEPTH, second, True),
+            (1 + DEPTH, first, True),
+            (1, pair, True),
+            (0, make, False),
+        ):
+            chunk = now - lag
+            valid = jnp.logical_and(chunk >= 0, chunk < PER_HALF)
+            if fixed:
+                even = (2 * chunk + 10 * PER_HALF) % 5 < 2
+
+                @pl.when(jnp.logical_and(valid, even))
+                def _(action=action, chunk=chunk):
+                    action(chunk, True)
+
+                @pl.when(jnp.logical_and(valid, jnp.logical_not(even)))
+                def _(action=action, chunk=chunk):
+                    action(chunk, False)
+
+            else:
+
+                @pl.when(valid)
+                def _(action=action, chunk=chunk):
+                    action(chunk)
+
+        seq_len = projected_ref.shape[0] // 2
+        for group in range(4):
+
+            @pl.when(jnp.logical_and(now < 8, now % 4 == group))
+            def _(group=group):
+                rows = pl.ds(pl.multiple_of(now // 4 * seq_len, seq_len), seq_len)
+                for head in range(4 * group, 4 * group + 4):
+                    attend_back_head(
+                        head, projected_ref.at[rows], grad_ref.at[rows], lse_ref.at[rows], b_in.at[rows]
+                    )
 
         return carry
 
-    lax.fori_loop(0, (PER_HALF + 3 * DEPTH + 2) // 2, turn, 0)
+    lax.fori_loop(0, PER_HALF + 3 * DEPTH + 1, turn, 0)
 
     def finish(chunk, carry):
         far_copy(chunk).wait()
@@ -252,12 +271,15 @@
     n = PER_HALF
     return pl.pallas_call(
         reduce_kernel,
-        out_shape=jax.ShapeDtypeStruct((2 * n,) + unit, jnp.float32),
-        in_specs=[pl.BlockSpec(memory_space=pl.ANY)] * 8,
-        out_specs=pl.BlockSpec(memory_space=pltpu.VMEM),
+        out_shape=(
+            jax.ShapeDtypeStruct((2 * n,) + unit, jnp.float32),
+            jax.ShapeDtypeStruct(operands[0].shape, bf),
+        ),
+        in_specs=in_vmem(3) + [pl.BlockSpec(memory_space=pl.ANY)] * 7,
+        out_specs=tuple(in_vmem(2)),
         scratch_shapes=[
-            pltpu.VMEM((2,) + operands[0].shape[1:], bf),
-            pltpu.VMEM((2, operands[4].shape[0], LANES), bf),
+            pltpu.VMEM((2,) + operands[3].shape[1:], bf),
+            pltpu.VMEM((2, operands[0].shape[0], LANES), bf),
             pltpu.VMEM((2, 2, 8) + unit, bf),
             pltpu.VMEM((DEPTH, 2, 2, 4) + unit, bf),
             pltpu.VMEM((DEPTH, 2, 4) + unit, bf),
@@ -290,17 +312,21 @@
     return rows.transpose(2, 1, 0, 3, 4).reshape(parts, 2, 576, tokens)
 
 
-def weight_grads(first_input, attended, second_in, activated, grad_projected, grad_branch, grad_hidden, grad_mlp):
-    done = reduce_weights(
-        by_holder(first_input, 1), by_holder(attended, 1), by_holder(second_in, 1),
-        by_holder(activated, 4), grad_projected, grad_branch, grad_hidden, grad_mlp,
-    )
-
-    def flat(lower, upper):
-        return done[lower:upper].transpose(1, 0, 2).reshape(72, (upper - lower) * LANES)
-
-    down = done[24:].reshape(4, 3, 72, LANES).transpose(0, 2, 1, 3).reshape(288, 3 * LANES)
-    return flat(0, 9), flat(9, 12), flat(12, 24), down
+def weight_grads(
+    projected, grad_attended, log_total, first_input, attended, second_in, activated,
+    grad_branch, grad_hidden, grad_mlp,
+):
+    done, grad_projected = reduce_weights(
+        projected, grad_attended, log_total, by_holder(first_input, 1), by_holder(attended, 1),
+        by_holder(second_in, 1), by_holder(activated, 4), grad_branch, grad_hidden, grad_mlp,
+    )
+
+    def flat(*pieces):
+        part = jnp.concatenate(pieces) if len(pieces) > 1 else pieces[0]
+        return part.transpose(1, 0, 2).reshape(72, part.shape[0] * LANES)
+
+    down = done[18:30].reshape(4, 3, 72, LANES).transpose(0, 2, 1, 3).reshape(288, 3 * LANES)
+    return grad_projected, (flat(done[15:18], done[30:]), flat(done[12:15]), flat(done[:12]), down)
 
 
 def place(index, wide_count):
@@ -599,14 +625,14 @@
 def head_parts(ref, head, width, count):
     at = head * width
     span = width * HEADS
-    return [ref[0, :, number * span + at : number * span + at + width] for number in range(count)]
+    return [ref[:, number * span + at : number * span + at + width] for number in range(count)]
 
 
 def attend_kernel(projected_ref, out_ref, lse_ref):
     width = out_ref.shape[2] // HEADS
     scale = width ** (-0.5)
     for head in range(HEADS):
-        query, key, value = head_parts(projected_ref, head, width, 3)
+        query, key, value = head_parts(projected_ref.at[0], head, width, 3)
         scores = matmul_back(query, key) * scale
         top = jnp.max(scores, axis=-1, keepdims=True)
         lse = top + jnp.log(jnp.sum(jnp.exp(scores - top), axis=-1, keepdims=True))
@@ -617,24 +643,28 @@
         lse_ref[0, :, head : head + 1] = lse
 
 
-def attend_back_kernel(projected_ref, grad_ref, lse_ref, out_ref):
-    model_width = grad_ref.shape[2]
+def attend_back_head(head, projected_ref, grad_ref, lse_ref, out_ref):
+    model_width = grad_ref.shape[1]
     width = model_width // HEADS
     scale = width ** (-0.5)
+    query, key, value = head_parts(projected_ref, head, width, 3)
+    (grad,) = head_parts(grad_ref, head, width, 1)
+    scores = matmul_back(query, key) * scale
+    probs = jnp.exp(scores - lse_ref[:, head : head + 1])
+    grad_value = matmul_outer(probs.astype(jnp.bfloat16), grad)
+    grad_probs = matmul_back(grad, value)
+    row_dot = jnp.sum(grad_probs * probs, axis=-1, keepdims=True)
+    grad_scores = (probs * (grad_probs - row_dot)).astype(jnp.bfloat16)
+    grad_query = matmul_rows(grad_scores, key) * scale
+    grad_key = matmul_outer(grad_scores, query) * scale
+    for number, part in enumerate((grad_query, grad_key, grad_value)):
+        at = number * model_width + head * width
+        out_ref[:, at : at + width] = part.astype(jnp.bfloat16)
+
+
+def attend_back_kernel(*refs):
     for head in range(HEADS):
-        query, key, value = head_parts(projected_ref, head, width, 3)
-        (grad,) = head_parts(grad_ref, head, width, 1)
-        scores = matmul_back(query, key) * scale
-        probs = jnp.exp(scores - lse_ref[0, :, head : head + 1])
-        grad_value = matmul_outer(probs.astype(jnp.bfloat16), grad)
-        grad_probs = matmul_back(grad, value)
-        row_dot = jnp.sum(grad_probs * probs, axis=-1, keepdims=True)
-        grad_scores = (probs * (grad_probs - row_dot)).astype(jnp.bfloat16)
-        grad_query = matmul_rows(grad_scores, key) * scale
-        grad_key = matmul_outer(grad_scores, query) * scale
-        for number, part in enumerate((grad_query, grad_key, grad_value)):
-            at = number * model_width + head * width
-            out_ref[0, :, at : at + width] = part.astype(jnp.bfloat16)
+        attend_back_head(head, *[ref.at[0] for ref in refs])
 
 
 def by_image(shape):
@@ -774,12 +804,22 @@
         .astype(jnp.bfloat16)
         .reshape(slots, seq_len, model_width)
     )
-    grad_projected = attend_call(
-        attend_back_kernel,
-        (projected, grad_attended, log_total),
-        jax.ShapeDtypeStruct((slots, seq_len, 3 * model_width), jnp.bfloat16),
-        "attend_back",
-    ).reshape(row_total, 3 * model_width)
+    fast = lax.axis_size("narrow") == 2 and wide_count == 16
+    if fast:
+        grad_projected, w_grads = weight_grads(
+            projected.reshape(row_total, 3 * model_width),
+            grad_attended.reshape(row_total, model_width),
+            log_total.reshape(row_total, HEADS),
+            first_input, attended, second_in, activated,
+            residual_branch_gradient, grad_hidden, grad_mlp,
+        )
+    else:
+        grad_projected = attend_call(
+            attend_back_kernel,
+            (projected, grad_attended, log_total),
+            jax.ShapeDtypeStruct((slots, seq_len, 3 * model_width), jnp.bfloat16),
+            "attend_back",
+        ).reshape(row_total, 3 * model_width)
     proj_sums = jnp.sum(grad_projected.astype(jnp.float32), axis=0)
     first_gradient = matmul_back(grad_projected, wb_inproj).reshape(slots, seq_len, model_width)
     selfattn_scale_gradient = jnp.sum(first_gradient * normalized_first, axis=1)
@@ -832,12 +872,7 @@
             tiled=True,
         ).astype(jnp.float32)
 
-    if lax.axis_size("narrow") == 2 and wide_count == 16:
-        w_grads = weight_grads(
-            first_input, attended, second_in, activated,
-            grad_projected, residual_branch_gradient, grad_hidden, grad_mlp,
-        )
-    else:
+    if not fast:
         shards = [reduce_block(*job) for job in block_jobs]
         input_grads = jnp.concatenate(shards[:4], axis=1)
         w_grads = tuple(

time: 576 us -> 559 us (0.970)
  Pallas kernels: 381 us -> 360 us
    pallas_call x2 -> x1, Pallas kernels: 50.1 us -> 20.9 us  [attend_call(): pl.pallas_call(kernel, grid=(slots,), out_shape=shapes, in_specs=[by_imag...]
    pallas_call x1, Pallas kernels: 170 us -> 178 us  [reduce_weights(): pl.pallas_call(reduce_kernel, out_shape=(jax.ShapeDtypeStruct((2 * n,) +...]
where the time goes in v8:
time: 559 us; the launch traced here: 550 us
  Pallas kernels  360 us (64%)
  matrix products  80.5 us (14%)
  local copies, waits for them, and re-layouts  48.1 us (9%)
  other arithmetic  28.2 us (5%)
  waiting for transfers between devices  17.8 us (3%)
  between operations  15.7 us (3%)
    pallas_call x1, Pallas kernels, reduce_weights(): pl.pallas_call(reduce_kernel, out_shape=(jax.ShapeDtypeStruct((2 * n,) +...  178 us
    pallas_call x1, Pallas kernels, front(): pl.pallas_call(partial(front_kernel, narrow_count, wide_count, with_weigh...  140 us
    dot_general x4, matrix products, matmul_back(): lax.dot_general(left, right, (((1,), (1,)), ((), ())), preferred_element_...  42.9 us
    dot_general x4, matrix products, matmul_rows(): return jnp.dot(left, right, preferred_element_type=jnp.float32)  37.6 us
    pallas_call x1, Pallas kernels, tail(): pl.pallas_call(partial(tail_kernel, narrow_count, wide_count), out_shape=...  21.4 us
    pallas_call x1, Pallas kernels, attend_call(): pl.pallas_call(kernel, grid=(slots,), out_shape=shapes, in_specs=[by_imag...  20.9 us
    all_gather x1, waiting for transfers between devices, per_device(): w_down = lax.all_gather(down_weight, 'wide', axis=0, tiled=True)  17.8 us
  transfers between devices with their start and end apart: 1, of which 1 were waited for; matrix products, arithmetic and copies ran while one was open for 9% of the time, Pallas kernels for 4%

profile of v8, /device:TPU:0, one launch (start us, length us, event | category | flops | bytes accessed | tf_op | source)
XLA Modules:
  0.0 550.2 jit_solution(13450535028944822937)
XLA Ops:
  10.1 2.4 copy.33.refs_1_.refs_11_
  13.3 2.1 pad_maximum_fusion.refs_3_
  15.3 139.5 %front.1 = (bf16[32,8,1152]{2,1,0:T(8,128)(2,1)}, bf16[16,8,432]{2,1,0:T(8,128)(2,1)}, bf16[4,2,2,72,9216]{4,3,2,1,0:T(8,128)(2,1)}) custom-call(bf16[8,1152]{1,0:T(8,128)(2,1)} %maximum_maximum_fusion.refs_0_, bf16[1152,432]{1,0:T(8,128)(2,1)} %copy.33.refs_1_.refs_11_, bf16[1,432]{1,0:T(2,128)(2,1)} %broadcast_in_dim.18.refs_2_, ...), custom_call_target="tpu_custom_call" | custom-call | tf_op jit(solution)/shard_map/front/pallas_call | solution.py:574
  163.0 2.8 convert_reduce_fusion.3
  168.2 9.7 %add_convert_fusion.projected_ref = bf16[512,3456]{1,0:T(8,128)(2,1)} fusion(bf16[512,1152]{1,0:T(8,128)(2,1)S(1)} %bitcast.115, bf16[1152,9216]{1,0:T(8,128)(2,1)} %bitcast.130, f32[3456]{0:T(1024)S(1)} %pad_maximum_fusion.1), kind=kOutput, calls=%fused_computation.16 | convolution fusion | flops 4080402432 | bytes 12695040 | tf_op jit(solution)/shard_map/dot_general | solution.py:33
  177.9 20.9 %attend.1 = (bf16[2,256,1152]{2,1,0:T(8,128)(2,1)}, f32[2,256,16]{2,1,0:T(8,128)}) custom-call(bf16[2,256,3456]{2,1,0:T(8,128)(2,1)} %bitcast.118), custom_call_target="tpu_custom_call" | custom-call | flops 1207959552 | bytes 7077888 | tf_op jit(solution)/shard_map/attend/pallas_call | solution.py:677
  201.6 3.6 convolution_add_fusion.1
  212.2 13.6 %multiply_convert_fusion = (bf16[512,4608]{1,0:T(8,128)(2,1)}, f32[512,4608]{1,0:T(8,128)}) fusion(f32[4608]{0:T(1024)S(1)} %copy-done.35, bf16[512,1152]{1,0:T(8,128)(2,1)S(1)} %bitcast.117, bf16[1152,9216]{1,0:T(8,128)(2,1)} %bitcast.132), kind=kOutput, calls=%fused_computation.10 | convolution fusion | flops 5459410944 | bytes 25970688 | tf_op jit(solution)/shard_map/dot_general | solution.py:33
  225.8 17.8 %all-gather.2.cloned.1.call-done = bf16[4608,1152]{1,0:T(8,128)(2,1)} async-done(((bf16[288,1152]{1,0:T(8,128)(2,1)}), bf16[4608,1152]{1,0:T(8,128)(2,1)}) %all-gather.2.cloned.1.call-update) | async-done | bytes 10616848 | tf_op jit(solution)/shard_map/all_gather | solution.py:741
  243.6 6.7 %copy.41 = bf16[4608,512]{1,0:T(8,128)(2,1)} copy(bf16[4608,512]{0,1:T(8,128)(2,1)} %bitcast.108) | data formatting | bytes 9437184 | tf_op jit(solution)/shard_map/transpose | solution.py:311
  250.3 5.1 copy.42
  255.4 10.7 %convolution_add_fusion = f32[512,1152]{1,0:T(8,128)} fusion(bf16[512,4608]{1,0:T(8,128)(2,1)S(1)} %bitcast.110, bf16[4608,1152]{1,0:T(8,128)(2,1)} %all-gather.2.cloned.1.call-done, f32[1152]{0:T(1024)S(1)} %copy-done.39), kind=kOutput, calls=%fused_computation.24 | convolution fusion | flops 5436407808 | bytes 17699328 | tf_op jit(solution)/shard_map/dot_general | solution.py:33
  266.1 16.0 %convert_reduce_fusion = (f32[4608]{0:T(1024)}, bf16[512,4608]{1,0:T(8,128)(2,1)S(1)}) fusion(f32[512,4608]{1,0:T(8,128)} %get-tuple-element.103, f32[4608]{0:T(1024)S(1)} %copy-done.36, bf16[512,1152]{1,0:T(8,128)(2,1)S(1)} %bitcast.107, bf16[4608,1152]{1,0:T(8,128)(2,1)} %all-gather.2.cloned.1.call-done), kind=kOutput, calls=%fused_computation.9 | convolution fusion | flops 5490077184 | bytes 25989120 | tf_op jit(solution)/shard_map/dot_general | solution.py:37
  282.1 12.4 %fusion.33 = (f32[512]{0:T(512)S(1)}, f32[512,1152]{1,0:T(8,128)}) fusion(f32[2,1152]{1,0:T(2,128)S(1)} %copy-done.19, bf16[512,4608]{1,0:T(8,128)(2,1)S(1)} %get-tuple-element.76.b_up, bf16[1152,9216]{1,0:T(8,128)(2,1)} %bitcast.133), kind=kOutput, calls=%fused_computation.46 | convolution fusion | flops 5436997120 | bytes 17705984 | tf_op jit(solution)/shard_map/dot_general | solution.py:37
  294.6 3.9 fusion.34
  298.7 3.5 convert_reduce_fusion.4
  302.2 5.1 convolution_convert_fusion.grad_ref
  307.3 178.1 %reduce_weights.1 = (f32[36,72,384]{2,1,0:T(8,128)}, bf16[512,3456]{1,0:T(8,128)(2,1)}) custom-call(bf16[512,3456]{1,0:T(8,128)(2,1)} %add_convert_fusion.projected_ref, bf16[512,1152]{1,0:T(8,128)(2,1)} %convolution_convert_fusion.grad_ref, f32[512,16]{1,0:T(8,128)} %bitcast.125, bf16[1,2,576,512]{3,2,1,0:T(8,128)(2,1)} %bitcast.103, ...), custom_call_target="tpu_custom_call" | custom-call | tf_op jit(solution)/shard_map/reduce_weights/pallas_call | solution.py:272
  485.4 9.5 %fusion.32 = (f32[512]{0:T(512)S(1)}, f32[512,1152]{1,0:T(8,128)S(1)}) fusion(f32[2,1152]{1,0:T(2,128)S(1)} %get-tuple-element.94, bf16[512,3456]{1,0:T(8,128)(2,1)} %get-tuple-element.36, bf16[1152,9216]{1,0:T(8,128)(2,1)} %bitcast.135), kind=kOutput, calls=%fused_computation.43 | convolution fusion | flops 4078042624 | bytes 13872128 | tf_op jit(solution)/shard_map/dot_general | solution.py:37
  499.3 2.3 fusion.30
  501.7 2.6 multiply_reduce_fusion.1
  504.3 21.4 %tail.1 = (f32[1152,432]{1,0:T(8,128)}, f32[8,432]{1,0:T(8,128)}, f32[8,1152]{1,0:T(8,128)}) custom-call(f32[2,1152]{1,0:T(2,128)} %get-tuple-element.71.refs_0_, f32[2,1152]{1,0:T(2,128)} %get-tuple-element.70.refs_1_, f32[2,1152]{1,0:T(2,128)} %get-tuple-element.87.refs_2_, f32[2,1152]{1,0:T(2,128)} %get-tuple-element.69.refs_3_, ...), custom_call_target="tpu_custom_call" | custom-call | tf_op jit(solution)/shard_map/tail/pallas_call | solution.py:599
  533.1 1.9 fusion.48
  541.1 1.9 copy.48
  (158 shorter events, 41.1 us)
Async XLA Ops:
  7.2 6.1 %copy-start.16 = (bf16[72,4608]{1,0:T(8,128)(2,1)S(1)}, bf16[72,4608]{1,0:T(8,128)(2,1)}, u32[]{:S(2)}) copy-start(bf16[72,4608]{1,0:T(8,128)(2,1)} %param.23) | copy-start | bytes 1990660
  7.2 6.1 %copy-start.17 = (bf16[72,3456]{1,0:T(8,128)(2,1)S(1)}, bf16[72,3456]{1,0:T(8,128)(2,1)}, u32[]{:S(2)}) copy-start(bf16[72,3456]{1,0:T(8,128)(2,1)} %param.19) | copy-start | bytes 1492996
  7.2 236.3 %all-gather.2.cloned.1.call-start = ((), (), s32[]{:S(2)}) async-start(), calls=%async_computation | async-start | bytes 11280384 | tf_op jit(solution)/shard_map/all_gather | solution.py:741
  15.3 146.3 %copy-start = (bf16[2,256,1152]{2,1,0:T(8,128)(2,1)S(1)}, bf16[2,256,1152]{2,1,0:T(8,128)(2,1)}, u32[]{:S(2)}) copy-start(bf16[2,256,1152]{2,1,0:T(8,128)(2,1)} %param.14) | copy-start | bytes 3538948
  154.9 8.1 %copy-start.8 = (bf16[2,256,1152]{2,1,0:T(8,128)(2,1)S(1)}, bf16[2,256,1152]{2,1,0:T(8,128)(2,1)}, u32[]{:S(2)}) copy-start(bf16[2,256,1152]{2,1,0:T(8,128)(2,1)} %param.27) | copy-start | bytes 3538948
  161.7 4.2 copy-start.41
  243.5 11.8 %slice-start = ((s8[4718592]{0:T(1024)(128)(4,1)}), s8[524288]{0:T(1024)(128)(4,1)S(1)}, s32[]{:S(2)}) async-start(s8[4718592]{0:T(1024)(128)(4,1)} %bitcast.109), calls=%async_computation.1 | async-start | bytes 1048576
  250.3 5.1 slice-start.1
  250.3 5.1 copy-start.39
  255.4 10.8 %copy-start.10 = (bf16[2,256,1152]{2,1,0:T(8,128)(2,1)S(1)}, bf16[2,256,1152]{2,1,0:T(8,128)(2,1)}, u32[]{:S(2)}) copy-start(bf16[2,256,1152]{2,1,0:T(8,128)(2,1)} %get-tuple-element.74) | copy-start | bytes 3538948
  255.4 10.8 %copy-start.36 = (f32[4608]{0:T(1024)S(1)}, f32[4608]{0:T(1024)}, u32[]{:S(2)}) copy-start(f32[4608]{0:T(1024)} %reshape.228) | copy-start | bytes 55300
  266.1 16.0 %copy-start.19 = (f32[2,1152]{1,0:T(2,128)S(1)}, f32[2,1152]{1,0:T(2,128)}, u32[]{:S(2)}) copy-start(f32[2,1152]{1,0:T(2,128)} %get-tuple-element.92) | copy-start | bytes 27652
  282.1 12.4 %copy-start.7 = (bf16[512,4608]{1,0:T(8,128)(2,1)}, bf16[512,4608]{1,0:T(8,128)(2,1)S(1)}, u32[]{:S(2)}) copy-start(bf16[512,4608]{1,0:T(8,128)(2,1)S(1)} %get-tuple-element.76.b_up) | copy-start | bytes 14155780
  282.1 12.4 %copy-start.25 = (f32[2,256]{1,0:T(2,128)S(1)}, f32[2,256]{1,0:T(2,128)}, u32[]{:S(2)}) copy-start(f32[2,256]{1,0:T(2,128)} %copy-done.24) | copy-start | bytes 6148
  282.1 12.4 %copy-start.34 = (f32[2,256]{1,0:T(2,128)S(1)}, f32[2,256]{1,0:T(2,128)}, u32[]{:S(2)}) copy-start(f32[2,256]{1,0:T(2,128)} %copy-done.33) | copy-start | bytes 6148
  294.5 4.0 copy-start.2
  294.5 4.0 copy-start.9
  294.5 4.1 copy-start.14
  294.5 4.1 copy-start.21
  294.6 4.1 copy-start.23
  294.6 4.1 copy-start.42
  302.2 5.1 copy-start.6
  485.4 9.5 %copy-start.12 = (bf16[512,3456]{1,0:T(8,128)(2,1)S(1)}, bf16[512,3456]{1,0:T(8,128)(2,1)}, u32[]{:S(2)}) copy-start(bf16[512,3456]{1,0:T(8,128)(2,1)} %get-tuple-element.36) | copy-start | bytes 10616836
  494.9 4.4 copy-start.1
  (22 other events, 42.3 us)
Sparse Core Ops, SparseCore 0:
  155.0 88.4 all-gather.1

commit v9 on v8

--- a/solution.py
+++ b/solution.py
@@ -11,6 +11,7 @@
 HEADS = 16
 MESH = pl.DeviceIdType.MESH
 DEPTH = 4
+AHEAD = 3
 
 
 norm_eps = 1e-06
@@ -214,13 +215,14 @@
     for half in range(2):
         fetch(0, half)
 
+    seq_len = projected_ref.shape[0] // 2
+
     def turn(now, carry):
         for lag, action, fixed in (
             (1 + 3 * DEPTH, third, False),
             (1 + 2 * DEPTH, second, True),
             (1 + DEPTH, first, True),
             (1, pair, True),
-            (0, make, False),
         ):
             chunk = now - lag
             valid = jnp.logical_and(chunk >= 0, chunk < PER_HALF)
@@ -241,16 +243,19 @@
                 def _(action=action, chunk=chunk):
                     action(chunk)
 
-        seq_len = projected_ref.shape[0] // 2
-        for group in range(4):
-
-            @pl.when(jnp.logical_and(now < 8, now % 4 == group))
+        for group in range(6):
+
+            @pl.when(jnp.logical_and(now < 12, now % 6 == group))
             def _(group=group):
-                rows = pl.ds(pl.multiple_of(now // 4 * seq_len, seq_len), seq_len)
-                for head in range(4 * group, 4 * group + 4):
+                rows = pl.ds(pl.multiple_of(now // 6 * seq_len, seq_len), seq_len)
+                for head in range(HEADS * group // 6, HEADS * (group + 1) // 6):
                     attend_back_head(
                         head, projected_ref.at[rows], grad_ref.at[rows], lse_ref.at[rows], b_in.at[rows]
                     )
+
+        @pl.when(now < PER_HALF)
+        def _():
+            make(now)
 
         return carry
 
@@ -318,7 +323,7 @@
 ):
     done, grad_projected = reduce_weights(
         projected, grad_attended, log_total, by_holder(first_input, 1), by_holder(attended, 1),
-        by_holder(second_in, 1), by_holder(activated, 4), grad_branch, grad_hidden, grad_mlp,
+        by_holder(second_in, 1), activated, grad_branch, grad_hidden, grad_mlp,
     )
 
     def flat(*pieces):
@@ -420,12 +425,16 @@
     def begin():
         for chunk in range(chunks):
             own(chunk).start()
+        for chunk in range(AHEAD):
             for copy in along_z(chunk):
                 copy.start()
 
     def run():
         stages = (lambda chunk: [own(chunk)] + along_z(chunk), one, two, across)
         for turn in range(chunks + 4):
+            if turn + AHEAD < chunks:
+                for copy in along_z(turn + AHEAD):
+                    copy.start()
             for stage in (2, 1, 0):
                 chunk = turn - 2 * stage
                 if 0 <= chunk < chunks:
@@ -775,7 +784,12 @@
     hidden = matmul_rows(second_in, w_up) + b_up.astype(jnp.float32)
     gelu_value, gelu_pull = jax.vjp(partial(jax.nn.gelu, approximate=True), hidden)
     activated = gelu_value.astype(jnp.bfloat16)
-    w_down, activated = lax.optimization_barrier((w_down, activated))
+    fast = lax.axis_size("narrow") == 2 and wide_count == 16
+    if fast:
+        held_activated = by_holder(activated, 4)
+        w_down, activated, held_activated = lax.optimization_barrier(
+            (w_down, activated, held_activated)
+        )
     mlp_out = (matmul_rows(activated, w_down) + b_down.astype(jnp.float32)).reshape(
         slots, seq_len, model_width
     )
@@ -804,13 +818,12 @@
         .astype(jnp.bfloat16)
         .reshape(slots, seq_len, model_width)
     )
-    fast = lax.axis_size("narrow") == 2 and wide_count == 16
     if fast:
         grad_projected, w_grads = weight_grads(
             projected.reshape(row_total, 3 * model_width),
             grad_attended.reshape(row_total, model_width),
             log_total.reshape(row_total, HEADS),
-            first_input, attended, second_in, activated,
+            first_input, attended, second_in, held_activated,
             residual_branch_gradient, grad_hidden, grad_mlp,
         )
     else:

time: 559 us -> 551 us (0.986)
  waiting for transfers between devices: 17.8 us -> 0.02 us
  local copies, waits for them, and re-layouts: 48.1 us -> 59.3 us
    all_gather x1, waiting for transfers between devices: 17.8 us -> 0.01 us  [per_device(): w_down = lax.all_gather(down_weight, 'wide', axis=0, tiled=True)]
    transpose x1 -> x0, local copies, waits for them, and re-layouts: 6.71 us -> none  [by_holder(): rows = left.T.reshape(8, 2, parts, 72, tokens)]
    convert_element_type x0 -> x1, local copies, waits for them, and re-layouts: none -> 6.65 us  [per_device(): activated = gelu_value.astype(jnp.bfloat16)]
    unnamed x95 -> x87, local copies, waits for them, and re-layouts: 8.83 us -> 13.5 us
  transfers between devices with their start and end apart: 1 -> 1, of which waited for: 1 -> 0; matrix products, arithmetic and copies ran while one was open for 9% -> 12% of each run, Pallas kernels for 4% -> 4%
where the time goes in v9:
time: 551 us; the launch traced here: 542 us
  Pallas kernels  357 us (65%)
  matrix products  77.1 us (14%)
  local copies, waits for them, and re-layouts  59.3 us (11%)
  other arithmetic  33.5 us (6%)
  between operations  15.4 us (3%)
    pallas_call x1, Pallas kernels, reduce_weights(): pl.pallas_call(reduce_kernel, out_shape=(jax.ShapeDtypeStruct((2 * n,) +...  181 us
    pallas_call x1, Pallas kernels, front(): pl.pallas_call(partial(front_kernel, narrow_count, wide_count, with_weigh...  134 us
    dot_general x4, matrix products, matmul_back(): lax.dot_general(left, right, (((1,), (1,)), ((), ())), preferred_element_...  41.2 us
    dot_general x4, matrix products, matmul_rows(): return jnp.dot(left, right, preferred_element_type=jnp.float32)  36 us
    pallas_call x1, Pallas kernels, tail(): pl.pallas_call(partial(tail_kernel, narrow_count, wide_count), out_shape=...  21.3 us
    pallas_call x1, Pallas kernels, attend_call(): pl.pallas_call(kernel, grid=(slots,), out_shape=shapes, in_specs=[by_imag...  20.6 us
    unnamed x87, local copies, waits for them, and re-layouts  13.5 us
  transfers between devices with their start and end apart: 1, of which 0 were waited for; matrix products, arithmetic and copies ran while one was open for 12% of the time, Pallas kernels for 4%

profile of v9, /device:TPU:0, one launch (start us, length us, event | category | flops | bytes accessed | tf_op | source)
XLA Modules:
  0.0 542.4 jit_solution(15625449941766475407)
XLA Ops:
  7.2 2.5 copy.33.refs_1_.refs_11_
  12.6 2.1 pad_maximum_fusion.refs_3_
  15.3 134.0 %front.1 = (bf16[32,8,1152]{2,1,0:T(8,128)(2,1)}, bf16[16,8,432]{2,1,0:T(8,128)(2,1)}, bf16[4,2,2,72,9216]{4,3,2,1,0:T(8,128)(2,1)}) custom-call(bf16[8,1152]{1,0:T(8,128)(2,1)} %maximum_maximum_fusion.refs_0_, bf16[1152,432]{1,0:T(8,128)(2,1)} %copy.33.refs_1_.refs_11_, bf16[1,432]{1,0:T(2,128)(2,1)} %broadcast_in_dim.18.refs_2_, ...), custom_call_target="tpu_custom_call" | custom-call | tf_op jit(solution)/shard_map/front/pallas_call | solution.py:583
  157.4 3.4 convert_reduce_fusion.3
  162.3 9.7 %add_convert_fusion.projected_ref = bf16[512,3456]{1,0:T(8,128)(2,1)} fusion(bf16[512,1152]{1,0:T(8,128)(2,1)S(1)} %bitcast.113, bf16[1152,9216]{1,0:T(8,128)(2,1)} %bitcast.128, f32[3456]{0:T(1024)S(1)} %pad_maximum_fusion.1), kind=kOutput, calls=%fused_computation.26 | convolution fusion | flops 4080402432 | bytes 12695040 | tf_op jit(solution)/shard_map/dot_general | solution.py:34
  171.9 20.6 %attend.1 = (bf16[2,256,1152]{2,1,0:T(8,128)(2,1)}, f32[2,256,16]{2,1,0:T(8,128)}) custom-call(bf16[2,256,3456]{2,1,0:T(8,128)(2,1)} %bitcast.116), custom_call_target="tpu_custom_call" | custom-call | flops 1207959552 | bytes 7077888 | tf_op jit(solution)/shard_map/attend/pallas_call | solution.py:686
  192.5 2.5 copy.40
  195.1 3.6 convolution_add_fusion.1
  203.9 12.6 %multiply_convert_fusion = (bf16[512,4608]{1,0:T(8,128)(2,1)}, f32[512,4608]{1,0:T(8,128)S(1)}) fusion(f32[4608]{0:T(1024)} %reshape.228, bf16[512,1152]{1,0:T(8,128)(2,1)} %bitcast.115, bf16[1152,9216]{1,0:T(8,128)(2,1)} %bitcast.130), kind=kOutput, calls=%fused_computation.19 | convolution fusion | flops 5459410944 | bytes 25972736 | tf_op jit(solution)/shard_map/dot_general | solution.py:34
  216.5 3.6 copy-done.4
  220.1 4.3 fusion.14
  224.4 6.7 %copy.37 = bf16[4608,512]{1,0:T(8,128)(2,1)} copy(bf16[4608,512]{0,1:T(8,128)(2,1)} %fusion.14) | data formatting | bytes 9437184 | tf_op jit(solution)/shard_map/convert_element_type | solution.py:786
  231.0 5.0 copy.38
  238.5 2.5 copy.41
  242.7 15.7 %convert_reduce_fusion = (f32[4608]{0:T(1024)}, bf16[512,4608]{1,0:T(8,128)(2,1)S(1)}) fusion(f32[512,4608]{1,0:T(8,128)} %copy-done.4, bf16[512,1152]{1,0:T(8,128)(2,1)S(1)} %bitcast.108, bf16[4608,1152]{1,0:T(8,128)(2,1)} %all-gather.2.cloned.1.call-done), kind=kOutput, calls=%fused_computation.18 | convolution fusion | flops 5487717888 | bytes 25970688 | tf_op jit(solution)/shard_map/dot_general | solution.py:38
  258.4 10.9 %fusion.44 = (f32[512]{0:T(512)S(1)}, f32[512,1152]{1,0:T(8,128)S(1)}) fusion(f32[2,1152]{1,0:T(2,128)S(1)} %copy-done.20, bf16[512,4608]{1,0:T(8,128)(2,1)S(1)} %get-tuple-element.78.b_up, bf16[1152,9216]{1,0:T(8,128)(2,1)} %bitcast.131), kind=kOutput, calls=%fused_computation.56 | convolution fusion | flops 5436997120 | bytes 17705984 | tf_op jit(solution)/shard_map/dot_general | solution.py:38
  271.0 10.0 %convolution_add_fusion = f32[512,1152]{1,0:T(8,128)S(1)} fusion(bf16[512,4608]{1,0:T(8,128)(2,1)} %get-tuple-element.34, bf16[4608,1152]{1,0:T(8,128)(2,1)} %all-gather.2.cloned.1.call-done, f32[1152]{0:T(1024)S(1)} %copy-done.38), kind=kOutput, calls=%fused_computation.34 | convolution fusion | flops 5436407808 | bytes 17699328 | tf_op jit(solution)/shard_map/dot_general | solution.py:34
  281.1 3.6 convert_reduce_fusion.4
  284.7 5.1 convolution_convert_fusion.grad_ref
  289.8 181.1 %reduce_weights.1 = (f32[36,72,384]{2,1,0:T(8,128)}, bf16[512,3456]{1,0:T(8,128)(2,1)}) custom-call(bf16[512,3456]{1,0:T(8,128)(2,1)} %add_convert_fusion.projected_ref, bf16[512,1152]{1,0:T(8,128)(2,1)} %convolution_convert_fusion.grad_ref, f32[512,16]{1,0:T(8,128)} %bitcast.123, bf16[1,2,576,512]{3,2,1,0:T(8,128)(2,1)} %bitcast.106, ...), custom_call_target="tpu_custom_call" | custom-call | tf_op jit(solution)/shard_map/reduce_weights/pallas_call | solution.py:277
  474.9 9.5 %fusion.43 = (f32[512]{0:T(512)S(1)}, f32[512,1152]{1,0:T(8,128)S(1)}) fusion(f32[2,1152]{1,0:T(2,128)S(1)} %get-tuple-element.96, bf16[512,3456]{1,0:T(8,128)(2,1)} %get-tuple-element.38, bf16[1152,9216]{1,0:T(8,128)(2,1)} %bitcast.133), kind=kOutput, calls=%fused_computation.53 | convolution fusion | flops 4078042624 | bytes 13872128 | tf_op jit(solution)/shard_map/dot_general | solution.py:38
  493.5 4.3 multiply_reduce_fusion.1
  497.8 21.3 %tail.1 = (f32[1152,432]{1,0:T(8,128)}, f32[8,432]{1,0:T(8,128)}, f32[8,1152]{1,0:T(8,128)}) custom-call(f32[2,1152]{1,0:T(2,128)} %get-tuple-element.73.refs_0_, f32[2,1152]{1,0:T(2,128)} %get-tuple-element.72.refs_1_, f32[2,1152]{1,0:T(2,128)} %get-tuple-element.89.refs_2_, f32[2,1152]{1,0:T(2,128)} %get-tuple-element.71.refs_3_, ...), custom_call_target="tpu_custom_call" | custom-call | tf_op jit(solution)/shard_map/tail/pallas_call | solution.py:608
  527.4 2.9 copy.48
  (150 shorter events, 49.5 us)
Async XLA Ops:
  7.2 5.4 copy-start.18
  7.2 5.4 copy-start.17
  7.2 235.5 %all-gather.2.cloned.1.call-start = ((), (), s32[]{:S(2)}) async-start(), calls=%async_computation | async-start | bytes 11280384 | tf_op jit(solution)/shard_map/all_gather | solution.py:750
  14.7 141.4 %copy-start = (bf16[2,256,1152]{2,1,0:T(8,128)(2,1)S(1)}, bf16[2,256,1152]{2,1,0:T(8,128)(2,1)}, u32[]{:S(2)}) copy-start(bf16[2,256,1152]{2,1,0:T(8,128)(2,1)} %param.14) | copy-start | bytes 3538948
  149.4 8.1 %copy-start.8 = (bf16[2,256,1152]{2,1,0:T(8,128)(2,1)S(1)}, bf16[2,256,1152]{2,1,0:T(8,128)(2,1)}, u32[]{:S(2)}) copy-start(bf16[2,256,1152]{2,1,0:T(8,128)(2,1)} %param.27) | copy-start | bytes 3538948
  156.1 4.7 copy-start.39
  156.8 4.0 copy-start.30
  171.9 23.1 %copy-start.37 = (f32[1152]{0:T(1024)S(1)}, f32[1152]{0:T(1024)}, u32[]{:S(2)}) copy-start(f32[1152]{0:T(1024)} %reshape.227) | copy-start | bytes 13828
  195.0 3.6 copy-start.24
  237.4 3.6 copy-start.11
  238.5 3.6 copy-start.32
  238.5 4.2 copy-start.10
  242.7 15.7 %copy-start.20 = (f32[2,1152]{1,0:T(2,128)S(1)}, f32[2,1152]{1,0:T(2,128)}, u32[]{:S(2)}) copy-start(f32[2,1152]{1,0:T(2,128)} %get-tuple-element.94) | copy-start | bytes 27652
  258.4 11.0 %copy-start.7 = (bf16[512,4608]{1,0:T(8,128)(2,1)}, bf16[512,4608]{1,0:T(8,128)(2,1)S(1)}, u32[]{:S(2)}) copy-start(bf16[512,4608]{1,0:T(8,128)(2,1)S(1)} %get-tuple-element.78.b_up) | copy-start | bytes 14155780
  258.4 11.0 %copy-start.27 = (f32[2,256]{1,0:T(2,128)S(1)}, f32[2,256]{1,0:T(2,128)}, u32[]{:S(2)}) copy-start(f32[2,256]{1,0:T(2,128)} %copy-done.26) | copy-start | bytes 6148
  258.4 11.0 %copy-start.36 = (f32[2,256]{1,0:T(2,128)S(1)}, f32[2,256]{1,0:T(2,128)}, u32[]{:S(2)}) copy-start(f32[2,256]{1,0:T(2,128)} %copy-done.35) | copy-start | bytes 6148
  270.9 10.1 %copy-start.3 = (f32[512,1152]{1,0:T(8,128)S(1)}, f32[512,1152]{1,0:T(8,128)}, u32[]{:S(2)}) copy-start(f32[512,1152]{1,0:T(8,128)} %copy-done.2) | copy-start | bytes 7077892
  271.0 10.1 %copy-start.9 = (bf16[2,256,1152]{2,1,0:T(8,128)(2,1)S(1)}, bf16[2,256,1152]{2,1,0:T(8,128)(2,1)}, u32[]{:S(2)}) copy-start(bf16[2,256,1152]{2,1,0:T(8,128)(2,1)} %param.27) | copy-start | bytes 3538948
  271.0 10.1 %copy-start.21 = (f32[2,1152]{1,0:T(2,128)S(1)}, f32[2,1152]{1,0:T(2,128)}, u32[]{:S(2)}) copy-start(f32[2,1152]{1,0:T(2,128)} %get-tuple-element.94) | copy-start | bytes 27652
  271.0 10.1 %copy-start.23 = (f32[2,1152]{1,0:T(2,128)S(1)}, f32[2,1152]{1,0:T(2,128)}, u32[]{:S(2)}) copy-start(f32[2,1152]{1,0:T(2,128)} %copy-done.22) | copy-start | bytes 27652
  271.0 10.1 %copy-start.25 = (f32[2,1152]{1,0:T(2,128)S(1)}, f32[2,1152]{1,0:T(2,128)}, u32[]{:S(2)}) copy-start(f32[2,1152]{1,0:T(2,128)} %get-tuple-element.97) | copy-start | bytes 27652
  271.0 10.1 %copy-start.40 = (f32[2]{0:T(128)S(1)}, f32[2]{0:T(128)}, u32[]{:S(2)}) copy-start(f32[2]{0:T(128)} %copy-done.39) | copy-start | bytes 28
  284.7 5.1 copy-start.6
  474.9 9.5 %copy-start.12 = (bf16[512,3456]{1,0:T(8,128)(2,1)S(1)}, bf16[512,3456]{1,0:T(8,128)(2,1)}, u32[]{:S(2)}) copy-start(bf16[512,3456]{1,0:T(8,128)(2,1)} %get-tuple-element.38) | copy-start | bytes 10616836
  (18 other events, 34.2 us)
Sparse Core Ops, SparseCore 0:
  149.5 87.7 all-gather.1

commit v10 on v9

--- a/solution.py
+++ b/solution.py
@@ -11,7 +11,9 @@
 HEADS = 16
 MESH = pl.DeviceIdType.MESH
 DEPTH = 4
-AHEAD = 3
+AHEAD = 4
+EARLY = 4
+GATHER_LANES = 256
 
 
 norm_eps = 1e-06
@@ -372,10 +374,11 @@
     core_peer = (narrow, wide + 1 - 2 * core)
     x_peer = (1 - narrow, wide)
     y_peer = (narrow, wide + 2 - 4 * row)
-    chunks = shard_ref.shape[1] // (2 * LANES)
+    chunks = shard_ref.shape[1] // (2 * GATHER_LANES)
 
     def span(chunk, half):
-        return pl.ds(pl.multiple_of((chunk + half * chunks) * LANES, LANES), LANES)
+        at = pl.multiple_of((chunk + half * chunks) * GATHER_LANES, GATHER_LANES)
+        return pl.ds(at, GATHER_LANES)
 
     def send(view, sems, chunk, number, peer):
         return pltpu.make_async_remote_copy(
@@ -429,9 +432,9 @@
             for copy in along_z(chunk):
                 copy.start()
 
-    def run():
+    def run(lower, upper):
         stages = (lambda chunk: [own(chunk)] + along_z(chunk), one, two, across)
-        for turn in range(chunks + 4):
+        for turn in range(lower, min(upper, chunks + 4)):
             if turn + AHEAD < chunks:
                 for copy in along_z(turn + AHEAD):
                     copy.start()
@@ -442,18 +445,21 @@
                         copy.wait()
                     for copy in stages[stage + 1](chunk):
                         copy.start()
+
+    def end():
+        run(EARLY, chunks + 4)
         for chunk in range(chunks):
             for copy in across(chunk):
                 copy.wait()
 
-    return begin, run
+    return begin, lambda: run(0, EARLY), end
 
 
 def front_kernel(narrow_count, wide_count, with_weights, *refs):
     if with_weights:
         pack_ref, weight_ref, bias_ref, shard_ref, all_ref, mod_ref, full_ref = refs[:7]
         part, send_sem, recv_sem, send_two, recv_two = refs[7:12]
-        begin, run = gather_steps(shard_ref, full_ref, *refs[12:])
+        begin, early, end = gather_steps(shard_ref, full_ref, *refs[12:])
     else:
         pack_ref, weight_ref, bias_ref, all_ref, mod_ref = refs[:5]
         part, send_sem, recv_sem, send_two, recv_two = refs[5:]
@@ -469,9 +475,10 @@
         )
 
     loop(total, lambda step: spread(step).start())
+    all_ref[me] = pack_ref[...]
     if with_weights:
         begin()
-    all_ref[me] = pack_ref[...]
+        early()
     loop(total, lambda step: spread(step).wait())
     rows = all_ref[pl.ds(base, wide_count)].astype(jnp.float32)
     rows = rows.reshape(wide_count * 8, rows.shape[2]).astype(jnp.bfloat16)
@@ -486,7 +493,7 @@
     loop(wide_count, lambda step: deal(step).start())
     mod_ref[wide] = part[wide]
     if with_weights:
-        run()
+        end()
     loop(wide_count, lambda step: deal(step).wait())
 
 
@@ -577,7 +584,7 @@
         operands.append(shard)
         shapes.append(jax.ShapeDtypeStruct((4, 2, 2) + shard.shape, jnp.bfloat16))
         out_specs.append(pl.BlockSpec(memory_space=pl.ANY))
-        n = shard.shape[1] // (2 * LANES)
+        n = shard.shape[1] // (2 * GATHER_LANES)
         for dims in ((n,), (n, 3), (n, 3), (2, n, 1), (2, n, 2), (2, n, 2)):
             scratch.append(pltpu.SemaphoreType.DMA(dims))
     results = pl.pallas_call(

time: 551 us -> 546 us (level)
  no operation moved by 1% of the time
where the time goes in v10:
time: 546 us; the launch traced here: 537 us
  Pallas kernels  352 us (64%)
  matrix products  77 us (14%)
  local copies, waits for them, and re-layouts  59.3 us (11%)
  other arithmetic  33.5 us (6%)
  between operations  15.4 us (3%)
    pallas_call x1, Pallas kernels, reduce_weights(): pl.pallas_call(reduce_kernel, out_shape=(jax.ShapeDtypeStruct((2 * n,) +...  180 us
    pallas_call x1, Pallas kernels, front(): pl.pallas_call(partial(front_kernel, narrow_count, wide_count, with_weigh...  129 us
    dot_general x4, matrix products, matmul_back(): lax.dot_general(left, right, (((1,), (1,)), ((), ())), preferred_element_...  41.2 us
    dot_general x4, matrix products, matmul_rows(): return jnp.dot(left, right, preferred_element_type=jnp.float32)  35.8 us
    pallas_call x1, Pallas kernels, tail(): pl.pallas_call(partial(tail_kernel, narrow_count, wide_count), out_shape=...  21.8 us
    pallas_call x1, Pallas kernels, attend_call(): pl.pallas_call(kernel, grid=(slots,), out_shape=shapes, in_specs=[by_imag...  20.6 us
    unnamed x87, local copies, waits for them, and re-layouts  13.5 us
  transfers between devices with their start and end apart: 1, of which 0 were waited for; matrix products, arithmetic and copies ran while one was open for 12% of the time, Pallas kernels for 4%

profile of v10, /device:TPU:0, one launch (start us, length us, event | category | flops | bytes accessed | tf_op | source)
XLA Modules:
  0.0 537.1 jit_solution(5189197946365838726)
XLA Ops:
  7.2 2.5 copy.33.refs_1_.refs_11_
  12.6 2.1 pad_maximum_fusion.refs_3_
  15.3 129.1 %front.1 = (bf16[32,8,1152]{2,1,0:T(8,128)(2,1)}, bf16[16,8,432]{2,1,0:T(8,128)(2,1)}, bf16[4,2,2,72,9216]{4,3,2,1,0:T(8,128)(2,1)}) custom-call(bf16[8,1152]{1,0:T(8,128)(2,1)} %maximum_maximum_fusion.refs_0_, bf16[1152,432]{1,0:T(8,128)(2,1)} %copy.33.refs_1_.refs_11_, bf16[1,432]{1,0:T(2,128)(2,1)} %broadcast_in_dim.18.refs_2_, ...), custom_call_target="tpu_custom_call" | custom-call | tf_op jit(solution)/shard_map/front/pallas_call | solution.py:590
  152.5 3.4 convert_reduce_fusion.3
  157.4 9.7 %add_convert_fusion.projected_ref = bf16[512,3456]{1,0:T(8,128)(2,1)} fusion(bf16[512,1152]{1,0:T(8,128)(2,1)S(1)} %bitcast.113, bf16[1152,9216]{1,0:T(8,128)(2,1)} %bitcast.128, f32[3456]{0:T(1024)S(1)} %pad_maximum_fusion.1), kind=kOutput, calls=%fused_computation.26 | convolution fusion | flops 4080402432 | bytes 12695040 | tf_op jit(solution)/shard_map/dot_general | solution.py:36
  167.1 20.6 %attend.1 = (bf16[2,256,1152]{2,1,0:T(8,128)(2,1)}, f32[2,256,16]{2,1,0:T(8,128)}) custom-call(bf16[2,256,3456]{2,1,0:T(8,128)(2,1)} %bitcast.116), custom_call_target="tpu_custom_call" | custom-call | flops 1207959552 | bytes 7077888 | tf_op jit(solution)/shard_map/attend/pallas_call | solution.py:693
  187.7 2.5 copy.40
  190.2 3.6 convolution_add_fusion.1
  199.0 12.5 %multiply_convert_fusion = (bf16[512,4608]{1,0:T(8,128)(2,1)}, f32[512,4608]{1,0:T(8,128)S(1)}) fusion(f32[4608]{0:T(1024)} %reshape.228, bf16[512,1152]{1,0:T(8,128)(2,1)} %bitcast.115, bf16[1152,9216]{1,0:T(8,128)(2,1)} %bitcast.130), kind=kOutput, calls=%fused_computation.19 | convolution fusion | flops 5459410944 | bytes 25972736 | tf_op jit(solution)/shard_map/dot_general | solution.py:36
  211.5 3.6 copy-done.4
  215.1 4.3 fusion.14
  219.4 6.7 %copy.37 = bf16[4608,512]{1,0:T(8,128)(2,1)} copy(bf16[4608,512]{0,1:T(8,128)(2,1)} %fusion.14) | data formatting | bytes 9437184 | tf_op jit(solution)/shard_map/convert_element_type | solution.py:793
  226.1 5.0 copy.38
  233.6 2.5 copy.41
  237.8 15.7 %convert_reduce_fusion = (f32[4608]{0:T(1024)}, bf16[512,4608]{1,0:T(8,128)(2,1)S(1)}) fusion(f32[512,4608]{1,0:T(8,128)} %copy-done.4, bf16[512,1152]{1,0:T(8,128)(2,1)S(1)} %bitcast.108, bf16[4608,1152]{1,0:T(8,128)(2,1)} %all-gather.2.cloned.1.call-done), kind=kOutput, calls=%fused_computation.18 | convolution fusion | flops 5487717888 | bytes 25970688 | tf_op jit(solution)/shard_map/dot_general | solution.py:40
  253.5 10.9 %fusion.44 = (f32[512]{0:T(512)S(1)}, f32[512,1152]{1,0:T(8,128)S(1)}) fusion(f32[2,1152]{1,0:T(2,128)S(1)} %copy-done.20, bf16[512,4608]{1,0:T(8,128)(2,1)S(1)} %get-tuple-element.78.b_up, bf16[1152,9216]{1,0:T(8,128)(2,1)} %bitcast.131), kind=kOutput, calls=%fused_computation.56 | convolution fusion | flops 5436997120 | bytes 17705984 | tf_op jit(solution)/shard_map/dot_general | solution.py:40
  266.1 10.0 %convolution_add_fusion = f32[512,1152]{1,0:T(8,128)S(1)} fusion(bf16[512,4608]{1,0:T(8,128)(2,1)} %get-tuple-element.34, bf16[4608,1152]{1,0:T(8,128)(2,1)} %all-gather.2.cloned.1.call-done, f32[1152]{0:T(1024)S(1)} %copy-done.38), kind=kOutput, calls=%fused_computation.34 | convolution fusion | flops 5436407808 | bytes 17699328 | tf_op jit(solution)/shard_map/dot_general | solution.py:36
  276.2 3.6 convert_reduce_fusion.4
  279.8 5.1 convolution_convert_fusion.grad_ref
  284.9 180.4 %reduce_weights.1 = (f32[36,72,384]{2,1,0:T(8,128)}, bf16[512,3456]{1,0:T(8,128)(2,1)}) custom-call(bf16[512,3456]{1,0:T(8,128)(2,1)} %add_convert_fusion.projected_ref, bf16[512,1152]{1,0:T(8,128)(2,1)} %convolution_convert_fusion.grad_ref, f32[512,16]{1,0:T(8,128)} %bitcast.123, bf16[1,2,576,512]{3,2,1,0:T(8,128)(2,1)} %bitcast.106, ...), custom_call_target="tpu_custom_call" | custom-call | tf_op jit(solution)/shard_map/reduce_weights/pallas_call | solution.py:279
  469.2 9.5 %fusion.43 = (f32[512]{0:T(512)S(1)}, f32[512,1152]{1,0:T(8,128)S(1)}) fusion(f32[2,1152]{1,0:T(2,128)S(1)} %get-tuple-element.96, bf16[512,3456]{1,0:T(8,128)(2,1)} %get-tuple-element.38, bf16[1152,9216]{1,0:T(8,128)(2,1)} %bitcast.133), kind=kOutput, calls=%fused_computation.53 | convolution fusion | flops 4078042624 | bytes 13872128 | tf_op jit(solution)/shard_map/dot_general | solution.py:40
  487.8 4.3 multiply_reduce_fusion.1
  492.2 21.8 %tail.1 = (f32[1152,432]{1,0:T(8,128)}, f32[8,432]{1,0:T(8,128)}, f32[8,1152]{1,0:T(8,128)}) custom-call(f32[2,1152]{1,0:T(2,128)} %get-tuple-element.73.refs_0_, f32[2,1152]{1,0:T(2,128)} %get-tuple-element.72.refs_1_, f32[2,1152]{1,0:T(2,128)} %get-tuple-element.89.refs_2_, f32[2,1152]{1,0:T(2,128)} %get-tuple-element.71.refs_3_, ...), custom_call_target="tpu_custom_call" | custom-call | tf_op jit(solution)/shard_map/tail/pallas_call | solution.py:615
  522.2 2.9 copy.48
  (150 shorter events, 49.5 us)
Async XLA Ops:
  7.2 5.4 %copy-start.18 = (bf16[72,3456]{1,0:T(8,128)(2,1)S(1)}, bf16[72,3456]{1,0:T(8,128)(2,1)}, u32[]{:S(2)}) copy-start(bf16[72,3456]{1,0:T(8,128)(2,1)} %param.19) | copy-start | bytes 1492996
  7.2 5.4 %copy-start.17 = (bf16[72,4608]{1,0:T(8,128)(2,1)S(1)}, bf16[72,4608]{1,0:T(8,128)(2,1)}, u32[]{:S(2)}) copy-start(bf16[72,4608]{1,0:T(8,128)(2,1)} %param.23) | copy-start | bytes 1990660
  7.2 230.6 %all-gather.2.cloned.1.call-start = ((), (), s32[]{:S(2)}) async-start(), calls=%async_computation | async-start | bytes 11280384 | tf_op jit(solution)/shard_map/all_gather | solution.py:757
  14.7 136.5 %copy-start = (bf16[2,256,1152]{2,1,0:T(8,128)(2,1)S(1)}, bf16[2,256,1152]{2,1,0:T(8,128)(2,1)}, u32[]{:S(2)}) copy-start(bf16[2,256,1152]{2,1,0:T(8,128)(2,1)} %param.14) | copy-start | bytes 3538948
  144.5 8.1 %copy-start.8 = (bf16[2,256,1152]{2,1,0:T(8,128)(2,1)S(1)}, bf16[2,256,1152]{2,1,0:T(8,128)(2,1)}, u32[]{:S(2)}) copy-start(bf16[2,256,1152]{2,1,0:T(8,128)(2,1)} %param.27) | copy-start | bytes 3538948
  151.2 4.7 copy-start.39
  151.9 4.0 copy-start.30
  167.1 23.1 %copy-start.37 = (f32[1152]{0:T(1024)S(1)}, f32[1152]{0:T(1024)}, u32[]{:S(2)}) copy-start(f32[1152]{0:T(1024)} %reshape.227) | copy-start | bytes 13828
  190.2 3.6 copy-start.24
  232.4 3.6 copy-start.11
  233.6 3.6 copy-start.32
  233.6 4.2 copy-start.10
  237.8 15.7 %copy-start.20 = (f32[2,1152]{1,0:T(2,128)S(1)}, f32[2,1152]{1,0:T(2,128)}, u32[]{:S(2)}) copy-start(f32[2,1152]{1,0:T(2,128)} %get-tuple-element.94) | copy-start | bytes 27652
  253.4 11.0 %copy-start.7 = (bf16[512,4608]{1,0:T(8,128)(2,1)}, bf16[512,4608]{1,0:T(8,128)(2,1)S(1)}, u32[]{:S(2)}) copy-start(bf16[512,4608]{1,0:T(8,128)(2,1)S(1)} %get-tuple-element.78.b_up) | copy-start | bytes 14155780
  253.4 11.0 %copy-start.27 = (f32[2,256]{1,0:T(2,128)S(1)}, f32[2,256]{1,0:T(2,128)}, u32[]{:S(2)}) copy-start(f32[2,256]{1,0:T(2,128)} %copy-done.26) | copy-start | bytes 6148
  253.4 11.0 %copy-start.36 = (f32[2,256]{1,0:T(2,128)S(1)}, f32[2,256]{1,0:T(2,128)}, u32[]{:S(2)}) copy-start(f32[2,256]{1,0:T(2,128)} %copy-done.35) | copy-start | bytes 6148
  266.0 10.1 %copy-start.3 = (f32[512,1152]{1,0:T(8,128)S(1)}, f32[512,1152]{1,0:T(8,128)}, u32[]{:S(2)}) copy-start(f32[512,1152]{1,0:T(8,128)} %copy-done.2) | copy-start | bytes 7077892
  266.0 10.1 %copy-start.9 = (bf16[2,256,1152]{2,1,0:T(8,128)(2,1)S(1)}, bf16[2,256,1152]{2,1,0:T(8,128)(2,1)}, u32[]{:S(2)}) copy-start(bf16[2,256,1152]{2,1,0:T(8,128)(2,1)} %param.27) | copy-start | bytes 3538948
  266.0 10.1 %copy-start.21 = (f32[2,1152]{1,0:T(2,128)S(1)}, f32[2,1152]{1,0:T(2,128)}, u32[]{:S(2)}) copy-start(f32[2,1152]{1,0:T(2,128)} %get-tuple-element.94) | copy-start | bytes 27652
  266.0 10.1 %copy-start.23 = (f32[2,1152]{1,0:T(2,128)S(1)}, f32[2,1152]{1,0:T(2,128)}, u32[]{:S(2)}) copy-start(f32[2,1152]{1,0:T(2,128)} %copy-done.22) | copy-start | bytes 27652
  266.0 10.1 %copy-start.25 = (f32[2,1152]{1,0:T(2,128)S(1)}, f32[2,1152]{1,0:T(2,128)}, u32[]{:S(2)}) copy-start(f32[2,1152]{1,0:T(2,128)} %get-tuple-element.97) | copy-start | bytes 27652
  266.1 10.1 %copy-start.40 = (f32[2]{0:T(128)S(1)}, f32[2]{0:T(128)}, u32[]{:S(2)}) copy-start(f32[2]{0:T(128)} %copy-done.39) | copy-start | bytes 28
  279.8 5.1 copy-start.6
  469.2 9.5 %copy-start.12 = (bf16[512,3456]{1,0:T(8,128)(2,1)S(1)}, bf16[512,3456]{1,0:T(8,128)(2,1)}, u32[]{:S(2)}) copy-start(bf16[512,3456]{1,0:T(8,128)(2,1)} %get-tuple-element.38) | copy-start | bytes 10616836
  (18 other events, 34.2 us)
Sparse Core Ops, SparseCore 0:
  144.6 86.8 all-gather.1
